TPU v7x, 32 devices: a whole 2x2x4 slice. The times are simulated.
32 devices in a mesh: ctx: 16 (over z, y, core), wt: 2 (over x).
Axes of the slice: x: 2, y: 2, z: 4, core: 2. Of those that a mesh axis runs over, the one named last changes fastest.
Arguments:
- block_in: bfloat16 [4, 4096, 512], P('wt', 'ctx'), may hold values from -6 to 6
- block_order: int32 [4, 32], P('wt'), may hold values from 0 to 31, as said below
- w_query: bfloat16 [512, 512], P('wt'), may hold values from -0.25 to 0.25
- b_query: bfloat16 [512], P('wt'), may hold values from -1.796875 to 1.796875
- w_key: bfloat16 [512, 512], P('wt'), may hold values from -0.25 to 0.25
- w_value: bfloat16 [512, 512], P('wt'), may hold values from -0.25 to 0.25
- b_value: bfloat16 [512], P('wt'), may hold values from -0.59765625 to 0.59765625
- w_out: bfloat16 [512, 512], P('wt'), may hold values from -1.5 to 1.5
- b_out: bfloat16 [512], P('wt'), may hold values from -1.796875 to 1.796875
- gain_one: bfloat16 [512], P('wt'), may hold values from 0.5 to 1.5
- shift_one: bfloat16 [512], P('wt'), may hold values from -1.796875 to 1.796875
- w_up: bfloat16 [512, 2048], P('wt'), may hold values from -0.25 to 0.25
- b_up: bfloat16 [2048], P('wt'), may hold values from -1.796875 to 1.796875
- w_down: bfloat16 [2048, 512], P('wt'), may hold values from -0.125 to 0.125
- b_down: bfloat16 [512], P('wt'), may hold values from -1.796875 to 1.796875
- gain_two: bfloat16 [512], P('wt'), may hold values from 0.5 to 1.5
- shift_two: bfloat16 [512], P('wt'), may hold values from -1.796875 to 1.796875
- cotangent: bfloat16 [4, 4096, 512], P('wt', 'ctx'), may hold values from -6 to 6
Outputs:
- block_out: bfloat16 [4, 4096, 512], P('wt', 'ctx')
- grad_in: bfloat16 [4, 4096, 512], P('wt', 'ctx')
- dw_query: float32 [512, 512], P('wt')
- db_query: float32 [512], P('wt')
- dw_key: float32 [512, 512], P('wt')
- dw_value: float32 [512, 512], P('wt')
- db_value: float32 [512], P('wt')
- dw_out: float32 [512, 512], P('wt')
- db_out: float32 [512], P('wt')
- dgain_one: float32 [512], P('wt')
- dshift_one: float32 [512], P('wt')
- dw_up: float32 [512, 2048], P('wt')
- db_up: float32 [2048], P('wt')
- dw_down: float32 [2048, 512], P('wt')
- db_down: float32 [512], P('wt')
- dgain_two: float32 [512], P('wt')
- dshift_two: float32 [512], P('wt')
Inputs may be any that keep to these rules, and one draw needn't show every extreme that they name: `block_order`: each row lists the 32 blocks of a sequence in stored order and is a permutation; entries 2 i and 2 i + 1 of a row sum to 31.
All inputs are finite; a program needn't handle non-finite values.
Results may differ from a plain program's by a relative error of at most 0.024.
Values may be sent and summed in bfloat16 or wider, within the bound.
A program may use at most 192 MiB of HBM per device.

v0:
```python
import math

import jax
import jax.numpy as jnp
from jax import lax
from jax.sharding import PartitionSpec as P

HEADS = 8
HEAD_DIM = 64
BLOCK = 128


masked_fill = -1e30
norm_eps = 1e-05


def smooth_gelu(values):
    inner = math.sqrt(2.0 / math.pi) * (values + 0.044715 * values * values * values)
    return 0.5 * values * (1.0 + jnp.tanh(inner))


def layer_norm(values, gain_vec, shift_vec):
    center = values - jnp.mean(values, axis=-1, keepdims=True)
    spread = jnp.mean(center * center, axis=-1, keepdims=True)
    return center * lax.rsqrt(spread + norm_eps) * gain_vec + shift_vec


def norm_back(values, gain_vec, upstream):
    outcome, pullback = jax.vjp(layer_norm, values, gain_vec, jnp.zeros_like(gain_vec))
    return pullback(upstream)


def project(left, right, pattern):
    return jnp.einsum(pattern, left, right, preferred_element_type=jnp.float32)


def block_scores(query_part, key_part, query_pos, key_pos):
    scores = project(query_part, key_part, "sqhd,skhd->shqk") * HEAD_DIM ** (-0.5)
    allowed = key_pos[:, None, None, :] <= query_pos[:, None, :, None]
    return jnp.where(allowed, scores, masked_fill)


def body(
    block_in,
    block_order,
    w_query,
    b_query,
    w_key,
    w_value,
    b_value,
    w_out,
    b_out,
    gain_one,
    shift_one,
    w_up,
    b_up,
    w_down,
    b_down,
    gain_two,
    shift_two,
    cotangent,
):
    seq_count, rows_seq, model_dim = block_in.shape
    row_total = seq_count * rows_seq
    scale_factor = HEAD_DIM ** (-0.5)
    (
        full_wq,
        full_bq,
        full_wk,
        full_wv,
        full_bv,
        full_wo,
        full_bo,
        full_g1,
        full_s1,
        full_wu,
        full_bu,
        full_wd,
        full_bd,
        full_g2,
        full_s2,
    ) = (
        lax.all_gather(w_query, "wt", axis=0, tiled=True),
        lax.all_gather(b_query, "wt", axis=0, tiled=True),
        lax.all_gather(w_key, "wt", axis=0, tiled=True),
        lax.all_gather(w_value, "wt", axis=0, tiled=True),
        lax.all_gather(b_value, "wt", axis=0, tiled=True),
        lax.all_gather(w_out, "wt", axis=0, tiled=True),
        lax.all_gather(b_out, "wt", axis=0, tiled=True),
        lax.all_gather(gain_one, "wt", axis=0, tiled=True),
        lax.all_gather(shift_one, "wt", axis=0, tiled=True),
        lax.all_gather(w_up, "wt", axis=0, tiled=True),
        lax.all_gather(b_up, "wt", axis=0, tiled=True),
        lax.all_gather(w_down, "wt", axis=0, tiled=True),
        lax.all_gather(b_down, "wt", axis=0, tiled=True),
        lax.all_gather(gain_two, "wt", axis=0, tiled=True),
        lax.all_gather(shift_two, "wt", axis=0, tiled=True),
    )
    tokens = block_in.reshape(row_total, model_dim)
    tokens_wide = tokens.astype(jnp.float32)
    queries = (project(tokens, full_wq, "rd,de->re") + full_bq.astype(jnp.float32)).astype(
        jnp.bfloat16
    )
    key_rows = project(tokens, full_wk, "rd,de->re").astype(jnp.bfloat16)
    value_rows = (project(tokens, full_wv, "rd,de->re") + full_bv.astype(jnp.float32)).astype(
        jnp.bfloat16
    )
    key_all, value_all = (
        lax.all_gather(key_rows.reshape(seq_count, rows_seq, model_dim), "ctx", axis=1, tiled=True),
        lax.all_gather(
            value_rows.reshape(seq_count, rows_seq, model_dim), "ctx", axis=1, tiled=True
        ),
    )
    seq_len = key_all.shape[1]
    key_heads = key_all.reshape(seq_count, seq_len, HEADS, HEAD_DIM)
    value_heads = value_all.reshape(seq_count, seq_len, HEADS, HEAD_DIM)
    query_heads = queries.reshape(seq_count, rows_seq, HEADS, HEAD_DIM)
    within = jnp.arange(BLOCK, dtype=jnp.int32)
    slot_first = lax.axis_index("ctx") * (rows_seq // BLOCK)
    own_blocks = lax.dynamic_slice_in_dim(block_order, slot_first, rows_seq // BLOCK, 1)
    query_pos = (own_blocks[:, :, None] * BLOCK + within).reshape(seq_count, rows_seq)
    key_pos = (block_order[:, :, None] * BLOCK + within).reshape(seq_count, seq_len)
    key_block = min(512, seq_len)
    block_count = seq_len // key_block

    def key_scores(begin_row):
        key_part = lax.dynamic_slice_in_dim(key_heads, begin_row, key_block, 1)
        scores = block_scores(
            query_heads,
            key_part,
            query_pos,
            lax.dynamic_slice_in_dim(key_pos, begin_row, key_block, 1),
        )
        return (key_part, scores)

    def max_step(step_num, loop_state):
        running, summed = loop_state
        key_part, scores = key_scores(step_num * key_block)
        updated = jnp.maximum(running, jnp.max(scores, axis=-1))
        summed = summed * jnp.exp(running - updated) + jnp.sum(
            jnp.exp(scores - updated[..., None]), axis=-1
        )
        return (updated, summed)

    stat_shape = (seq_count, HEADS, rows_seq)
    running, summed = lax.fori_loop(
        0,
        block_count,
        max_step,
        (jnp.full(stat_shape, masked_fill, jnp.float32), jnp.zeros(stat_shape, jnp.float32)),
    )
    log_total = running + jnp.log(summed)

    def value_step(step_num, weighted):
        begin_row = step_num * key_block
        key_part, scores = key_scores(begin_row)
        prob_low = jnp.exp(scores - log_total[..., None]).astype(jnp.bfloat16)
        value_part = lax.dynamic_slice_in_dim(value_heads, begin_row, key_block, 1)
        return weighted + project(prob_low, value_part, "shqk,skhd->sqhd")

    weighted = lax.fori_loop(
        0, block_count, value_step, jnp.zeros((seq_count, rows_seq, HEADS, HEAD_DIM), jnp.float32)
    )
    attended = weighted.reshape(row_total, model_dim)
    attended_low = attended.astype(jnp.bfloat16)
    mixture = (
        tokens_wide + project(attended_low, full_wo, "re,ed->rd") + full_bo.astype(jnp.float32)
    )
    normed = layer_norm(mixture, full_g1.astype(jnp.float32), full_s1.astype(jnp.float32))
    normed_low = normed.astype(jnp.bfloat16)
    pre_act = project(normed_low, full_wu, "rd,df->rf") + full_bu.astype(jnp.float32)
    active_low = smooth_gelu(pre_act).astype(jnp.bfloat16)
    ffn_out = project(active_low, full_wd, "rf,fd->rd") + full_bd.astype(jnp.float32)
    summed_res = ffn_out + normed + tokens_wide
    layer_result = layer_norm(summed_res, full_g2.astype(jnp.float32), full_s2.astype(jnp.float32))
    back_wq, back_wk, back_wv, back_wo, back_wu, back_wd, back_g1, back_g2 = (
        lax.all_gather(w_query, "wt", axis=0, tiled=True),
        lax.all_gather(w_key, "wt", axis=0, tiled=True),
        lax.all_gather(w_value, "wt", axis=0, tiled=True),
        lax.all_gather(w_out, "wt", axis=0, tiled=True),
        lax.all_gather(w_up, "wt", axis=0, tiled=True),
        lax.all_gather(w_down, "wt", axis=0, tiled=True),
        lax.all_gather(gain_one, "wt", axis=0, tiled=True),
        lax.all_gather(gain_two, "wt", axis=0, tiled=True),
    )
    upstream = cotangent.reshape(row_total, model_dim).astype(jnp.float32)
    d_summed, second_gain, second_shift = norm_back(
        summed_res, back_g2.astype(jnp.float32), upstream
    )
    d_ffn = d_summed.astype(jnp.bfloat16)
    d_active = project(d_ffn, back_wd, "rd,fd->rf")
    gelu_value, gelu_pull = jax.vjp(smooth_gelu, pre_act)
    d_pre = gelu_pull(d_active)[0].astype(jnp.bfloat16)
    d_normed = d_summed + project(d_pre, back_wu, "rf,df->rd")
    d_mixture, first_gain, first_shift = norm_back(mixture, back_g1.astype(jnp.float32), d_normed)
    d_branch = d_mixture.astype(jnp.bfloat16)
    d_attended = project(d_branch, back_wo, "rd,ed->re").astype(jnp.bfloat16)
    row_delta = jnp.sum(
        (d_attended.astype(jnp.float32) * attended).reshape(seq_count, rows_seq, HEADS, HEAD_DIM),
        axis=-1,
    )
    delta_heads = jnp.transpose(row_delta, (0, 2, 1))
    grad_heads = d_attended.reshape(seq_count, rows_seq, HEADS, HEAD_DIM)

    def sweep_block(begin_row):
        key_part, scores = key_scores(begin_row)
        value_part = lax.dynamic_slice_in_dim(value_heads, begin_row, key_block, 1)
        prob_rows = jnp.exp(scores - log_total[..., None])
        d_probs = project(grad_heads, value_part, "sqhd,skhd->shqk")
        d_scores = (prob_rows * (d_probs - delta_heads[..., None])).astype(jnp.bfloat16)
        query_term = project(d_scores, key_part, "shqk,skhd->sqhd") * scale_factor
        return (prob_rows, d_scores, query_term)

    head_zeros = jnp.zeros((seq_count, rows_seq, HEADS, HEAD_DIM), jnp.float32)

    def both_step(step_num, loop_state):
        query_acc, key_acc, value_acc = loop_state
        begin_row = step_num * key_block
        prob_rows, d_scores, query_term = sweep_block(begin_row)
        key_term = project(d_scores, query_heads, "shqk,sqhd->skhd") * scale_factor
        value_term = project(prob_rows.astype(jnp.bfloat16), grad_heads, "shqk,sqhd->skhd")
        key_acc = lax.dynamic_update_slice_in_dim(key_acc, key_term, begin_row, 1)
        value_acc = lax.dynamic_update_slice_in_dim(value_acc, value_term, begin_row, 1)
        return (query_acc + query_term, key_acc, value_acc)

    all_zeros = jnp.zeros((seq_count, seq_len, HEADS, HEAD_DIM), jnp.float32)
    query_acc, key_acc, value_acc = lax.fori_loop(
        0, block_count, both_step, (head_zeros, all_zeros, all_zeros)
    )
    key_own, value_own = (
        lax.psum_scatter(
            key_acc.reshape(seq_count, seq_len, model_dim).astype(jnp.bfloat16),
            "ctx",
            scatter_dimension=1,
            tiled=True,
        ).astype(jnp.float32),
        lax.psum_scatter(
            value_acc.reshape(seq_count, seq_len, model_dim).astype(jnp.bfloat16),
            "ctx",
            scatter_dimension=1,
            tiled=True,
        ).astype(jnp.float32),
    )
    d_query = query_acc.reshape(row_total, model_dim).astype(jnp.bfloat16)
    d_key = key_own.reshape(row_total, model_dim).astype(jnp.bfloat16)
    d_value = value_own.reshape(row_total, model_dim).astype(jnp.bfloat16)
    grad_rows = (
        d_summed
        + d_mixture
        + project(d_query, back_wq, "re,de->rd")
        + project(d_key, back_wk, "re,de->rd")
        + project(d_value, back_wv, "re,de->rd")
    )
    local_grads = (
        project(tokens, d_query, "rd,re->de"),
        jnp.sum(d_query.astype(jnp.float32), axis=0),
        project(tokens, d_key, "rd,re->de"),
        project(tokens, d_value, "rd,re->de"),
        jnp.sum(d_value.astype(jnp.float32), axis=0),
        project(attended_low, d_branch, "re,rd->ed"),
        jnp.sum(d_branch.astype(jnp.float32), axis=0),
        first_gain,
        first_shift,
        project(normed_low, d_pre, "rd,rf->df"),
        jnp.sum(d_pre.astype(jnp.float32), axis=0),
        project(active_low, d_ffn, "rf,rd->fd"),
        jnp.sum(d_ffn.astype(jnp.float32), axis=0),
        second_gain,
        second_shift,
    )
    shards = (
        lax.psum_scatter(
            local_grads[0].astype(jnp.bfloat16), "wt", scatter_dimension=0, tiled=True
        ).astype(jnp.float32),
        lax.psum_scatter(
            local_grads[1].astype(jnp.bfloat16), "wt", scatter_dimension=0, tiled=True
        ).astype(jnp.float32),
        lax.psum_scatter(
            local_grads[2].astype(jnp.bfloat16), "wt", scatter_dimension=0, tiled=True
        ).astype(jnp.float32),
        lax.psum_scatter(
            local_grads[3].astype(jnp.bfloat16), "wt", scatter_dimension=0, tiled=True
        ).astype(jnp.float32),
        lax.psum_scatter(
            local_grads[4].astype(jnp.bfloat16), "wt", scatter_dimension=0, tiled=True
        ).astype(jnp.float32),
        lax.psum_scatter(
            local_grads[5].astype(jnp.bfloat16), "wt", scatter_dimension=0, tiled=True
        ).astype(jnp.float32),
        lax.psum_scatter(
            local_grads[6].astype(jnp.bfloat16), "wt", scatter_dimension=0, tiled=True
        ).astype(jnp.float32),
        lax.psum_scatter(
            local_grads[7].astype(jnp.bfloat16), "wt", scatter_dimension=0, tiled=True
        ).astype(jnp.float32),
        lax.psum_scatter(
            local_grads[8].astype(jnp.bfloat16), "wt", scatter_dimension=0, tiled=True
        ).astype(jnp.float32),
        lax.psum_scatter(
            local_grads[9].astype(jnp.bfloat16), "wt", scatter_dimension=0, tiled=True
        ).astype(jnp.float32),
        lax.psum_scatter(
            local_grads[10].astype(jnp.bfloat16), "wt", scatter_dimension=0, tiled=True
        ).astype(jnp.float32),
        lax.psum_scatter(
            local_grads[11].astype(jnp.bfloat16), "wt", scatter_dimension=0, tiled=True
        ).astype(jnp.float32),
        lax.psum_scatter(
            local_grads[12].astype(jnp.bfloat16), "wt", scatter_dimension=0, tiled=True
        ).astype(jnp.float32),
        lax.psum_scatter(
            local_grads[13].astype(jnp.bfloat16), "wt", scatter_dimension=0, tiled=True
        ).astype(jnp.float32),
        lax.psum_scatter(
            local_grads[14].astype(jnp.bfloat16), "wt", scatter_dimension=0, tiled=True
        ).astype(jnp.float32),
    )
    totals = (
        lax.psum(shards[0].astype(jnp.bfloat16), "ctx").astype(jnp.float32),
        lax.psum(shards[1].astype(jnp.bfloat16), "ctx").astype(jnp.float32),
        lax.psum(shards[2].astype(jnp.bfloat16), "ctx").astype(jnp.float32),
        lax.psum(shards[3].astype(jnp.bfloat16), "ctx").astype(jnp.float32),
        lax.psum(shards[4].astype(jnp.bfloat16), "ctx").astype(jnp.float32),
        lax.psum(shards[5].astype(jnp.bfloat16), "ctx").astype(jnp.float32),
        lax.psum(shards[6].astype(jnp.bfloat16), "ctx").astype(jnp.float32),
        lax.psum(shards[7].astype(jnp.bfloat16), "ctx").astype(jnp.float32),
        lax.psum(shards[8].astype(jnp.bfloat16), "ctx").astype(jnp.float32),
        lax.psum(shards[9].astype(jnp.bfloat16), "ctx").astype(jnp.float32),
        lax.psum(shards[10].astype(jnp.bfloat16), "ctx").astype(jnp.float32),
        lax.psum(shards[11].astype(jnp.bfloat16), "ctx").astype(jnp.float32),
        lax.psum(shards[12].astype(jnp.bfloat16), "ctx").astype(jnp.float32),
        lax.psum(shards[13].astype(jnp.bfloat16), "ctx").astype(jnp.float32),
        lax.psum(shards[14].astype(jnp.bfloat16), "ctx").astype(jnp.float32),
    )
    return (
        layer_result.reshape(seq_count, rows_seq, model_dim).astype(jnp.bfloat16),
        grad_rows.reshape(seq_count, rows_seq, model_dim).astype(jnp.bfloat16),
    ) + tuple(totals)


def solution(mesh):
    in_specs = (
        P("wt", "ctx", None),
        P("wt", None),
        P("wt", None),
        P("wt"),
        P("wt", None),
        P("wt", None),
        P("wt"),
        P("wt", None),
        P("wt"),
        P("wt"),
        P("wt"),
        P("wt", None),
        P("wt"),
        P("wt", None),
        P("wt"),
        P("wt"),
        P("wt"),
        P("wt", "ctx", None),
    )
    out_specs = (
        P("wt", "ctx", None),
        P("wt", "ctx", None),
        P("wt", None),
        P("wt"),
        P("wt", None),
        P("wt", None),
        P("wt"),
        P("wt", None),
        P("wt"),
        P("wt"),
        P("wt"),
        P("wt", None),
        P("wt"),
        P("wt", None),
        P("wt"),
        P("wt"),
        P("wt"),
    )
    return jax.shard_map(body, mesh=mesh, in_specs=in_specs, out_specs=out_specs, check_vma=False)
```

profile of v0, /device:TPU:0, one launch (start us, length us, event | category | flops | bytes accessed | tf_op | source)
XLA Modules:
  0.0 941.8 jit_solution(15241960359057708758)
XLA Ops:
  7.2 10.3 %all_gather.62 = bf16[512,512]{1,0:T(8,128)(2,1)S(1)} all-gather(bf16[256,512]{1,0:T(8,128)(2,1)} %param.28), channel_id=1, replica_groups=mesh['ctx'=16,'wt'=2] {'wt'}, dimensions={0}, use_global_device_ids=true | all-gather | bytes 786432 | tf_op jit(solution)/shard_map/all_gather | solution.py:85
  25.6 7.2 all_gather.59
  37.4 7.1 all_gather.64
  44.5 4.2 all-gather.1
  52.4 7.2 all_gather.66
  63.8 4.2 all-gather.3
  72.4 4.3 all_gather.71
  85.2 4.2 all-gather.7
  89.5 7.7 all-gather.15.cloned.1.call-done
  97.2 11.5 %copy.97 = bf16[2,4096,512]{1,2,0:T(8,128)(2,1)} copy(bf16[2,4096,512]{2,1,0:T(8,128)(2,1)} %all-gather.15.cloned.1.call-done) | data formatting | bytes 16777216 | tf_op jit(solution)/shard_map/all_gather | solution.py:109
  108.7 92.0 %while.48 = (s32[]{:T(128)}, f32[2,8,256]{2,1,0:T(8,128)S(1)}, f32[2,8,256]{2,1,0:T(8,128)S(1)}, s32[2,4096]{1,0:T(2,128)S(1)}, bf16[2,4096,8,64]{1,3,2,0:T(8,12...) while((s32[]{:T(128)}, f32[2,8,256]{2,1,0:T(8,128)S(1)}, ...), condition=%wide.region_3.4_spmd.clone, body=%wide.region_0.3_spmd.clone.sunk | while | flops 283398656 | bytes 19370172 | solution.py:146
  109.0 6.0 fusion.156
  114.9 5.1 exponential_reduce_fusion.2
  120.4 6.0 fusion.156
  126.4 5.1 exponential_reduce_fusion.2
  131.9 6.1 fusion.156
  138.0 5.2 exponential_reduce_fusion.2
  143.6 6.0 fusion.156
  149.5 5.2 exponential_reduce_fusion.2
  155.1 6.0 fusion.156
  161.1 5.1 exponential_reduce_fusion.2
  166.6 6.0 fusion.156
  172.5 5.1 exponential_reduce_fusion.2
  178.0 6.1 fusion.156
  184.1 5.1 exponential_reduce_fusion.2
  189.5 6.0 fusion.156
  195.5 5.1 exponential_reduce_fusion.2
  200.7 11.6 %copy.96 = bf16[2,4096,512]{1,2,0:T(8,128)(2,1)} copy(bf16[2,4096,512]{2,1,0:T(8,128)(2,1)} %all-gather.13.cloned.1.call-done) | data formatting | bytes 16777216 | tf_op jit(solution)/shard_map/all_gather | solution.py:110
  212.3 47.6 %while.49 = (s32[]{:T(128)}, f32[2,256,8,64]{1,3,2,0:T(8,128)}, bf16[2,4096,8,64]{1,3,2,0:T(8,128)(2,1)}, s32[2,4096]{1,0:T(2,128)S(1)}, bf16[2,4096,8,64]{1,3,2...) while((s32[]{:T(128)}, f32[2,256,8,64]{1,3,2,0:T(8,128)}, ...), condition=%wide.region_5.6_spmd.clone, body=%wide.region_4.5_spmd.clone.sunk | while | flops 546046464 | bytes 5281472 | solution.py:161
  212.6 5.5 fusion.162
  218.4 5.6 fusion.162
  224.4 5.6 fusion.162
  230.3 5.6 fusion.162
  236.2 5.6 fusion.162
  242.2 5.6 fusion.162
  248.1 5.6 fusion.162
  254.0 5.6 fusion.162
  266.2 5.3 fusion.83
  271.5 5.0 fusion.95
  279.6 4.5 fusion.88
  300.9 4.3 broadcast_in_dim.141
  305.2 4.3 broadcast_in_dim.141.clone
  309.4 155.9 %while.50 = (s32[]{:T(128)}, f32[2,256,8,64]{1,3,2,0:T(8,128)S(1)}, bf16[2,4096,8,64]{1,3,2,0:T(8,128)(2,1)}, bf16[2,4096,8,64]{1,3,2,0:T(8,128)(2,1)}, bf16[2,4...) while((s32[]{:T(128)}, f32[2,256,8,64]{1,3,2,0:T(8,128)S(1)}, ...), condition=%wide.region_16.17_spmd.clone, body=%wide.region_15.16_spmd.clone.sunk | while | flops 1364722176 | bytes 69013800 | solution.py:227
  320.8 4.6 fusion.174
  339.1 4.6 fusion.174
  357.6 4.6 fusion.174
  376.0 4.6 fusion.174
  394.6 4.6 fusion.174
  413.1 4.6 fusion.174
  431.5 4.6 fusion.174
  449.8 4.6 fusion.174
  469.9 4.8 convolution_convert_fusion.1
  474.8 6.3 convolution_convert_fusion
  481.1 88.0 %reduce-scatter.9.cloned.1.call-done = bf16[2,256,512]{1,2,0:T(8,128)(2,1)} async-done(((bf16[2,4096,512]{1,2,0:T(8,128)(2,1)}), bf16[2,256,512]{1,2,0:T(8,128)(2,1)}) %reduce-scatter.9.cloned.1.call-update) | async-done | bytes 524304 | tf_op jit(solution)/shard_map/reduce_scatter | solution.py:231
  571.5 106.2 %reduce-scatter.11.cloned.1.call-done = bf16[2,256,512]{1,2,0:T(8,128)(2,1)} async-done(((bf16[2,4096,512]{1,2,0:T(8,128)(2,1)}), bf16[2,256,512]{1,2,0:T(8,128)(2,1)}) %reduce-scatter.11.cloned.1.call-update) | async-done | bytes 524304 | tf_op jit(solution)/shard_map/reduce_scatter | solution.py:237
  680.3 14.0 %reduce-scatter.19.cloned.1.call-done = bf16[256,512]{1,0:T(8,128)(2,1)} async-done(((bf16[512,512]{1,0:T(8,128)(2,1)}), bf16[256,512]{1,0:T(8,128)(2,1)}) %reduce-scatter.19.cloned.1.call-update) | async-done | bytes 262160 | tf_op jit(solution)/shard_map/reduce_scatter | solution.py:287
  694.3 17.5 %reduce-scatter.13.cloned.1.call-done = bf16[256,512]{0,1:T(8,128)(2,1)} async-done(((bf16[512,512]{0,1:T(8,128)(2,1)}), bf16[256,512]{0,1:T(8,128)(2,1)}) %reduce-scatter.13.cloned.1.call-update) | async-done | bytes 262160 | tf_op jit(solution)/shard_map/reduce_scatter | solution.py:272
  711.8 34.7 %reduce-scatter.21.cloned.1.call-done = bf16[256,2048]{1,0:T(8,128)(2,1)} async-done(((bf16[512,2048]{1,0:T(8,128)(2,1)}), bf16[256,2048]{1,0:T(8,128)(2,1)}) %reduce-scatter.21.cloned.1.call-update) | async-done | bytes 1048592 | tf_op jit(solution)/shard_map/reduce_scatter | solution.py:299
  746.5 34.6 %reduce-scatter.23.cloned.1.call-done = bf16[1024,512]{1,0:T(8,128)(2,1)} async-done(((bf16[2048,512]{1,0:T(8,128)(2,1)}), bf16[1024,512]{1,0:T(8,128)(2,1)}) %reduce-scatter.23.cloned.1.call-update) | async-done | bytes 1048592 | tf_op jit(solution)/shard_map/reduce_scatter | solution.py:305
  781.1 17.4 %reduce-scatter.15.cloned.1.call-done = bf16[256,512]{0,1:T(8,128)(2,1)} async-done(((bf16[512,512]{0,1:T(8,128)(2,1)}), bf16[256,512]{0,1:T(8,128)(2,1)}) %reduce-scatter.15.cloned.1.call-update) | async-done | bytes 262160 | tf_op jit(solution)/shard_map/reduce_scatter | solution.py:278
  798.5 17.3 %reduce-scatter.17.cloned.1.call-done = bf16[256,512]{0,1:T(8,128)(2,1)} async-done(((bf16[512,512]{0,1:T(8,128)(2,1)}), bf16[256,512]{0,1:T(8,128)(2,1)}) %reduce-scatter.17.cloned.1.call-update) | async-done | bytes 262160 | tf_op jit(solution)/shard_map/reduce_scatter | solution.py:281
  821.7 7.0 all-reduce.11
  829.3 32.7 %all-reduce.9 = (bf16[256]{0:T(256)(128)(2,1)S(1)}, bf16[256]{0:T(256)(128)(2,1)S(1)}, bf16[256]{0:T(256)(128)(2,1)S(1)}, bf16[256]{0:T(256)(128)(2,1)S(1)}, bf1...) all-reduce(bf16[256]{0:T(256)(128)(2,1)S(1)} %dynamic-slice.1, ...), channel_id=1, replica_groups=mesh['ctx'=16,'wt'=2] {'ctx'}, use_global_device_ids=true, to_apply=%region_23.24 | all-reduce | flops 3072 | bytes 12288 | tf_op jit(solution)/shard_map/psum | solution.py:320
  871.7 53.9 %all-reduce.14.cloned.1.call-done = (bf16[256,512]{0,1:T(8,128)(2,1)}, bf16[256,512]{0,1:T(8,128)(2,1)}, bf16[256,512]{0,1:T(8,128)(2,1)}, bf16[256,512]{1,0:T(8...) async-done(((bf16[256,512]{0,1:T(8,128)(2,1)}, bf16[256,512]{0,1:T(8,128)(2,1)}, bf16[256,512]{0,1:T(8,128)(2,1)}, bf16[256,512]{1,0:T(8,128)(2,1)}, ...) | async-done | bytes 3145744 | tf_op jit(solution)/shard_map/psum | solution.py:319
  (395 shorter events, 208.1 us)
Async XLA Ops:
  7.2 30.2 %copy-start.23 = (bf16[256,512]{1,0:T(8,128)(2,1)S(1)}, bf16[256,512]{1,0:T(8,128)(2,1)}, u32[]{:S(2)}) copy-start(bf16[256,512]{1,0:T(8,128)(2,1)} %param.26) | copy-start | bytes 786436
  7.2 90.0 %all-gather.15.cloned.1.call-start = ((), (), s32[]{:S(2)}) async-start(), calls=%async_computation.9 | async-start | bytes 8912896 | tf_op jit(solution)/shard_map/all_gather | solution.py:109
  17.6 26.9 %copy-start.32 = (bf16[256]{0:T(256)(128)(2,1)S(1)}, bf16[256]{0:T(256)(128)(2,1)}, u32[]{:S(2)}) copy-start(bf16[256]{0:T(256)(128)(2,1)} %param.27) | copy-start | bytes 1540
  17.6 31.2 %copy-start.3 = (bf16[2,256,512]{2,1,0:T(8,128)(2,1)S(1)}, bf16[2,256,512]{2,1,0:T(8,128)(2,1)}, u32[]{:S(2)}) copy-start(bf16[2,256,512]{2,1,0:T(8,128)(2,1)} %param.24) | copy-start | bytes 1572868
  20.6 180.0 %all-gather.13.cloned.1.call-start = ((), (), s32[]{:S(2)}) async-start(), calls=%async_computation.8 | async-start | bytes 8912896 | tf_op jit(solution)/shard_map/all_gather | solution.py:110
  35.9 16.4 %copy-start.29 = (s32[2,32]{1,0:T(2,128)S(1)}, s32[2,32]{1,0:T(2,128)}, u32[]{:S(2)}) copy-start(s32[2,32]{1,0:T(2,128)} %param.25) | copy-start | bytes 772
  35.9 16.5 %copy-start.24 = (bf16[256,512]{1,0:T(8,128)(2,1)S(1)}, bf16[256,512]{1,0:T(8,128)(2,1)}, u32[]{:S(2)}) copy-start(bf16[256,512]{1,0:T(8,128)(2,1)} %param.31) | copy-start | bytes 786436
  35.9 23.7 %copy-start.33 = (bf16[256]{0:T(256)(128)(2,1)S(1)}, bf16[256]{0:T(256)(128)(2,1)}, u32[]{:S(2)}) copy-start(bf16[256]{0:T(256)(128)(2,1)} %param.32) | copy-start | bytes 1540
  35.9 27.9 %copy-start.34 = (bf16[256]{0:T(256)(128)(2,1)S(1)}, bf16[256]{0:T(256)(128)(2,1)}, u32[]{:S(2)}) copy-start(bf16[256]{0:T(256)(128)(2,1)} %param.33) | copy-start | bytes 1540
  36.0 230.2 %all-gather.17.cloned.1.call-start = ((), (), s32[]{:S(2)}) async-start(), calls=%async_computation.10 | async-start | bytes 3145728 | tf_op jit(solution)/shard_map/all_gather | solution.py:92
  36.7 31.4 %copy-start.35 = (bf16[256]{0:T(256)(128)(2,1)S(1)}, bf16[256]{0:T(256)(128)(2,1)}, u32[]{:S(2)}) copy-start(bf16[256]{0:T(256)(128)(2,1)} %param.34) | copy-start | bytes 1540
  36.7 35.7 %copy-start.30 = (bf16[1024]{0:T(1024)(128)(2,1)S(1)}, bf16[1024]{0:T(1024)(128)(2,1)}, u32[]{:S(2)}) copy-start(bf16[1024]{0:T(1024)(128)(2,1)} %param.36) | copy-start | bytes 6148
  36.7 40.0 %copy-start.36 = (bf16[256]{0:T(256)(128)(2,1)S(1)}, bf16[256]{0:T(256)(128)(2,1)}, u32[]{:S(2)}) copy-start(bf16[256]{0:T(256)(128)(2,1)} %param.38) | copy-start | bytes 1540
  36.7 44.2 %copy-start.37 = (bf16[256]{0:T(256)(128)(2,1)S(1)}, bf16[256]{0:T(256)(128)(2,1)}, u32[]{:S(2)}) copy-start(bf16[256]{0:T(256)(128)(2,1)} %param.39) | copy-start | bytes 1540
  36.7 48.5 %copy-start.38 = (bf16[256]{0:T(256)(128)(2,1)S(1)}, bf16[256]{0:T(256)(128)(2,1)}, u32[]{:S(2)}) copy-start(bf16[256]{0:T(256)(128)(2,1)} %param.40) | copy-start | bytes 1540
  36.8 234.8 %all-gather.19.cloned.1.call-start = ((), (), s32[]{:S(2)}) async-start(), calls=%async_computation.11 | async-start | bytes 3145728 | tf_op jit(solution)/shard_map/all_gather | solution.py:94
  37.3 531.8 %reduce-scatter.9.cloned.1.call-start = ((), (), s32[]{:S(2)}) async-start(), calls=%async_computation.12 | async-start | bytes 8912896 | tf_op jit(solution)/shard_map/reduce_scatter | solution.py:231
  44.5 5.5 copy-start.18
  271.5 5.3 copy-start.13
  276.5 2.3 copy-start.15
  276.5 3.1 copy-start.31
  278.7 5.5 copy-start.4
  278.8 5.3 copy-start.21
  279.6 4.5 copy-start.2
  279.6 4.5 copy-start.19
  284.1 1.7 copy-start.40
  285.8 1.7 copy-start.10
  285.8 1.7 copy-start.14
  287.5 1.7 copy-start.11
  317.8 2.9 copy-start.20
  325.3 2.0 copy-start
  336.2 2.9 copy-start.20
  343.7 2.0 copy-start
  354.7 2.9 copy-start.20
  362.2 2.0 copy-start
  373.1 2.9 copy-start.20
  380.6 2.0 copy-start
  391.6 2.9 copy-start.20
  399.1 2.0 copy-start
  410.1 2.9 copy-start.20
  417.6 2.0 copy-start
  428.6 2.9 copy-start.20
  436.1 2.0 copy-start
  446.9 2.9 copy-start.20
  454.4 2.0 copy-start
  465.4 212.4 %reduce-scatter.11.cloned.1.call-start = ((), (), s32[]{:S(2)}) async-start(), calls=%async_computation.13 | async-start | bytes 8912896 | tf_op jit(solution)/shard_map/reduce_scatter | solution.py:237
  465.4 1.0 copy-start.12
  465.9 228.4 %reduce-scatter.19.cloned.1.call-start = ((), (), s32[]{:S(2)}) async-start(), calls=%async_computation.17 | async-start | bytes 786432 | tf_op jit(solution)/shard_map/reduce_scatter | solution.py:287
  467.7 244.1 %reduce-scatter.13.cloned.1.call-start = ((), (), s32[]{:S(2)}) async-start(), calls=%async_computation.14 | async-start | bytes 786432 | tf_op jit(solution)/shard_map/reduce_scatter | solution.py:272
  469.9 4.9 copy-start.22
  469.9 276.6 %reduce-scatter.21.cloned.1.call-start = ((), (), s32[]{:S(2)}) async-start(), calls=%async_computation.18 | async-start | bytes 3145728 | tf_op jit(solution)/shard_map/reduce_scatter | solution.py:299
  474.7 306.4 %reduce-scatter.23.cloned.1.call-start = ((), (), s32[]{:S(2)}) async-start(), calls=%async_computation.19 | async-start | bytes 3145728 | tf_op jit(solution)/shard_map/reduce_scatter | solution.py:305
  481.1 336.0 %copy-start.39 = (u32[32]{0:T(128)S(1)}, u32[32]{0:T(128)}, u32[]{:S(2)}) copy-start(u32[32]{0:T(128)} %constant.187) | copy-start | bytes 388
  481.1 338.0 %copy-start.5 = (f32[512,512]{1,0:T(8,128)S(1)}, f32[512,512]{1,0:T(8,128)}, u32[]{:S(2)}) copy-start(f32[512,512]{1,0:T(8,128)} %copy-done.4) | copy-start | bytes 3145732
  481.1 338.0 %copy-start.7 = (f32[512,512]{1,0:T(8,128)S(1)}, f32[512,512]{1,0:T(8,128)}, u32[]{:S(2)}) copy-start(f32[512,512]{1,0:T(8,128)} %copy-done.6) | copy-start | bytes 3145732
  481.1 317.4 %reduce-scatter.15.cloned.1.call-start = ((), (), s32[]{:S(2)}) async-start(), calls=%async_computation.15 | async-start | bytes 786432 | tf_op jit(solution)/shard_map/reduce_scatter | solution.py:278
  571.5 244.4 %reduce-scatter.17.cloned.1.call-start = ((), (), s32[]{:S(2)}) async-start(), calls=%async_computation.16 | async-start | bytes 786432 | tf_op jit(solution)/shard_map/reduce_scatter | solution.py:281
  680.0 141.6 %copy-start.8 = (bf16[2,256,512]{1,2,0:T(8,128)(2,1)S(1)}, bf16[2,256,512]{1,2,0:T(8,128)(2,1)}, u32[]{:S(2)}) copy-start(bf16[2,256,512]{1,2,0:T(8,128)(2,1)} %reduce-scatter.11.cloned.1.call-done) | copy-start | bytes 1572868
  680.0 245.6 %all-reduce.14.cloned.1.call-start = ((), (), s32[]{:S(2)}) async-start(), calls=%async_computation.20 | async-start | bytes 6291456 | tf_op jit(solution)/shard_map/psum | solution.py:319
  821.6 48.9 %copy-start.17 = (bf16[512,512]{1,0:T(8,128)(2,1)S(1)}, bf16[512,512]{1,0:T(8,128)(2,1)}, u32[]{:S(2)}) copy-start(bf16[512,512]{1,0:T(8,128)(2,1)} %copy-done.16) | copy-start | bytes 1572868
  925.6 5.7 copy-start.28
  925.6 6.6 copy-start.27
  925.6 7.5 copy-start.26
  925.6 8.4 copy-start.25
  (4 other events, 3.6 us)
Sparse Core Ops, SparseCore 0:
  20.8 76.3 all-gather.14
  99.9 73.1 all-gather.12
  174.7 31.3 all-gather.16
  207.5 33.1 all-gather.18
  465.5 103.6 reduce-scatter.8
  573.1 104.5 reduce-scatter.10
  680.0 14.2 reduce-scatter.18
  697.2 14.5 reduce-scatter.12
  714.6 31.8 reduce-scatter.20
  749.2 31.8 reduce-scatter.22
  783.9 14.5 reduce-scatter.14
  801.3 14.5 reduce-scatter.16
  820.1 105.4 all-reduce.13
where the time goes:
time: 948 us; the launch traced here: 942 us
  waiting for transfers between devices  393 us (41%)
  matrix products  271 us (29%)
  blocking collectives  110 us (12%)
  local copies, waits for them, and re-layouts  75.5 us (8%)
  other arithmetic  66 us (7%)
  between operations  16 us (2%)
  loops' own time  9.82 us (1%)
    dot_general x74, matrix products, project(): return jnp.einsum(pattern, left, right, preferred_element_type=jnp.float32)  271 us
    reduce_scatter x1, waiting for transfers between devices, body(): lax.psum_scatter(value_acc.reshape(seq_count, seq_len, model_dim).astype(...  106 us
    reduce_scatter x1, waiting for transfers between devices, body(): lax.psum_scatter(key_acc.reshape(seq_count, seq_len, model_dim).astype(jn...  88 us
    psum x1, waiting for transfers between devices, body(): lax.psum(shards[0].astype(jnp.bfloat16), 'ctx').astype(jnp.float32)  53.9 us
    reduce_sum x8, other arithmetic, max_step(): jnp.sum(jnp.exp(scores - updated[..., None]), axis=-1)  41.1 us
    reduce_scatter x1, waiting for transfers between devices, body(): lax.psum_scatter(local_grads[9].astype(jnp.bfloat16), 'wt', scatter_dimen...  34.7 us
    reduce_scatter x1, waiting for transfers between devices, body(): lax.psum_scatter(local_grads[11].astype(jnp.bfloat16), 'wt', scatter_dime...  34.6 us
    psum x1, blocking collectives, body(): lax.psum(shards[1].astype(jnp.bfloat16), 'ctx').astype(jnp.float32)  32.7 us
  transfers between devices with their start and end apart: 13, of which 10 were waited for; matrix products, arithmetic and copies ran while one was open for 23% of the time, Pallas kernels for 0%

commit v1 on v0

v1 whole, which is shorter than its diff:
```python
import functools
import math

import jax
import jax.numpy as jnp
from jax import lax
from jax.experimental import pallas as pl
from jax.experimental.pallas import tpu as pltpu
from jax.sharding import PartitionSpec as P

norm_eps = 1e-05

BLOCK = 128
LOG2E = 1.4426950408889634
bf16, f32 = jnp.bfloat16, jnp.float32
NT = (((1,), (1,)), ((), ()))
TN = (((0,), (0,)), ((), ()))

def dot(a, b, dims=(((1,), (0,)), ((), ()))):
    return lax.dot_general(a, b, dims, preferred_element_type=f32)

def fwd_kernel(nb, blk_ref, x_ref, wq_ref, wkv_ref, bq_ref, bkv_ref,
               o_ref, lse_ref, k_ref, v_ref, qt_ref, q_ref, vt_s, qs_s, acc_s, m_s, l_s, d_s):
    qs_s[...] = jnp.zeros_like(qs_s)
    d_s[...] = lax.broadcasted_iota(jnp.int32, d_s.shape, 0) - (lax.broadcasted_iota(jnp.int32, d_s.shape, 1) & 127)
    def proj(p, _):
        x = x_ref[pl.ds(pl.multiple_of(p * 256, 256), 256), :]
        kv = dot(x, wkv_ref[...])
        k = kv[:, :256].astype(bf16)
        v = (kv[:, 256:] + bkv_ref[...]).astype(bf16)
        for u in range(2):
            r = pl.ds(pl.multiple_of(blk_ref[2 * p + u] * BLOCK, BLOCK), BLOCK)
            k_ref[r, :] = k[u * BLOCK:(u + 1) * BLOCK]
            vb = v[u * BLOCK:(u + 1) * BLOCK]
            v_ref[r, :] = vb
            vt_s[:, r] = vb.astype(f32).T.astype(bf16)
        return 0
    lax.fori_loop(0, nb // 2, proj, 0)
    def projq(p, _):
        x = x_ref[pl.ds(pl.multiple_of(p * 256, 256), 256), :]
        q = (dot(x, wq_ref[...]) + bq_ref[...]) * (LOG2E / 8.0)
        q_ref[pl.ds(pl.multiple_of(p * 256, 256), 256), :] = q.astype(bf16)
        for u in range(2):
            qt = q[u * BLOCK:(u + 1) * BLOCK].T.astype(bf16)
            qt_ref[2 * p + u] = qt
            for h in range(4):
                qs_s[2 * p + u, 64 * h:64 * h + 64, 128 * h:128 * h + 128] = qt[64 * h:64 * h + 64]
        return 0
    lax.fori_loop(0, 4, projq, 0)

    def pair(p, _):
        b0 = blk_ref[2 * p]
        first_lo = b0 < nb // 2
        lo = jnp.where(first_lo, b0, nb - 1 - b0)
        hi = nb - 1 - lo
        u_lo = 2 * p + jnp.where(first_lo, 0, 1)
        u_hi = 2 * p + jnp.where(first_lo, 1, 0)
        n_lo = lax.div(lo, 2)
        n_hi = lax.div(hi, 2)
        def scores(kt, u):
            return dot(k_ref[pl.ds(pl.multiple_of(kt * 256, 256), 256), :], qs_s[u])
        def pv(kt, p16):
            c = pl.ds(pl.multiple_of(kt * 256, 256), 256)
            return jnp.concatenate([dot(vt_s[0:128, c], p16[:, 0:256]), dot(vt_s[128:256, c], p16[:, 256:512])], axis=1)
        for (s, kt, u, qp) in ((0, n_lo, u_lo, lo), (1, n_hi, u_hi, hi)):
            st = scores(kt, u)
            st = jnp.where(d_s[...] <= qp * 128 - kt * 256, st, -1e30)
            m = jnp.max(st, axis=0, keepdims=True)
            pr = jnp.exp2(st - m)
            m_s[s] = m
            l_s[s] = jnp.sum(pr, axis=0, keepdims=True)
            acc_s[s] = pv(kt, pr.astype(bf16))
        for t in range(nb // 2 - 1):
            is_lo = t < n_lo
            s = jnp.where(is_lo, 0, 1)
            kt = jnp.where(is_lo, t, t - n_lo)
            u = jnp.where(is_lo, u_lo, u_hi)
            st = scores(kt, u)
            m_old = m_s[s]
            m = jnp.maximum(m_old, jnp.max(st, axis=0, keepdims=True))
            pr = jnp.exp2(st - m)
            al = jnp.exp2(m_old - m)
            m_s[s] = m
            l_s[s] = l_s[s] * al + jnp.sum(pr, axis=0, keepdims=True)
            acc_s[s] = acc_s[s] * al + pv(kt, pr.astype(bf16))
        for (s, u) in ((0, u_lo), (1, u_hi)):
            l = l_s[s]
            lse_ref[u] = m_s[s] + jnp.log2(l)
            a = acc_s[s] * (1.0 / l)
            ot = jnp.concatenate([a[64 * (h % 2):64 * (h % 2) + 64, 128 * h:128 * h + 128] for h in range(4)], axis=0)
            o_ref[pl.ds(pl.multiple_of(u * 128, 128), 128), :] = ot.T
        return 0
    lax.fori_loop(0, 4, pair, 0)

def attn_fwd(blk, x, wq, wkv, bq, bkv):
    nb = blk.shape[0]
    V = pl.BlockSpec(memory_space=pltpu.VMEM)
    return pl.pallas_call(
        functools.partial(fwd_kernel, nb),
        out_shape=(jax.ShapeDtypeStruct((1024, 256), f32), jax.ShapeDtypeStruct((8, 1, 512), f32),
                   jax.ShapeDtypeStruct((nb * 128, 256), bf16), jax.ShapeDtypeStruct((nb * 128, 256), bf16),
                   jax.ShapeDtypeStruct((8, 256, 128), bf16), jax.ShapeDtypeStruct((1024, 256), bf16)),
        in_specs=[pl.BlockSpec(memory_space=pltpu.SMEM)] + [V] * 5, out_specs=(V,) * 6,
        scratch_shapes=[pltpu.VMEM((256, nb * 128), bf16), pltpu.VMEM((8, 256, 512), bf16), pltpu.VMEM((2, 128, 512), f32),
                        pltpu.VMEM((2, 1, 512), f32), pltpu.VMEM((2, 1, 512), f32), pltpu.VMEM((256, 512), jnp.int32)],
        compiler_params=pltpu.CompilerParams(vmem_limit_bytes=56 << 20),
        name="attn_fwd")(blk, x, wq, wkv, bq, bkv)

def bwd_kernel(nb, blk_ref, x_ref, k_ref, v_ref, qt_ref, q_ref, lse_ref, do_ref, of_ref, wq_ref, wkv_ref,
               dx_ref, dw_ref, db_ref, dxq_s, dqa_s, kt_s, qs_s, qn_s, dot_s, don_s, dl_s, dk_s, dv_s, dq_s, d_s):
    qs_s[...] = jnp.zeros_like(qs_s)
    qn_s[...] = jnp.zeros_like(qn_s)
    dot_s[...] = jnp.zeros_like(dot_s)
    don_s[...] = jnp.zeros_like(don_s)
    dk_s[...] = jnp.zeros_like(dk_s)
    dv_s[...] = jnp.zeros_like(dv_s)
    d_s[...] = lax.broadcasted_iota(jnp.int32, d_s.shape, 0) - (lax.broadcasted_iota(jnp.int32, d_s.shape, 1) & 127)
    def prep_k(j, _):
        r = pl.ds(pl.multiple_of(j * 256, 256), 256)
        kt_s[:, r] = k_ref[r, :].astype(f32).T.astype(bf16)
        return 0
    lax.fori_loop(0, nb // 2, prep_k, 0)
    def prep_q(u, s):
        r = pl.ds(pl.multiple_of(u * 128, 128), 128)
        do = do_ref[r, :]
        doT = do.astype(f32).T
        dlT = doT * of_ref[r, :].T
        q = q_ref[r, :]
        qt = qt_ref[u]
        for h in range(4):
            hs = slice(64 * h, 64 * h + 64)
            cs = slice(128 * h, 128 * h + 128)
            qs_s[s, hs, cs] = qt[hs]
            dot_s[s, hs, cs] = doT[hs].astype(bf16)
            dl_s[s, :, cs] = jnp.sum(dlT[hs], axis=0, keepdims=True)
            qn_s[s, cs, hs] = q[:, hs]
            don_s[s, cs, hs] = do[:, hs]
    def pair(p, _):
        b0 = blk_ref[2 * p]
        first_lo = b0 < nb // 2
        lo = jnp.where(first_lo, b0, nb - 1 - b0)
        hi = nb - 1 - lo
        u_lo = 2 * p + jnp.where(first_lo, 0, 1)
        u_hi = 2 * p + jnp.where(first_lo, 1, 0)
        n_lo = lax.div(lo, 2)
        n_hi = lax.div(hi, 2)
        prep_q(u_lo, 0)
        prep_q(u_hi, 1)
        def step(s, kt, u, qp, masked):
            r = pl.ds(pl.multiple_of(kt * 256, 256), 256)
            st = dot(k_ref[r, :], qs_s[s]) - lse_ref[u]
            if masked:
                st = jnp.where(d_s[...] <= qp * 128 - kt * 256, st, -1e30)
            pr = jnp.exp2(st)
            dp = dot(v_ref[r, :], dot_s[s]) - dl_s[s]
            ds = (pr * dp).astype(bf16)
            dv_s[r, :] += dot(pr.astype(bf16), don_s[s])
            dk_s[r, :] += dot(ds, qn_s[s])
            dq = jnp.concatenate([dot(kt_s[0:128, r], ds[:, 0:256]), dot(kt_s[128:256, r], ds[:, 256:512])], axis=1)
            if masked:
                dq_s[s] = dq
            else:
                dq_s[s] += dq
        step(0, n_lo, u_lo, lo, True)
        step(1, n_hi, u_hi, hi, True)
        for t in range(nb // 2 - 1):
            is_lo = t < n_lo
            step(jnp.where(is_lo, 0, 1), jnp.where(is_lo, t, t - n_lo), jnp.where(is_lo, u_lo, u_hi), 0, False)
        for (s, u) in ((0, u_lo), (1, u_hi)):
            a = dq_s[s] * 0.125
            dqT = jnp.concatenate([a[64 * (h % 2):64 * (h % 2) + 64, 128 * h:128 * h + 128] for h in range(4)], axis=0)
            dqa_s[pl.ds(pl.multiple_of(u * 128, 128), 128), :] = dqT.T.astype(bf16)
        return 0
    lax.fori_loop(0, 4, pair, 0)
    dw_ref[...] = jnp.zeros_like(dw_ref)
    db_ref[...] = jnp.zeros_like(db_ref)
    def fin_q(u, _):
        r = pl.ds(pl.multiple_of(u * 128, 128), 128)
        dq = dqa_s[r, :]
        dxq_s[r, :] = dot(dq, wq_ref[...], NT)
        dw_ref[:, 0:256] += dot(x_ref[r, :], dq, TN)
        db_ref[0:1, :] += jnp.sum(dq.astype(f32), axis=0, keepdims=True)
        return 0
    lax.fori_loop(0, 8, fin_q, 0)
    def fin_k(b, with_q):
        r = pl.ds(pl.multiple_of(b * 128, 128), 128)
        g = pl.ds(pl.multiple_of(blk_ref[b] * 128, 128), 128)
        dkv = jnp.concatenate([(dk_s[g, :] * (1.0 / LOG2E)).astype(bf16), dv_s[g, :].astype(bf16)], axis=1)
        d = dot(dkv, wkv_ref[...], NT)
        if with_q:
            d = d + dxq_s[r, :]
        dx_ref[r, :] = d.astype(bf16)
        dw_ref[:, 256:768] += dot(x_ref[r, :], dkv, TN)
        db_ref[1:2, :] += jnp.sum(dkv[:, 256:].astype(f32), axis=0, keepdims=True)
    def fin_a(b, _):
        fin_k(b, True)
        return 0
    def fin_b(b, _):
        fin_k(b, False)
        return 0
    lax.fori_loop(0, 8, fin_a, 0)
    lax.fori_loop(8, nb, fin_b, 0)

def attn_bwd(blk, x, k, v, qt, q, lse, do, of, wq, wkv):
    nb = blk.shape[0]
    V = pl.BlockSpec(memory_space=pltpu.VMEM)
    return pl.pallas_call(
        functools.partial(bwd_kernel, nb),
        out_shape=(jax.ShapeDtypeStruct((nb * 128, 512), bf16), jax.ShapeDtypeStruct((512, 768), f32),
                   jax.ShapeDtypeStruct((8, 256), f32)),
        in_specs=[pl.BlockSpec(memory_space=pltpu.SMEM)] + [V] * 10, out_specs=(V,) * 3,
        scratch_shapes=[pltpu.VMEM((1024, 512), f32), pltpu.VMEM((1024, 256), bf16), pltpu.VMEM((256, nb * 128), bf16), pltpu.VMEM((2, 256, 512), bf16), pltpu.VMEM((2, 512, 256), bf16),
                        pltpu.VMEM((2, 256, 512), bf16), pltpu.VMEM((2, 512, 256), bf16), pltpu.VMEM((2, 1, 512), f32),
                        pltpu.VMEM((nb * 128, 256), f32), pltpu.VMEM((nb * 128, 256), f32), pltpu.VMEM((2, 128, 512), f32),
                        pltpu.VMEM((256, 512), jnp.int32)],
        compiler_params=pltpu.CompilerParams(vmem_limit_bytes=60 << 20),
        name="attn_bwd")(blk, x, k, v, qt, q, lse, do, of, wq, wkv)


def dense_kernel(x_ref, cot_ref, att_ref, wo_ref, wu_ref, wd_ref, vec_ref, bup_ref,
                 out_ref, dsm_ref, do_ref, gw_ref, gv_ref, act_s, gp_s, norm_s, dpre_s):
    ff = wu_ref.shape[1]
    chunk = 512
    x = x_ref[...].astype(f32)
    vec = lambda i: vec_ref[i:i + 1, :]
    b_out, g1, s1, b_down, g2, s2 = (vec(i) for i in range(6))
    mean = lambda v: jnp.mean(v, axis=-1, keepdims=True)
    col = lambda v: jnp.sum(v, axis=0, keepdims=True)
    mix = x + dot(att_ref[...], wo_ref[...]) + b_out
    cen = mix - mean(mix)
    r1 = lax.rsqrt(mean(cen * cen) + norm_eps)
    n1 = cen * r1
    normed = n1 * g1 + s1
    nlow = normed.astype(bf16)
    norm_s[...] = nlow
    ffn = None
    for f in range(0, ff, chunk):
        fs = slice(f, f + chunk)
        pre = dot(nlow, wu_ref[:, fs]) + bup_ref[:, fs]
        c0 = math.sqrt(2.0 / math.pi)
        sq = pre * pre
        th = jnp.tanh(c0 * pre * (1.0 + 0.044715 * sq))
        half = 0.5 * (1.0 + th)
        act = (pre * half).astype(bf16)
        act_s[:, fs] = act
        gp_s[:, fs] = half + 0.5 * pre * (1.0 - th * th) * (c0 * (1.0 + 3 * 0.044715 * sq))
        part = dot(act, wd_ref[fs, :])
        ffn = part if ffn is None else ffn + part
    summed = ffn + b_down + normed + x
    cen = summed - mean(summed)
    r2 = lax.rsqrt(mean(cen * cen) + norm_eps)
    n2 = cen * r2
    out_ref[...] = (n2 * g2 + s2).astype(bf16)
    up = cot_ref[...].astype(f32)
    gv_ref[4:5, :] = col(up * n2)
    gv_ref[5:6, :] = col(up)
    dn = up * g2
    dsum = r2 * (dn - mean(dn) - n2 * mean(dn * n2))
    dffn = dsum.astype(bf16)
    gv_ref[3:4, :] = col(dffn.astype(f32))
    dnorm = dsum
    half_rows = wo_ref.shape[0] // 2
    half_ff = ff // 2
    def put(g, at, rows):
        gw_ref[0, at:at + rows, :] = g[:rows].astype(bf16)
        gw_ref[1, at:at + rows, :] = g[rows:].astype(bf16)
    for f in range(0, ff, chunk):
        fs = slice(f, f + chunk)
        dact = dot(dffn, wd_ref[fs, :], NT)
        dpre = (dact * gp_s[:, fs]).astype(bf16)
        gv_ref[8 + f // chunk:9 + f // chunk, :] = col(dpre.astype(f32))
        dnorm = dnorm + dot(dpre, wu_ref[:, fs], NT)
        put(dot(norm_s[...], dpre, TN), half_rows + (f // chunk) * half_rows, half_rows)
        gd = dot(act_s[:, fs], dffn, TN).astype(bf16)
        base = half_rows * (1 + ff // chunk)
        which, off = f // half_ff, f % half_ff
        gw_ref[which, base + off:base + off + chunk, :] = gd
    gv_ref[1:2, :] = col(dnorm * n1)
    gv_ref[2:3, :] = col(dnorm)
    dn = dnorm * g1
    dmix = r1 * (dn - mean(dn) - n1 * mean(dn * n1))
    dsm_ref[...] = dsum + dmix
    dbr = dmix.astype(bf16)
    gv_ref[0:1, :] = col(dbr.astype(f32))
    do_ref[...] = dot(dbr, wo_ref[...], NT).astype(bf16)
    put(dot(att_ref[...], dbr, TN), 0, half_rows)


def dense(x, cot, att, wo, wu, wd, vecs, bup):
    V = pl.BlockSpec(memory_space=pltpu.VMEM)
    tok, dim = x.shape
    ff = wu.shape[1]
    rows = (2 * dim * ff + dim * dim) // 2 // dim
    return pl.pallas_call(
        dense_kernel,
        out_shape=(jax.ShapeDtypeStruct((tok, dim), bf16), jax.ShapeDtypeStruct((tok, dim), f32),
                   jax.ShapeDtypeStruct((tok, dim), bf16), jax.ShapeDtypeStruct((2, rows, dim), bf16),
                   jax.ShapeDtypeStruct((16, dim), f32)),
        in_specs=[V] * 8, out_specs=(V,) * 5,
        scratch_shapes=[pltpu.VMEM((tok, ff), bf16), pltpu.VMEM((tok, ff), f32), pltpu.VMEM((tok, dim), bf16),
                        pltpu.VMEM((8, 128), f32)],
        compiler_params=pltpu.CompilerParams(vmem_limit_bytes=56 << 20),
        name="dense")(x, cot, att, wo, wu, wd, vecs, bup)


def body(block_in, block_order, w_query, b_query, w_key, w_value, b_value, w_out, b_out, gain_one, shift_one,
         w_up, b_up, w_down, b_down, gain_two, shift_two, cotangent, *, nc, nw):
    seqs, rows, dim = block_in.shape
    nz = nc // 4
    hb = rows // BLOCK
    half = dim // 2
    me = lax.axis_index("ctx")
    yy = (me // 2) % 2
    cc = me % 2
    zz = me // 4
    xor = lambda v: [(i, i ^ v) for i in range(nc)]
    ring = [(i, ((i // 4 + 1) % nz) * 4 + i % 4) for i in range(nc)]
    perm = lambda v, p: lax.ppermute(v, "ctx", p)
    gather = lambda v: lax.all_gather(v, "wt", axis=0, tiled=True)
    pick = lambda v, i: lax.dynamic_index_in_dim(v, i, 0, keepdims=False)

    cols = lambda w: lax.dynamic_slice_in_dim(w, cc * half, half, 1)
    wqkv = gather(jnp.concatenate([cols(w_query), cols(w_key), cols(w_value)], axis=1))
    wq, wkv = wqkv[:, :half], wqkv[:, half:]
    small = jnp.concatenate([v.reshape(-1, dim // nw) for v in (b_query, b_value, b_out, gain_one, shift_one, b_down, gain_two, shift_two, b_up)], axis=0)
    small = lax.all_gather(small, "wt", axis=0)
    ffr = b_up.shape[0] // (dim // nw)
    vecs = jnp.transpose(small[:, :8], (1, 0, 2)).reshape(8, dim).astype(f32)
    bup = small[:, 8:].reshape(1, -1).astype(f32)
    bq = lax.dynamic_slice_in_dim(vecs[0:1], cc * half, half, 1)
    bv = lax.dynamic_slice_in_dim(vecs[1:2], cc * half, half, 1)
    bkv = bv
    dvec = vecs[2:8]

    own = pick(block_in, yy)
    got = perm(pick(block_in, 1 - yy), xor(2))
    ring_x = jnp.concatenate([own, got], axis=0)
    pieces = []
    for r in range(nz):
        pieces += [ring_x, perm(ring_x, xor(1))]
        if r < nz - 1:
            ring_x = perm(ring_x, ring)
    x_all = jnp.concatenate(pieces, axis=0)
    r_ids = (zz - jnp.arange(nz, dtype=jnp.int32)) % nz
    quad = (me % 4) ^ jnp.array([0, 2, 1, 3], jnp.int32)
    order_row = pick(block_order, yy)
    slots = (r_ids[:, None, None] * 4 + quad[None, :, None]) * hb + jnp.arange(hb, dtype=jnp.int32)
    blk = order_row[slots.reshape(-1)]

    wo, wu, wd = gather(w_out), gather(w_up), gather(w_down)
    o, lse, k, v, qt, q = attn_fwd(blk, x_all, wq, wkv, bq, bkv)
    o16 = o.astype(bf16)
    o_self = o16[:rows]
    o_y = perm(o16[rows:2 * rows], xor(2))
    o_c = perm(o16[2 * rows:3 * rows], xor(1))
    o_yc = perm(o16[3 * rows:], xor(3))
    by_seq = lambda a, b: jnp.where(yy == 0, jnp.concatenate([a, b], 0), jnp.concatenate([b, a], 0))
    mine, other = by_seq(o_self, o_y), by_seq(o_c, o_yc)
    att = jnp.where(cc == 0, jnp.concatenate([mine, other], 1), jnp.concatenate([other, mine], 1))

    out, dsm, d_o, gw, gv = dense(block_in.reshape(-1, dim), cotangent.reshape(-1, dim), att, wo, wu, wd, dvec, bup)

    d_o = d_o.reshape(seqs, rows, dim)
    d_own, d_oth = pick(d_o, yy), pick(d_o, 1 - yy)
    fh = lambda v, c: lax.dynamic_slice_in_dim(v, c * half, half, 1)
    do_all = jnp.concatenate([fh(d_own, cc), perm(fh(d_oth, cc), xor(2)), perm(fh(d_own, 1 - cc), xor(1)), perm(fh(d_oth, 1 - cc), xor(3))], axis=0)
    dx, gq, gb = attn_bwd(blk, x_all, k, v, qt, q, lse, do_all, o, wq, wkv)
    dx = dx.reshape(nz, 2, 2 * rows, dim)
    part = lambda r: dx[r, 0].astype(f32) + perm(dx[r, 1], xor(1)).astype(f32)
    acc = None
    for r in list(range(1, nz)) + [0]:
        acc = part(r) if acc is None else perm(acc.astype(bf16), ring).astype(f32) + part(r)
    from_y = perm(acc[rows:].astype(bf16), xor(2)).astype(f32)
    dkv_sum = by_seq(acc[:rows], from_y)
    grad_in = (dsm + dkv_sum).astype(bf16).reshape(seqs, rows, dim)

    gvec = jnp.zeros((18, dim), f32).at[:16].set(gv)
    gvec = lax.dynamic_update_slice(gvec, gb[0:1], (16, cc * half))
    gvec = lax.dynamic_update_slice(gvec, gb[1:2], (17, cc * half))
    gvec = lax.psum(gvec, ("ctx", "wt"))
    wi = lax.axis_index("wt")
    def share(vv):
        n = vv.size // nw
        return lax.dynamic_slice_in_dim(vv.reshape(-1), wi * n, n, 0)
    rr = w_query.shape[0]
    ff = w_up.shape[1]
    hr = dim // 2
    g_out = gw[:, :hr].reshape(dim, dim)
    g_up = gw[:, hr:hr + (ff // dim) * hr].reshape(2, ff // dim, hr, dim).transpose(0, 2, 1, 3).reshape(dim, ff)
    g_down = gw[:, hr + (ff // dim) * hr:].reshape(ff, dim)
    zq = jnp.zeros((3, dim, dim), bf16)
    gq3 = gq.astype(bf16).reshape(dim, 3, half).transpose(1, 0, 2)
    g_qkv = lax.dynamic_update_slice(zq, gq3, (0, 0, cc * half))
    def total(g):
        s = lax.psum_scatter(g, "wt", scatter_dimension=0, tiled=True)
        return lax.psum(s, "ctx").astype(f32)
    gqkv = [total(g_qkv[i]) for i in range(3)]
    return (out.reshape(seqs, rows, dim), grad_in, gqkv[0], share(gvec[16]), gqkv[1], gqkv[2], share(gvec[17]), total(g_out), share(gvec[0]),
            share(gvec[1]), share(gvec[2]), total(g_up), share(gvec[8:8 + ff // dim]), total(g_down), share(gvec[3]), share(gvec[4]), share(gvec[5]))


def solution(mesh):
    seq, mat, vec = P("wt", "ctx", None), P("wt", None), P("wt")
    ins = (seq, mat, mat, vec, mat, mat, vec, mat, vec, vec, vec, mat, vec, mat, vec, vec, vec, seq)
    outs = (seq, seq, mat, vec, mat, mat, vec, mat, vec, vec, vec, mat, vec, mat, vec, vec, vec)
    run = functools.partial(body, nc=mesh.shape["ctx"], nw=mesh.shape["wt"])
    return jax.shard_map(run, mesh=mesh, in_specs=ins, out_specs=outs, check_vma=False)
```

time: 948 us -> 453 us (0.48)
  matrix products: 271 us -> 0 us
  waiting for transfers between devices: 393 us -> 190 us
  Pallas kernels: 0 us -> 101 us
  other arithmetic: 66 us -> 20.8 us
  blocking collectives: 110 us -> 66.7 us
  local copies, waits for them, and re-layouts: 75.5 us -> 43.7 us
  starting transfers between devices: 0.74 us -> 15.8 us
  loops' own time: 9.82 us -> 0 us
    reduce_scatter x8 -> x6, waiting for transfers between devices: 330 us -> 42.8 us  [total(): s = lax.psum_scatter(g, 'wt', scatter_dimension=0, tiled=True)]
    dot_general x74 -> x0, matrix products: 271 us -> none  [project(): return jnp.einsum(pattern, left, right, preferred_element_type=jnp.float32)]
    pallas_call x0 -> x3, Pallas kernels: none -> 101 us  [the longest x1 50.8 us: attn_bwd(): pl.pallas_call(functools.partial(bwd_kernel, nb), out_shape=(jax.ShapeDty...]
    ppermute x0 -> x22, waiting for transfers between devices: none -> 65 us  [body(): perm = lambda v, p: lax.ppermute(v, 'ctx', p)]
    reduce_sum x19 -> x0, other arithmetic: 47.1 us -> none  [the longest x8 41.1 us: max_step(): jnp.sum(jnp.exp(scores - updated[..., None]), axis=-1)]
    all_gather x13 -> x3, blocking collectives: 70 us -> 26.7 us  [the longest x2 22.2 us: body(): gather = lambda v: lax.all_gather(v, 'wt', axis=0, tiled=True)]
    psum x1, waiting for transfers between devices: 53.9 us -> 79.2 us  [total(): return lax.psum(s, 'ctx').astype(f32)]
    all_gather x2 -> x0, local copies, waits for them, and re-layouts: 23.1 us -> none  [the longest x1 11.6 us: body(): lax.all_gather(value_rows.reshape(seq_count, rows_seq, model_dim), 'ctx',...]
  transfers between devices with their start and end apart: 13 -> 31, of which waited for: 10 -> 12; matrix products, arithmetic and copies ran while one was open for 23% -> 12% of each run, Pallas kernels for 0% -> 19%
where the time goes in v1:
time: 453 us; the launch traced here: 452 us
  waiting for transfers between devices  190 us (42%)
  Pallas kernels  101 us (22%)
  blocking collectives  66.7 us (15%)
  local copies, waits for them, and re-layouts  43.7 us (10%)
  other arithmetic  20.8 us (5%)
  starting transfers between devices  15.8 us (3%)
  between operations  14.3 us (3%)
    psum x1, waiting for transfers between devices, total(): return lax.psum(s, 'ctx').astype(f32)  79.2 us
    ppermute x22, waiting for transfers between devices, body(): perm = lambda v, p: lax.ppermute(v, 'ctx', p)  65 us
    pallas_call x1, Pallas kernels, attn_bwd(): pl.pallas_call(functools.partial(bwd_kernel, nb), out_shape=(jax.ShapeDty...  50.8 us
    reduce_scatter x6, waiting for transfers between devices, total(): s = lax.psum_scatter(g, 'wt', scatter_dimension=0, tiled=True)  42.8 us
    psum x1, blocking collectives, body(): gvec = lax.psum(gvec, ('ctx', 'wt'))  39.9 us
    pallas_call x1, Pallas kernels, attn_fwd(): pl.pallas_call(functools.partial(fwd_kernel, nb), out_shape=(jax.ShapeDty...  36 us
    all_gather x2, blocking collectives, body(): gather = lambda v: lax.all_gather(v, 'wt', axis=0, tiled=True)  22.2 us
    ppermute x22, starting transfers between devices, body(): perm = lambda v, p: lax.ppermute(v, 'ctx', p)  15 us
  transfers between devices with their start and end apart: 31, of which 12 were waited for; matrix products, arithmetic and copies ran while one was open for 12% of the time, Pallas kernels for 19%

profile of v1, /device:TPU:0, one launch (start us, length us, event | category | flops | bytes accessed | tf_op | source)
XLA Modules:
  0.0 452.3 jit_solution(13520635642655035372)
XLA Ops:
  8.0 1.0 dynamic-slice_bitcast_fusion
  9.0 3.0 collective-permute-start
  12.1 1.7 constant_dynamic-update-slice_fusion.8
  14.6 1.0 constant_dynamic-slice_fusion.10
  21.8 4.5 all-gather.1
  26.3 1.6 collective-permute-start.2
  28.0 12.8 %collective-permute-done.2 = bf16[512,512]{1,0:T(8,128)(2,1)S(1)} collective-permute-done((bf16[512,512]{1,0:T(8,128)(2,1)S(1)}, bf16[512,512]{1,0:T(8,128)(2,1)S(1)}, u32[]{:S(2)}, u32[]{:S(2)}) %collective-permute-start.2) | collective-permute-done | bytes 524320 | tf_op jit(solution)/shard_map/ppermute | solution.py:318
  40.9 12.9 %all_gather.18 = bf16[512,768]{1,0:T(8,128)(2,1)S(1)} all-gather(bf16[256,768]{1,0:T(8,128)(2,1)S(1)} %pad_maximum_fusion.2), channel_id=1, replica_groups=mesh['ctx'=16,'wt'=2] {'wt'}, dimensions={0}, use_global_device_ids=true | all-gather | bytes 1179648 | tf_op jit(solution)/shard_map/all_gather | solution.py:319
  54.3 1.0 collective-permute-start.6
  55.3 0.8 slice.184.wkv_ref
  56.2 0.7 slice.183.wq_ref
  56.9 1.2 gather_fusion
  59.2 0.7 constant_dynamic-update-slice_fusion.7
  59.9 1.9 constant_dynamic-update-slice_fusion.6
  61.8 7.6 %collective-permute-done.6 = bf16[512,512]{1,0:T(8,128)(2,1)S(1)} collective-permute-done((bf16[512,512]{1,0:T(8,128)(2,1)S(1)}, bf16[512,512]{1,0:T(8,128)(2,1)S(1)}, u32[]{:S(2)}, u32[]{:S(2)}) %collective-permute-start.6) | collective-permute-done | bytes 524320 | tf_op jit(solution)/shard_map/ppermute | solution.py:318
  69.4 0.8 constant_dynamic-update-slice_fusion.5
  70.2 0.8 constant_dynamic-update-slice_fusion.4
  71.1 0.8 constant_dynamic-update-slice_fusion.3
  71.9 0.9 constant_dynamic-update-slice_fusion.2
  72.7 0.9 constant_dynamic-update-slice_fusion.1
  73.6 0.9 constant_dynamic-update-slice_fusion.x_ref
  74.5 36.0 %attn_fwd.1 = (f32[1024,256]{1,0:T(8,128)}, f32[8,1,512]{2,1,0:T(1,128)}, bf16[4096,256]{1,0:T(8,128)(2,1)}, bf16[4096,256]{1,0:T(8,128)(2,1)}, bf16[8,256,128]{2,1,0:T(8,128)(2,1)}, /*index=5*/bf16[1024,256]{1,0:T(8,128)(2,1)}) custom-call(s32[32]{0:T(128)} %gather_fusion, bf16[4096,512]{1,0:T(8,128)(2,1)} %constant_dynamic-update-slice_fusion.x_ref, ...), custom_call_target="tpu_custom_call" | custom-call | tf_op jit(solution)/shard_map/attn_fwd/pallas_call | solution.py:98
  110.5 1.3 convert_element_type.99
  111.8 1.5 collective-permute-start.8
  114.0 9.4 %all_gather.21.wo_ref = bf16[512,512]{1,0:T(8,128)(2,1)} all-gather(bf16[256,512]{1,0:T(8,128)(2,1)S(1)} %copy-done.3), channel_id=1, replica_groups=mesh['ctx'=16,'wt'=2] {'wt'}, dimensions={0}, use_global_device_ids=true | all-gather | bytes 786432 | tf_op jit(solution)/shard_map/all_gather | solution.py:319
  124.9 0.9 maximum_select_fusion.1.att_ref
  125.8 14.7 %dense.1 = (bf16[512,512]{1,0:T(8,128)(2,1)}, f32[512,512]{1,0:T(8,128)}, bf16[512,512]{1,0:T(8,128)(2,1)}, bf16[2,2304,512]{2,1,0:T(8,128)(2,1)}, f32[16,512]{1,0:T(8,128)}) custom-call(bf16[512,512]{1,0:T(8,128)(2,1)} %bitcast.95, bf16[512,512]{1,0:T(8,128)(2,1)} %bitcast.97, bf16[512,512]{1,0:T(8,128)(2,1)} %maximum_select_fusion.1.att_ref, ...), custom_call_target="tpu_custom_call" | custom-call | tf_op jit(solution)/shard_map/dense/pallas_call | solution.py:294
  140.5 1.9 slice.171
  142.7 1.4 dynamic-slice_bitcast_fusion.5
  144.1 1.5 collective-permute-start.11
  146.3 3.4 collective-permute-done.11
  149.6 1.7 collective-permute-done.13
  151.4 0.8 pad_maximum_fusion.1.do_ref
  152.2 50.8 %attn_bwd.1 = (bf16[4096,512]{1,0:T(8,128)(2,1)}, f32[512,768]{1,0:T(8,128)}, f32[8,256]{1,0:T(8,128)}) custom-call(s32[32]{0:T(128)} %gather_fusion, bf16[4096,512]{1,0:T(8,128)(2,1)} %constant_dynamic-update-slice_fusion.x_ref, bf16[4096,256]{1,0:T(8,128)(2,1)} %get-tuple-element.46.k_ref, bf16[4096,256]{1,0:T(8,128)(2,1)} %get-tuple-element.47.v_ref, ...), custom_call_target="tpu_custom_call" | custom-call | tf_op jit(solution)/shard_map/attn_bwd/pallas_call | solution.py:207
  203.0 1.5 convert_element_type.122
  205.2 1.2 slice_bitcast_fusion
  207.7 3.8 fusion.12
  211.5 1.6 copy.43
  213.1 1.9 copy.44
  215.1 0.7 reduce-scatter.17.cloned.1.call-update
  216.1 2.5 slice_bitcast_fusion.9
  218.7 0.7 collective-permute-start.14
  219.4 1.5 collective-permute-done.14
  220.9 1.2 fusion.7
  222.7 15.5 %collective-permute-done.15 = bf16[512,512]{1,0:T(8,128)(2,1)S(1)} collective-permute-done((bf16[512,512]{1,0:T(8,128)(2,1)S(1)}, bf16[512,512]{1,0:T(8,128)(2,1)S(1)}, u32[]{:S(2)}, u32[]{:S(2)}) %collective-permute-start.15) | collective-permute-done | bytes 524320 | tf_op jit(solution)/shard_map/ppermute | solution.py:318
  238.2 1.2 fusion.6
  239.5 0.8 fusion.16
  240.8 39.9 %psum.50 = f32[18,512]{1,0:T(8,128)S(1)} all-reduce(f32[18,512]{1,0:T(8,128)S(1)} %dynamic_update_slice.11), channel_id=1, replica_groups=mesh['ctx'=16,'wt'=2] {'ctx','wt'}, use_global_device_ids=true, to_apply=%region_2.3 | all-reduce | flops 9216 | bytes 73728 | tf_op jit(solution)/shard_map/psum | solution.py:380
  281.9 8.0 %reduce-scatter.15.cloned.1.call-done = bf16[256,2048]{1,0:T(8,128)(2,1)} async-done(((bf16[512,2048]{1,0:T(8,128)(2,1)}), bf16[256,2048]{1,0:T(8,128)(2,1)}) %reduce-scatter.15.cloned.1.call-update) | async-done | bytes 1048592 | tf_op jit(solution)/shard_map/reduce_scatter | solution.py:395
  289.9 34.8 %reduce-scatter.17.cloned.1.call-done = bf16[1024,512]{1,0:T(8,128)(2,1)} async-done(((bf16[2048,512]{1,0:T(8,128)(2,1)}), bf16[1024,512]{1,0:T(8,128)(2,1)}) %reduce-scatter.17.cloned.1.call-update) | async-done | bytes 1048592 | tf_op jit(solution)/shard_map/reduce_scatter | solution.py:395
  324.7 1.3 fusion.4
  326.0 1.5 collective-permute-start.19
  329.2 16.6 %collective-permute-done.19 = bf16[512,512]{1,0:T(8,128)(2,1)S(1)} collective-permute-done((bf16[512,512]{1,0:T(8,128)(2,1)S(1)}, bf16[512,512]{1,0:T(8,128)(2,1)S(1)}, u32[]{:S(2)}, u32[]{:S(2)}) %collective-permute-start.19) | collective-permute-done | bytes 524320 | tf_op jit(solution)/shard_map/ppermute | solution.py:318
  345.8 1.2 fusion.2
  347.1 1.5 collective-permute-start.21
  351.0 5.3 %collective-permute-done.21 = bf16[256,512]{1,0:T(8,128)(2,1)S(1)} collective-permute-done((bf16[256,512]{1,0:T(8,128)(2,1)S(1)}, bf16[256,512]{1,0:T(8,128)(2,1)S(1)}, u32[]{:S(2)}, u32[]{:S(2)}) %collective-permute-start.21) | collective-permute-done | bytes 262176 | tf_op jit(solution)/shard_map/ppermute | solution.py:318
  356.3 1.1 fusion.1
  357.4 79.2 %all-reduce.4.cloned.1.call-done = (bf16[256,512]{1,0:T(8,128)(2,1)}, bf16[256,512]{1,0:T(8,128)(2,1)}, bf16[256,512]{1,0:T(8,128)(2,1)}, bf16[256,512]{1,0:T(8,...) async-done(((bf16[256,512]{1,0:T(8,128)(2,1)}, bf16[256,512]{1,0:T(8,128)(2,1)}, bf16[256,512]{1,0:T(8,128)(2,1)}, bf16[256,512]{1,0:T(8,128)(2,1)}, ...) | async-done | bytes 3145744 | tf_op jit(solution)/shard_map/psum | solution.py:396
  436.6 2.9 convert_element_type.127
  439.5 2.8 convert_element_type.128
  442.3 0.9 convert_element_type.123
  443.2 0.9 convert_element_type.124
  444.1 0.9 convert_element_type.125
  444.9 0.9 convert_element_type.126
  (122 shorter events, 21.3 us)
Async XLA Ops:
  7.2 20.8 %copy-start = (bf16[256,512]{1,0:T(8,128)(2,1)S(1)}, bf16[256,512]{1,0:T(8,128)(2,1)}, u32[]{:S(2)}) copy-start(bf16[256,512]{1,0:T(8,128)(2,1)} %param.23) | copy-start | bytes 786436
  7.2 48.1 %copy-start.9 = (s32[2,32]{1,0:T(2,128)S(1)}, s32[2,32]{1,0:T(2,128)}, u32[]{:S(2)}) copy-start(s32[2,32]{1,0:T(2,128)} %param.22) | copy-start | bytes 772
  7.2 118.6 %all-gather.5.cloned.1.call-start = ((), (), s32[]{:S(2)}) async-start(), calls=%async_computation.6 | async-start | bytes 3145728 | tf_op jit(solution)/shard_map/all_gather | solution.py:319
  7.9 117.9 %all-gather.7.cloned.1.call-start = ((), (), s32[]{:S(2)}) async-start(), calls=%async_computation.7 | async-start | bytes 3145728 | tf_op jit(solution)/shard_map/all_gather | solution.py:319
  9.0 17.3 %collective-permute-start = (bf16[256,512]{1,0:T(8,128)(2,1)S(1)}, bf16[256,512]{1,0:T(8,128)(2,1)S(1)}, u32[]{:S(2)}, u32[]{:S(2)}) collective-permute-start(bf16[256,512]{1,0:T(8,128)(2,1)S(1)} %dynamic-slice_bitcast_fusion), channel_id=1, source_target_pairs={{0,4},{2,6},{4,0},{6,2},{8,12},{10,14},{12,8},{14,10},{16,20},{18,... | collective-permute-start | bytes 786440 | tf_op jit(solution)/shard_map/ppermute | solution.py:318
  12.1 269.8 %reduce-scatter.13.cloned.1.call-start = ((), (), s32[]{:S(2)}) async-start(), calls=%async_computation.11 | async-start | bytes 786432 | tf_op jit(solution)/shard_map/reduce_scatter | solution.py:395
  26.3 14.5 %collective-permute-start.2 = (bf16[512,512]{1,0:T(8,128)(2,1)S(1)}, bf16[512,512]{1,0:T(8,128)(2,1)S(1)}, u32[]{:S(2)}, u32[]{:S(2)}) collective-permute-start(bf16[512,512]{1,0:T(8,128)(2,1)S(1)} %pad_maximum_fusion), channel_id=1, source_target_pairs={{0,8},{2,10},{4,12},{6,14},{8,16},{10,18},{12,20},{14,22},{16,24},... | collective-permute-start | bytes 1572872 | tf_op jit(solution)/shard_map/ppermute | solution.py:318
  40.8 13.5 %collective-permute-start.4 = (bf16[512,512]{1,0:T(8,128)(2,1)S(1)}, bf16[512,512]{1,0:T(8,128)(2,1)S(1)}, u32[]{:S(2)}, u32[]{:S(2)}) collective-permute-start(bf16[512,512]{1,0:T(8,128)(2,1)S(1)} %collective-permute-done.2), channel_id=1, source_target_pairs={{0,8},{2,10},{4,12},{6,14},{8,16},{10,18},{12,20},{14,22},{16,24},... | collective-permute-start | bytes 1572872 | tf_op jit(solution)/shard_map/ppermute | solution.py:318
  40.8 19.0 %collective-permute-start.1 = (bf16[512,512]{1,0:T(8,128)(2,1)S(1)}, bf16[512,512]{1,0:T(8,128)(2,1)}, u32[]{:S(2)}, u32[]{:S(2)}) collective-permute-start(bf16[512,512]{1,0:T(8,128)(2,1)S(1)} %pad_maximum_fusion), channel_id=1, source_target_pairs={{0,2},{2,0},{4,6},{6,4},{8,10},{10,8},{12,14},{14,12},{16,18},{18,... | collective-permute-start | bytes 1572872 | tf_op jit(solution)/shard_map/ppermute | solution.py:318
  54.3 15.1 %collective-permute-start.6 = (bf16[512,512]{1,0:T(8,128)(2,1)S(1)}, bf16[512,512]{1,0:T(8,128)(2,1)S(1)}, u32[]{:S(2)}, u32[]{:S(2)}) collective-permute-start(bf16[512,512]{1,0:T(8,128)(2,1)S(1)} %collective-permute-done.4), channel_id=1, source_target_pairs={{0,8},{2,10},{4,12},{6,14},{8,16},{10,18},{12,20},{14,22},{16,24},... | collective-permute-start | bytes 1572872 | tf_op jit(solution)/shard_map/ppermute | solution.py:318
  55.3 14.9 %collective-permute-start.3 = (bf16[512,512]{1,0:T(8,128)(2,1)S(1)}, bf16[512,512]{1,0:T(8,128)(2,1)S(1)}, u32[]{:S(2)}, u32[]{:S(2)}) collective-permute-start(bf16[512,512]{1,0:T(8,128)(2,1)S(1)} %collective-permute-done.2), channel_id=1, source_target_pairs={{0,2},{2,0},{4,6},{6,4},{8,10},{10,8},{12,14},{14,12},{16,18},{18,... | collective-permute-start | bytes 1572872 | tf_op jit(solution)/shard_map/ppermute | solution.py:318
  58.7 13.2 %collective-permute-start.5 = (bf16[512,512]{1,0:T(8,128)(2,1)S(1)}, bf16[512,512]{1,0:T(8,128)(2,1)S(1)}, u32[]{:S(2)}, u32[]{:S(2)}) collective-permute-start(bf16[512,512]{1,0:T(8,128)(2,1)S(1)} %collective-permute-done.4), channel_id=1, source_target_pairs={{0,2},{2,0},{4,6},{6,4},{8,10},{10,8},{12,14},{14,12},{16,18},{18,... | collective-permute-start | bytes 1572872 | tf_op jit(solution)/shard_map/ppermute | solution.py:318
  69.4 4.2 collective-permute-start.7
  73.6 40.4 %copy-start.3 = (bf16[256,512]{1,0:T(8,128)(2,1)S(1)}, bf16[256,512]{1,0:T(8,128)(2,1)}, u32[]{:S(2)}) copy-start(bf16[256,512]{1,0:T(8,128)(2,1)} %param.28) | copy-start | bytes 786436
  111.8 12.8 %collective-permute-start.8 = (bf16[256,256]{1,0:T(8,128)(2,1)S(1)}, bf16[256,256]{1,0:T(8,128)(2,1)S(1)}, u32[]{:S(2)}, u32[]{:S(2)}) collective-permute-start(bf16[256,256]{1,0:T(8,128)(2,1)S(1)} %get-tuple-element.81), channel_id=1, source_target_pairs={{0,4},{2,6},{4,0},{6,2},{8,12},{10,14},{12,8},{14,10},{16,20},{18,... | collective-permute-start | bytes 393224 | tf_op jit(solution)/shard_map/ppermute | solution.py:318
  113.3 11.4 %collective-permute-start.10 = (bf16[256,256]{1,0:T(8,128)(2,1)S(1)}, bf16[256,256]{1,0:T(8,128)(2,1)S(1)}, u32[]{:S(2)}, u32[]{:S(2)}) collective-permute-start(bf16[256,256]{1,0:T(8,128)(2,1)S(1)} %get-tuple-element.79), channel_id=1, source_target_pairs={{0,6},{2,4},{4,2},{6,0},{8,14},{10,12},{12,10},{14,8},{16,22},{18,... | collective-permute-start | bytes 393224 | tf_op jit(solution)/shard_map/ppermute | solution.py:318
  113.8 11.0 %collective-permute-start.9 = (bf16[256,256]{1,0:T(8,128)(2,1)S(1)}, bf16[256,256]{1,0:T(8,128)(2,1)S(1)}, u32[]{:S(2)}, u32[]{:S(2)}) collective-permute-start(bf16[256,256]{1,0:T(8,128)(2,1)S(1)} %get-tuple-element.80), channel_id=1, source_target_pairs={{0,2},{2,0},{4,6},{6,4},{8,10},{10,8},{12,14},{14,12},{16,18},{18,... | collective-permute-start | bytes 393224 | tf_op jit(solution)/shard_map/ppermute | solution.py:318
  142.4 139.5 %reduce-scatter.11.cloned.1.call-start = ((), (), s32[]{:S(2)}) async-start(), calls=%async_computation.10 | async-start | bytes 786432 | tf_op jit(solution)/shard_map/reduce_scatter | solution.py:395
  144.1 5.6 %collective-permute-start.11 = (bf16[256,256]{1,0:T(8,128)(2,1)S(1)}, bf16[256,256]{1,0:T(8,128)(2,1)S(1)}, u32[]{:S(2)}, u32[]{:S(2)}) collective-permute-start(bf16[256,256]{1,0:T(8,128)(2,1)S(1)} %get-tuple-element.77), channel_id=1, source_target_pairs={{0,4},{2,6},{4,0},{6,2},{8,12},{10,14},{12,8},{14,10},{16,20},{18,... | collective-permute-start | bytes 393224 | tf_op jit(solution)/shard_map/ppermute | solution.py:318
  145.6 4.1 collective-permute-start.12
  145.6 5.8 %collective-permute-start.13 = (bf16[256,256]{1,0:T(8,128)(2,1)S(1)}, bf16[256,256]{1,0:T(8,128)(2,1)S(1)}, u32[]{:S(2)}, u32[]{:S(2)}) collective-permute-start(bf16[256,256]{1,0:T(8,128)(2,1)S(1)} %get-tuple-element.75), channel_id=1, source_target_pairs={{0,6},{2,4},{4,2},{6,0},{8,14},{10,12},{12,10},{14,8},{16,22},{18,... | collective-permute-start | bytes 393224 | tf_op jit(solution)/shard_map/ppermute | solution.py:318
  206.4 75.4 %reduce-scatter.7.cloned.1.call-start = ((), (), s32[]{:S(2)}) async-start(), calls=%async_computation.8 | async-start | bytes 786432 | tf_op jit(solution)/shard_map/reduce_scatter | solution.py:395
  207.0 74.8 %reduce-scatter.9.cloned.1.call-start = ((), (), s32[]{:S(2)}) async-start(), calls=%async_computation.9 | async-start | bytes 786432 | tf_op jit(solution)/shard_map/reduce_scatter | solution.py:395
  207.6 82.3 %reduce-scatter.15.cloned.1.call-start = ((), (), s32[]{:S(2)}) async-start(), calls=%async_computation.12 | async-start | bytes 3145728 | tf_op jit(solution)/shard_map/reduce_scatter | solution.py:395
  215.1 7.1 %copy-start.8 = (f32[16,512]{1,0:T(8,128)S(1)}, f32[16,512]{1,0:T(8,128)}, u32[]{:S(2)}) copy-start(f32[16,512]{1,0:T(8,128)} %get-tuple-element.54) | copy-start | bytes 98308
  215.1 109.5 %reduce-scatter.17.cloned.1.call-start = ((), (), s32[]{:S(2)}) async-start(), calls=%async_computation.13 | async-start | bytes 3145728 | tf_op jit(solution)/shard_map/reduce_scatter | solution.py:395
  215.8 220.8 %all-reduce.4.cloned.1.call-start = ((), (), s32[]{:S(2)}) async-start(), calls=%async_computation.14 | async-start | bytes 6291456 | tf_op jit(solution)/shard_map/psum | solution.py:396
  218.7 2.3 collective-permute-start.14
  219.4 3.3 collective-permute-start.16
  222.1 16.1 %collective-permute-start.15 = (bf16[512,512]{1,0:T(8,128)(2,1)S(1)}, bf16[512,512]{1,0:T(8,128)(2,1)S(1)}, u32[]{:S(2)}, u32[]{:S(2)}) collective-permute-start(bf16[512,512]{1,0:T(8,128)(2,1)S(1)} %fusion.7), channel_id=1, source_target_pairs={{0,8},{2,10},{4,12},{6,14},{8,16},{10,18},{12,20},{14,22},{16,24},... | collective-permute-start | bytes 1572872 | tf_op jit(solution)/shard_map/ppermute | solution.py:318
  222.2 102.5 %collective-permute-start.18 = (bf16[512,512]{1,0:T(8,128)(2,1)}, bf16[512,512]{1,0:T(8,128)(2,1)S(1)}, u32[]{:S(2)}, u32[]{:S(2)}) collective-permute-start(bf16[512,512]{1,0:T(8,128)(2,1)} %get-tuple-element.69), channel_id=1, source_target_pairs={{0,2},{2,0},{4,6},{6,4},{8,10},{10,8},{12,14},{14,12},{16,18},{18,... | collective-permute-start | bytes 1572872 | tf_op jit(solution)/shard_map/ppermute | solution.py:318
  239.4 85.3 %collective-permute-start.17 = (bf16[512,512]{1,0:T(8,128)(2,1)S(1)}, bf16[512,512]{1,0:T(8,128)(2,1)S(1)}, u32[]{:S(2)}, u32[]{:S(2)}) collective-permute-start(bf16[512,512]{1,0:T(8,128)(2,1)S(1)} %fusion.6), channel_id=1, source_target_pairs={{0,8},{2,10},{4,12},{6,14},{8,16},{10,18},{12,20},{14,22},{16,24},... | collective-permute-start | bytes 1572872 | tf_op jit(solution)/shard_map/ppermute | solution.py:318
  240.3 89.0 %collective-permute-start.20 = (bf16[512,512]{1,0:T(8,128)(2,1)S(1)}, bf16[512,512]{1,0:T(8,128)(2,1)S(1)}, u32[]{:S(2)}, u32[]{:S(2)}) collective-permute-start(bf16[512,512]{1,0:T(8,128)(2,1)S(1)} %get-tuple-element.68), channel_id=1, source_target_pairs={{0,2},{2,0},{4,6},{6,4},{8,10},{10,8},{12,14},{14,12},{16,18},{18,... | collective-permute-start | bytes 1572872 | tf_op jit(solution)/shard_map/ppermute | solution.py:318
  324.7 31.7 %copy-start.2 = (f32[512,512]{1,0:T(8,128)S(1)}, f32[512,512]{1,0:T(8,128)}, u32[]{:S(2)}) copy-start(f32[512,512]{1,0:T(8,128)} %get-tuple-element.45) | copy-start | bytes 3145732
  326.0 19.8 %collective-permute-start.19 = (bf16[512,512]{1,0:T(8,128)(2,1)S(1)}, bf16[512,512]{1,0:T(8,128)(2,1)S(1)}, u32[]{:S(2)}, u32[]{:S(2)}) collective-permute-start(bf16[512,512]{1,0:T(8,128)(2,1)S(1)} %fusion.4), channel_id=1, source_target_pairs={{0,8},{2,10},{4,12},{6,14},{8,16},{10,18},{12,20},{14,22},{16,24},... | collective-permute-start | bytes 1572872 | tf_op jit(solution)/shard_map/ppermute | solution.py:318
  347.1 9.1 %collective-permute-start.21 = (bf16[256,512]{1,0:T(8,128)(2,1)S(1)}, bf16[256,512]{1,0:T(8,128)(2,1)S(1)}, u32[]{:S(2)}, u32[]{:S(2)}) collective-permute-start(bf16[256,512]{1,0:T(8,128)(2,1)S(1)} %slice.239), channel_id=1, source_target_pairs={{0,4},{2,6},{4,0},{6,2},{8,12},{10,14},{12,8},{14,10},{16,20},{18,... | collective-permute-start | bytes 786440 | tf_op jit(solution)/shard_map/ppermute | solution.py:318
  436.6 5.7 %copy-start.7 = (bf16[256,512]{1,0:T(8,128)(2,1)S(1)}, bf16[256,512]{1,0:T(8,128)(2,1)}, u32[]{:S(2)}) copy-start(bf16[256,512]{1,0:T(8,128)(2,1)} %get-tuple-element.57) | copy-start | bytes 786436
  436.6 6.6 %copy-start.6 = (bf16[256,512]{1,0:T(8,128)(2,1)S(1)}, bf16[256,512]{1,0:T(8,128)(2,1)}, u32[]{:S(2)}) copy-start(bf16[256,512]{1,0:T(8,128)(2,1)} %get-tuple-element.58) | copy-start | bytes 786436
  436.6 7.5 %copy-start.5 = (bf16[256,512]{1,0:T(8,128)(2,1)S(1)}, bf16[256,512]{1,0:T(8,128)(2,1)}, u32[]{:S(2)}) copy-start(bf16[256,512]{1,0:T(8,128)(2,1)} %get-tuple-element.59) | copy-start | bytes 786436
  436.6 9.2 %copy-start.1 = (bf16[256,512]{1,0:T(8,128)(2,1)S(1)}, bf16[256,512]{1,0:T(8,128)(2,1)}, u32[]{:S(2)}) copy-start(bf16[256,512]{1,0:T(8,128)(2,1)} %param.23) | copy-start | bytes 786436
  436.6 8.3 %copy-start.4 = (bf16[256,512]{1,0:T(8,128)(2,1)S(1)}, bf16[256,512]{1,0:T(8,128)(2,1)}, u32[]{:S(2)}) copy-start(bf16[256,512]{1,0:T(8,128)(2,1)} %get-tuple-element.60) | copy-start | bytes 786436
Sparse Core Ops, SparseCore 0:
  9.6 36.7 all-gather.4
  47.9 33.7 all-gather.6
  142.5 12.6 reduce-scatter.12
  206.6 12.9 reduce-scatter.10
  222.3 14.5 reduce-scatter.6
  239.6 14.7 reduce-scatter.8
  257.2 32.6 reduce-scatter.14
  292.8 31.8 reduce-scatter.16
  328.9 107.6 all-reduce.3

commit v2 on v1

--- a/solution.py
+++ b/solution.py
@@ -107,7 +107,7 @@
         name="attn_fwd")(blk, x, wq, wkv, bq, bkv)
 
 def bwd_kernel(nb, blk_ref, x_ref, k_ref, v_ref, qt_ref, q_ref, lse_ref, do_ref, of_ref, wq_ref, wkv_ref,
-               dx_ref, dw_ref, db_ref, dxq_s, dqa_s, kt_s, qs_s, qn_s, dot_s, don_s, dl_s, dk_s, dv_s, dq_s, d_s):
+               dx_ref, gq_ref, db_ref, dw_ref, dxq_s, dqa_s, kt_s, qs_s, qn_s, dot_s, don_s, dl_s, dk_s, dv_s, dq_s, d_s):
     qs_s[...] = jnp.zeros_like(qs_s)
     qn_s[...] = jnp.zeros_like(qn_s)
     dot_s[...] = jnp.zeros_like(dot_s)
@@ -200,16 +200,19 @@
         return 0
     lax.fori_loop(0, 8, fin_a, 0)
     lax.fori_loop(8, nb, fin_b, 0)
+    for k in range(2):
+        for m in range(3):
+            gq_ref[k, m * 256:m * 256 + 256, :] = dw_ref[k * 256:k * 256 + 256, m * 256:m * 256 + 256].astype(bf16)
 
 def attn_bwd(blk, x, k, v, qt, q, lse, do, of, wq, wkv):
     nb = blk.shape[0]
     V = pl.BlockSpec(memory_space=pltpu.VMEM)
     return pl.pallas_call(
         functools.partial(bwd_kernel, nb),
-        out_shape=(jax.ShapeDtypeStruct((nb * 128, 512), bf16), jax.ShapeDtypeStruct((512, 768), f32),
+        out_shape=(jax.ShapeDtypeStruct((nb * 128, 512), bf16), jax.ShapeDtypeStruct((2, 768, 256), bf16),
                    jax.ShapeDtypeStruct((8, 256), f32)),
         in_specs=[pl.BlockSpec(memory_space=pltpu.SMEM)] + [V] * 10, out_specs=(V,) * 3,
-        scratch_shapes=[pltpu.VMEM((1024, 512), f32), pltpu.VMEM((1024, 256), bf16), pltpu.VMEM((256, nb * 128), bf16), pltpu.VMEM((2, 256, 512), bf16), pltpu.VMEM((2, 512, 256), bf16),
+        scratch_shapes=[pltpu.VMEM((512, 768), f32), pltpu.VMEM((1024, 512), f32), pltpu.VMEM((1024, 256), bf16), pltpu.VMEM((256, nb * 128), bf16), pltpu.VMEM((2, 256, 512), bf16), pltpu.VMEM((2, 512, 256), bf16),
                         pltpu.VMEM((2, 256, 512), bf16), pltpu.VMEM((2, 512, 256), bf16), pltpu.VMEM((2, 1, 512), f32),
                         pltpu.VMEM((nb * 128, 256), f32), pltpu.VMEM((nb * 128, 256), f32), pltpu.VMEM((2, 128, 512), f32),
                         pltpu.VMEM((256, 512), jnp.int32)],
@@ -303,6 +306,324 @@
         name="dense")(x, cot, att, wo, wu, wd, vecs, bup)
 
 
+MESH = pl.DeviceIdType.MESH
+
+
+def places(nz):
+    me, wi = lax.axis_index("ctx"), lax.axis_index("wt")
+    z, y, c = me // 4, lax.rem(me // 2, 2), lax.rem(me, 2)
+    low = lax.rem(me, 4)
+    at = lambda zz, ll: (zz * 4 + ll, wi)
+    to = dict(up=at(lax.rem(z + 1, nz), low), down=at(lax.rem(z + nz - 1, nz), low), core=at(z, low + 1 - 2 * c), y=at(z, low + 2 - 4 * y),
+              x=(me, 1 - wi))
+    return me, wi, z, y, c, low, to
+
+
+def meet(targets):
+    bar = pltpu.get_barrier_semaphore()
+    for t in targets:
+        pl.semaphore_signal(bar, inc=1, device_id=t, device_id_type=MESH)
+    pl.semaphore_wait(bar, len(targets))
+
+
+class Wires:
+    def __init__(self, send, recv):
+        self.send, self.recv, self.n, self.live = send, recv, 0, []
+
+    def make(self, src, dst, to):
+        cp = pltpu.make_async_remote_copy(src, dst, self.send.at[self.n], self.recv.at[self.n], device_id=to, device_id_type=MESH)
+        self.n += 1
+        return cp
+
+    def go(self, src, dst, to):
+        cp = self.make(src, dst, to)
+        cp.start()
+        self.live.append(cp)
+        return cp
+
+    def drain(self):
+        for cp in self.live:
+            cp.wait_send()
+
+
+def rows_of(start, size, mult=16):
+    return pl.ds(pl.multiple_of(start, mult), size)
+
+
+def gather_kernel(nz, with_w, *refs):
+    if with_w:
+        (x_ref, wq_ref, wk_ref, wv_ref, wo_ref, wu_ref, wd_ref, sm_ref,
+         xall, wqkv, wo, wu, wd, sm, send, recv, lsem) = refs
+    else:
+        x_ref, xall, send, recv, lsem = refs
+    me, wi, z, y, c, low, to = places(nz)
+    rows = x_ref.shape[1]
+    local = []
+
+    def copy(src, dst):
+        cp = pltpu.make_async_copy(src, dst, lsem.at[len(local)])
+        cp.start()
+        local.append(cp)
+
+    copy(x_ref.at[y], xall.at[0, 0])
+    if with_w:
+        R, half = wq_ref.shape[0], wq_ref.shape[1] // 2
+        for i, w in enumerate((wq_ref, wk_ref, wv_ref)):
+            copy(w.at[:, rows_of(c * half, half, 128)], wqkv.at[rows_of(wi * R, R), pl.ds(i * half, half)])
+        for w, full in ((wo_ref, wo), (wu_ref, wu), (wd_ref, wd)):
+            n = w.shape[0]
+            copy(w, full.at[rows_of(wi * n, n)])
+        copy(sm_ref, sm.at[wi])
+    near = [to["up"], to["down"], to["core"], to["y"]] + ([to["x"]] if with_w else [])
+    meet(near)
+    wires = Wires(send, recv)
+    yx = wires.go(x_ref.at[1 - y], xall.at[0, 1], to["y"])
+    ring = {(1, 0): wires.go(x_ref.at[y], xall.at[1, 0], to["up"])}
+    core = {(0, 0): wires.go(x_ref.at[y], xall.at[0, 2], to["core"])}
+    if with_w:
+        xs = []
+        for i, w in enumerate((wq_ref, wk_ref, wv_ref)):
+            xs.append(wires.go(w.at[:, rows_of(c * half, half, 128)], wqkv.at[rows_of(wi * R, R), pl.ds(i * half, half)], to["x"]))
+        xs.append(wires.go(sm_ref, sm.at[wi], to["x"]))
+        big = []
+        for w, full in ((wo_ref, wo), (wu_ref, wu), (wd_ref, wd)):
+            n = w.shape[0]
+            h = n // 2
+            cp = wires.go(w.at[rows_of(c * h, h)], full.at[rows_of(wi * n + c * h, h)], to["x"])
+            big.append((cp, full, rows_of((1 - wi) * n + c * h, h)))
+    yx.wait_recv()
+    ring[1, 1] = wires.go(xall.at[0, 1], xall.at[1, 1], to["up"])
+    core[0, 1] = wires.go(xall.at[0, 1], xall.at[0, 3], to["core"])
+    shared = []
+    for r in range(1, nz):
+        for s in range(2):
+            ring[r, s].wait_recv()
+            if r < nz - 1:
+                ring[r + 1, s] = wires.go(xall.at[r, s], xall.at[r + 1, s], to["up"])
+            core[r, s] = wires.go(xall.at[r, s], xall.at[r, 2 + s], to["core"])
+        if with_w and r - 1 < len(big):
+            cp, full, where = big[r - 1]
+            cp.wait_recv()
+            shared.append(wires.go(full.at[where], full.at[where], to["core"]))
+    if with_w:
+        for cp, full, where in big[nz - 1:]:
+            cp.wait_recv()
+            shared.append(wires.go(full.at[where], full.at[where], to["core"]))
+        for cp in xs + shared:
+            cp.wait_recv()
+    for cp in core.values():
+        cp.wait_recv()
+    wires.drain()
+    for cp in local:
+        cp.wait()
+
+
+def gather_all(nz, x, weights=None, small=None):
+    A = pl.BlockSpec(memory_space=pl.ANY)
+    sds = jax.ShapeDtypeStruct
+    rows, dim = x.shape[1:]
+    outs = [sds((nz, 4, rows, dim), bf16)]
+    ins = [x]
+    ncopy = 1 + 2 * (nz - 1) + 2 * nz
+    if weights is not None:
+        wq, wk, wv, wo, wu, wd = weights
+        ins += list(weights) + [small]
+        outs += [sds((dim, 3 * dim // 2), bf16)] + [sds((2 * w.shape[0], w.shape[1]), bf16) for w in (wo, wu, wd)] + [sds((2,) + small.shape, bf16)]
+        ncopy += 10
+    return pl.pallas_call(
+        functools.partial(gather_kernel, nz, weights is not None),
+        out_shape=tuple(outs), in_specs=[A] * len(ins), out_specs=(A,) * len(outs),
+        scratch_shapes=[pltpu.SemaphoreType.DMA((ncopy,)), pltpu.SemaphoreType.DMA((ncopy,)), pltpu.SemaphoreType.DMA((8,))],
+        compiler_params=pltpu.CompilerParams(collective_id=1, has_side_effects=True, vmem_limit_bytes=16 << 20),
+        name="gather_all")(*ins)
+
+
+def add_into(dst, parts, rows, step=64):
+    def body(i, _):
+        r = rows_of(i * step, step)
+        total = parts[0](r)[...].astype(f32)
+        for p in parts[1:]:
+            total = total + p(r)[...].astype(f32)
+        d = dst(r)
+        d[...] = total.astype(bf16)
+        return 0
+    lax.fori_loop(0, rows // step, body, 0)
+
+
+def offset(ref, lead, start):
+    def view(r):
+        at = pl.ds(pl.multiple_of(start + r.start, 16), r.size)
+        return ref.at[lead + (at,)]
+    return view
+
+
+STREAMS = ((768, 512), (768, 512), (768, 512), (1536, 256))
+
+
+def reduce_kernel(nz, dx_ref, gw_ref, gq_ref, gv_ref, dxo, go, gqo, gvo,
+                  dx_core, dx_acc, dx_in, cr, cs, xr, xs_, yr, ys_, zr, cq, xrq, xsq, yrq, ysq, zrq, gvs, gvr, send, recv):
+    me, wi, z, y, c, low, to = places(nz)
+    zto = [(lax.rem(z + d, nz) * 4 + low, wi) for d in range(1, nz)]
+    meet([to["core"], to["y"], to["x"]] + zto)
+    w = Wires(send, recv)
+    hrow = 256
+    got = {}
+    for s in range(3):
+        got["c", s] = w.go(gw_ref.at[:, rows_of(s * 768 + (1 - c) * 384, 384)], cr.at[s], to["core"])
+        r = s + 1
+        got["d", r] = w.go(dx_ref.at[r, pl.ds(512, 512)], dx_core.at[r], to["core"])
+    got["d", 0] = w.go(dx_ref.at[0, pl.ds(512, 512)], dx_core.at[0], to["core"])
+
+    width = [384, 384, 384, 768]
+    n_y = [v // 2 for v in width]
+    n_z = [v // (2 * nz) for v in width]
+    X_in = [xr.at[s] for s in range(3)] + [xrq]
+    X_sum = [xs_.at[s] for s in range(3)] + [xsq]
+    Y_in = [yr.at[s] for s in range(3)] + [yrq]
+    Y_sum = [ys_.at[s] for s in range(3)] + [ysq]
+    Z_in = [zr.at[s] for s in range(3)] + [zrq]
+    out = [go.at[s] for s in range(3)] + [gqo]
+
+    def x_send(s):
+        if s < 3:
+            got["c", s].wait_recv()
+            for k in range(2):
+                add_into(offset(cs, (s, k), 0), [offset(gw_ref, (k,), s * 768 + c * 384), offset(cr, (s, k), 0)], 384)
+            got["x", s] = w.go(cs.at[s, 1 - wi], X_in[s], to["x"])
+        else:
+            got["x", s] = w.go(gq_ref.at[1 - wi], X_in[s], to["x"])
+
+    def y_send(s):
+        got["x", s].wait_recv()
+        mine = offset(cs, (s, wi), 0) if s < 3 else offset(gq_ref, (wi,), 0)
+        add_into(offset(X_sum[s], (), 0), [mine, offset(X_in[s], (), 0)], width[s])
+        got["y", s] = w.go(X_sum[s].at[rows_of((1 - y) * n_y[s], n_y[s])], Y_in[s], to["y"])
+
+    def z_send(s):
+        got["y", s].wait_recv()
+        add_into(offset(Y_sum[s], (), 0), [offset(X_sum[s], (), y * n_y[s]), offset(Y_in[s], (), 0)], n_y[s])
+        for d in range(1, nz):
+            zd = lax.rem(z + d, nz)
+            got["z", s, d] = w.go(Y_sum[s].at[rows_of(zd * n_z[s], n_z[s])], Z_in[s].at[d - 1], zto[d - 1])
+
+    def z_share(s):
+        for d in range(1, nz):
+            got["z", s, d].wait_recv()
+        base = c * width[s] + y * n_y[s] + z * n_z[s]
+        add_into(offset(out[s], (), base), [offset(Y_sum[s], (), z * n_z[s])] + [offset(Z_in[s], (d,), 0) for d in range(nz - 1)], n_z[s], 48)
+        at = rows_of(base, n_z[s])
+        for d in range(1, nz):
+            got["zs", s, d] = w.go(out[s].at[at], out[s].at[at], zto[d - 1])
+
+    def y_share(s):
+        for d in range(1, nz):
+            got["zs", s, d].wait_recv()
+        at = rows_of(c * width[s] + y * n_y[s], n_y[s])
+        got["ys", s] = w.go(out[s].at[at], out[s].at[at], to["y"])
+
+    def c_share(s):
+        got["ys", s].wait_recv()
+        at = rows_of(c * width[s], width[s])
+        got["cs", s] = w.go(out[s].at[at], out[s].at[at], to["core"])
+
+    def fold(r):
+        got["d", r].wait_recv()
+        add_into(offset(dx_acc, (r,), 0), [offset(dx_ref, (r,), 0), offset(dx_core, (r,), 0)], 512)
+
+    def hop(r, h):
+        if r != 1:
+            got["r", r, h].wait_recv()
+            if r:
+                add_into(offset(dx_acc, (r,), h * hrow), [offset(dx_acc, (r,), h * hrow), offset(dx_in, (r,), h * hrow)], hrow)
+            else:
+                dst = offset(dxo, (0,), 0) if h == 0 else offset(dx_acc, (0,), hrow)
+                add_into(dst, [offset(dx_acc, (0,), h * hrow), offset(dx_in, (0,), h * hrow)], hrow)
+        at = pl.ds(h * hrow, hrow)
+        if r:
+            n = (r + 1) % nz
+            got["r", n, h] = w.go(dx_acc.at[r, at], dx_in.at[n, at], to["up"])
+        elif h:
+            got["dy"] = w.go(dx_acc.at[0, at], dxo.at[1], to["y"])
+
+    vec_to = [to["core"], to["y"], to["x"]] + [(zz * 4 + low, wi) for zz in (z + 1 - 2 * lax.rem(z, 2), z + 2 - 4 * (z // 2))]
+
+    def vec_send(k):
+        if k == 0:
+            gvs[0] = gv_ref[...]
+        else:
+            got["v", k - 1].wait_recv()
+            gvs[k] = gvs[k - 1] + gvr[k - 1]
+        if k < 5:
+            got["v", k] = w.go(gvs.at[k], gvr.at[k], vec_to[k])
+        else:
+            gvo[...] = gvs[5]
+
+    x_send(3)
+    vec_send(0)
+    fold(1)
+    hop(1, 1)
+    hop(1, 0)
+    x_send(0)
+    vec_send(1)
+    x_send(1)
+    fold(2)
+    hop(2, 1)
+    x_send(2)
+    vec_send(2)
+    fold(3)
+    y_send(3)
+    hop(2, 0)
+    vec_send(3)
+    fold(0)
+    z_send(3)
+    hop(3, 1)
+    y_send(0)
+    z_share(3)
+    vec_send(4)
+    hop(3, 0)
+    z_send(0)
+    vec_send(5)
+    y_share(3)
+    y_send(1)
+    hop(0, 1)
+    z_share(0)
+    c_share(3)
+    z_send(1)
+    y_send(2)
+    hop(0, 0)
+    y_share(0)
+    z_share(1)
+    z_send(2)
+    c_share(0)
+    y_share(1)
+    z_share(2)
+    c_share(1)
+    y_share(2)
+    c_share(2)
+    for s in range(4):
+        got["cs", s].wait_recv()
+    got["dy"].wait_recv()
+    w.drain()
+
+
+def reduce_all(nz, dx, gw, gq, gv):
+    V = pl.BlockSpec(memory_space=pltpu.VMEM)
+    sds = jax.ShapeDtypeStruct
+    M = lambda *s: pltpu.VMEM(s, bf16)
+    ncopy = 100
+    return pl.pallas_call(
+        functools.partial(reduce_kernel, nz),
+        out_shape=(sds((2, 256, 512), bf16), sds((3, 768, 512), bf16), sds((1536, 256), bf16), sds(gv.shape, f32)),
+        in_specs=[V] * 4, out_specs=(V,) * 4,
+        scratch_shapes=[M(nz, 512, 512), M(nz, 512, 512), M(nz, 512, 512), M(3, 2, 384, 512), M(3, 2, 384, 512),
+                        M(3, 384, 512), M(3, 384, 512), M(3, 192, 512), M(3, 192, 512), M(3, nz - 1, 48, 512),
+                        M(8, 128), M(768, 256), M(768, 256), M(384, 256), M(384, 256), M(nz - 1, 96, 256),
+                        pltpu.VMEM((6,) + gv.shape, f32), pltpu.VMEM((5,) + gv.shape, f32),
+                        pltpu.SemaphoreType.DMA((ncopy,)), pltpu.SemaphoreType.DMA((ncopy,))],
+        compiler_params=pltpu.CompilerParams(collective_id=2, has_side_effects=True, vmem_limit_bytes=60 << 20),
+        name="reduce_all")(dx, gw, gq, gv)
+
+
 def body(block_in, block_order, w_query, b_query, w_key, w_value, b_value, w_out, b_out, gain_one, shift_one,
          w_up, b_up, w_down, b_down, gain_two, shift_two, cotangent, *, nc, nw):
     seqs, rows, dim = block_in.shape
@@ -319,35 +640,30 @@
     gather = lambda v: lax.all_gather(v, "wt", axis=0, tiled=True)
     pick = lambda v, i: lax.dynamic_index_in_dim(v, i, 0, keepdims=False)
 
-    cols = lambda w: lax.dynamic_slice_in_dim(w, cc * half, half, 1)
-    wqkv = gather(jnp.concatenate([cols(w_query), cols(w_key), cols(w_value)], axis=1))
+    ours = nw == 2 and nz == 4
+    small = jnp.concatenate([v.reshape(-1, dim // nw) for v in (b_query, b_value, b_out, gain_one, shift_one, b_down, gain_two, shift_two, b_up)], axis=0)
+    if ours:
+        small = jnp.pad(small, ((0, -small.shape[0] % 16), (0, 0)))
+        x_all, wqkv, wo, wu, wd, small = gather_all(nz, block_in, (w_query, w_key, w_value, w_out, w_up, w_down), small)
+    else:
+        cols = lambda w: lax.dynamic_slice_in_dim(w, cc * half, half, 1)
+        wqkv = gather(jnp.concatenate([cols(w_query), cols(w_key), cols(w_value)], axis=1))
+        small = lax.all_gather(small, "wt", axis=0)
+        wo, wu, wd = gather(w_out), gather(w_up), gather(w_down)
+        x_all = gather_all(nz, block_in)[0]
+    x_all = x_all.reshape(-1, dim)
     wq, wkv = wqkv[:, :half], wqkv[:, half:]
-    small = jnp.concatenate([v.reshape(-1, dim // nw) for v in (b_query, b_value, b_out, gain_one, shift_one, b_down, gain_two, shift_two, b_up)], axis=0)
-    small = lax.all_gather(small, "wt", axis=0)
-    ffr = b_up.shape[0] // (dim // nw)
     vecs = jnp.transpose(small[:, :8], (1, 0, 2)).reshape(8, dim).astype(f32)
-    bup = small[:, 8:].reshape(1, -1).astype(f32)
+    bup = small[:, 8:8 + b_up.shape[0] // (dim // nw)].reshape(1, -1).astype(f32)
     bq = lax.dynamic_slice_in_dim(vecs[0:1], cc * half, half, 1)
-    bv = lax.dynamic_slice_in_dim(vecs[1:2], cc * half, half, 1)
-    bkv = bv
+    bkv = lax.dynamic_slice_in_dim(vecs[1:2], cc * half, half, 1)
     dvec = vecs[2:8]
-
-    own = pick(block_in, yy)
-    got = perm(pick(block_in, 1 - yy), xor(2))
-    ring_x = jnp.concatenate([own, got], axis=0)
-    pieces = []
-    for r in range(nz):
-        pieces += [ring_x, perm(ring_x, xor(1))]
-        if r < nz - 1:
-            ring_x = perm(ring_x, ring)
-    x_all = jnp.concatenate(pieces, axis=0)
     r_ids = (zz - jnp.arange(nz, dtype=jnp.int32)) % nz
     quad = (me % 4) ^ jnp.array([0, 2, 1, 3], jnp.int32)
     order_row = pick(block_order, yy)
     slots = (r_ids[:, None, None] * 4 + quad[None, :, None]) * hb + jnp.arange(hb, dtype=jnp.int32)
     blk = order_row[slots.reshape(-1)]
 
-    wo, wu, wd = gather(w_out), gather(w_up), gather(w_down)
     o, lse, k, v, qt, q = attn_fwd(blk, x_all, wq, wkv, bq, bkv)
     o16 = o.astype(bf16)
     o_self = o16[:rows]
@@ -365,38 +681,45 @@
     fh = lambda v, c: lax.dynamic_slice_in_dim(v, c * half, half, 1)
     do_all = jnp.concatenate([fh(d_own, cc), perm(fh(d_oth, cc), xor(2)), perm(fh(d_own, 1 - cc), xor(1)), perm(fh(d_oth, 1 - cc), xor(3))], axis=0)
     dx, gq, gb = attn_bwd(blk, x_all, k, v, qt, q, lse, do_all, o, wq, wkv)
-    dx = dx.reshape(nz, 2, 2 * rows, dim)
-    part = lambda r: dx[r, 0].astype(f32) + perm(dx[r, 1], xor(1)).astype(f32)
-    acc = None
-    for r in list(range(1, nz)) + [0]:
-        acc = part(r) if acc is None else perm(acc.astype(bf16), ring).astype(f32) + part(r)
-    from_y = perm(acc[rows:].astype(bf16), xor(2)).astype(f32)
-    dkv_sum = by_seq(acc[:rows], from_y)
-    grad_in = (dsm + dkv_sum).astype(bf16).reshape(seqs, rows, dim)
-
-    gvec = jnp.zeros((18, dim), f32).at[:16].set(gv)
+    gvec = jnp.zeros((24, dim), f32).at[:16].set(gv)
     gvec = lax.dynamic_update_slice(gvec, gb[0:1], (16, cc * half))
     gvec = lax.dynamic_update_slice(gvec, gb[1:2], (17, cc * half))
-    gvec = lax.psum(gvec, ("ctx", "wt"))
     wi = lax.axis_index("wt")
+    ff, hr = w_up.shape[1], dim // 2
+    nu = ff // dim
+    if ours:
+        dxo, go, gqo, gvec = reduce_all(nz, dx.reshape(nz, 4 * rows, dim), gw, gq, gvec)
+        go = go.reshape(-1, dim)
+        t_out = go[:hr].astype(f32)
+        t_up = go[hr:hr + nu * hr].astype(f32).reshape(nu, hr, dim).transpose(1, 0, 2).reshape(hr, ff)
+        t_down = go[hr + nu * hr:].astype(f32)
+        gqo = gqo.reshape(2, 3, hr, half).transpose(1, 2, 0, 3).reshape(3, hr, dim)
+        t_qkv = [gqo[i].astype(f32) for i in range(3)]
+        dkv_sum = by_seq(dxo[0], dxo[1]).astype(f32)
+    else:
+        dx = dx.reshape(nz, 2, 2 * rows, dim)
+        part = lambda r: dx[r, 0].astype(f32) + perm(dx[r, 1], xor(1)).astype(f32)
+        acc = None
+        for r in list(range(1, nz)) + [0]:
+            acc = part(r) if acc is None else perm(acc.astype(bf16), ring).astype(f32) + part(r)
+        from_y = perm(acc[rows:].astype(bf16), xor(2)).astype(f32)
+        dkv_sum = by_seq(acc[:rows], from_y)
+        gvec = lax.psum(gvec, ("ctx", "wt"))
+        g_out = gw[:, :hr].reshape(dim, dim)
+        g_up = gw[:, hr:hr + nu * hr].reshape(2, nu, hr, dim).transpose(0, 2, 1, 3).reshape(dim, ff)
+        g_down = gw[:, hr + nu * hr:].reshape(ff, dim)
+        gq3 = gq.reshape(2, 3, hr, half).transpose(1, 0, 2, 3).reshape(3, dim, half)
+        g_qkv = lax.dynamic_update_slice(jnp.zeros((3, dim, dim), bf16), gq3, (0, 0, cc * half))
+        total = lambda g: lax.psum(lax.psum_scatter(g, "wt", scatter_dimension=0, tiled=True), "ctx").astype(f32)
+        t_out, t_up, t_down = total(g_out), total(g_up), total(g_down)
+        t_qkv = [total(g_qkv[i]) for i in range(3)]
+    grad_in = (dsm + dkv_sum).astype(bf16).reshape(seqs, rows, dim)
+
     def share(vv):
         n = vv.size // nw
         return lax.dynamic_slice_in_dim(vv.reshape(-1), wi * n, n, 0)
-    rr = w_query.shape[0]
-    ff = w_up.shape[1]
-    hr = dim // 2
-    g_out = gw[:, :hr].reshape(dim, dim)
-    g_up = gw[:, hr:hr + (ff // dim) * hr].reshape(2, ff // dim, hr, dim).transpose(0, 2, 1, 3).reshape(dim, ff)
-    g_down = gw[:, hr + (ff // dim) * hr:].reshape(ff, dim)
-    zq = jnp.zeros((3, dim, dim), bf16)
-    gq3 = gq.astype(bf16).reshape(dim, 3, half).transpose(1, 0, 2)
-    g_qkv = lax.dynamic_update_slice(zq, gq3, (0, 0, cc * half))
-    def total(g):
-        s = lax.psum_scatter(g, "wt", scatter_dimension=0, tiled=True)
-        return lax.psum(s, "ctx").astype(f32)
-    gqkv = [total(g_qkv[i]) for i in range(3)]
-    return (out.reshape(seqs, rows, dim), grad_in, gqkv[0], share(gvec[16]), gqkv[1], gqkv[2], share(gvec[17]), total(g_out), share(gvec[0]),
-            share(gvec[1]), share(gvec[2]), total(g_up), share(gvec[8:8 + ff // dim]), total(g_down), share(gvec[3]), share(gvec[4]), share(gvec[5]))
+    return (out.reshape(seqs, rows, dim), grad_in, t_qkv[0], share(gvec[16]), t_qkv[1], t_qkv[2], share(gvec[17]), t_out, share(gvec[0]),
+            share(gvec[1]), share(gvec[2]), t_up, share(gvec[8:8 + nu]), t_down, share(gvec[3]), share(gvec[4]), share(gvec[5]))
 
 
 def solution(mesh):

time: 453 us -> 319 us (0.70)
  waiting for transfers between devices: 190 us -> 9.67 us
  Pallas kernels: 101 us -> 256 us
  blocking collectives: 66.7 us -> 0 us
  between operations: 14.3 us -> 0.98 us
  starting transfers between devices: 15.8 us -> 4.41 us
  other arithmetic: 20.8 us -> 9.87 us
  local copies, waits for them, and re-layouts: 43.7 us -> 37.9 us
    pallas_call x0 -> x2, Pallas kernels: none -> 154 us  [the longest x1 110 us: reduce_all(): pl.pallas_call(functools.partial(reduce_kernel, nz), out_shape=(sds((2, 2...]
    psum x1 -> x0, waiting for transfers between devices: 79.2 us -> none  [total(): return lax.psum(s, 'ctx').astype(f32)]
    ppermute x22 -> x6, waiting for transfers between devices: 65 us -> 9.67 us  [body(): perm = lambda v, p: lax.ppermute(v, 'ctx', p)]
    reduce_scatter x6 -> x0, waiting for transfers between devices: 42.8 us -> none  [total(): s = lax.psum_scatter(g, 'wt', scatter_dimension=0, tiled=True)]
    psum x1 -> x0, blocking collectives: 39.9 us -> none  [body(): gvec = lax.psum(gvec, ('ctx', 'wt'))]
    all_gather x3 -> x0, blocking collectives: 26.7 us -> none  [the longest x2 22.2 us: body(): gather = lambda v: lax.all_gather(v, 'wt', axis=0, tiled=True)]
    ppermute x22 -> x6, starting transfers between devices: 15 us -> 4.41 us  [body(): perm = lambda v, p: lax.ppermute(v, 'ctx', p)]
    convert_element_type x12 -> x4, other arithmetic: 14.4 us -> 5.16 us  [the longest x1 3.22 us: body(): t_down = go[hr + nu * hr:].astype(f32)]
  transfers between devices with their start and end apart: 31 -> 6, of which waited for: 12 -> 4; matrix products, arithmetic and copies ran while one was open for 12% -> 1% of each run, Pallas kernels for 19% -> 0%
where the time goes in v2:
time: 319 us
  Pallas kernels  256 us (80%)
  local copies, waits for them, and re-layouts  37.9 us (12%)
  other arithmetic  9.87 us (3%)
  waiting for transfers between devices  9.67 us (3%)
  starting transfers between devices  4.41 us (1%)
    pallas_call x1, Pallas kernels, reduce_all(): pl.pallas_call(functools.partial(reduce_kernel, nz), out_shape=(sds((2, 2...  110 us
    pallas_call x1, Pallas kernels, attn_bwd(): pl.pallas_call(functools.partial(bwd_kernel, nb), out_shape=(jax.ShapeDty...  50.8 us
    pallas_call x1, Pallas kernels, gather_all(): pl.pallas_call(functools.partial(gather_kernel, nz, weights is not None),...  44.7 us
    pallas_call x1, Pallas kernels, attn_fwd(): pl.pallas_call(functools.partial(fwd_kernel, nb), out_shape=(jax.ShapeDty...  36 us
    unnamed x41, local copies, waits for them, and re-layouts  16 us
    pallas_call x1, Pallas kernels, dense(): pl.pallas_call(dense_kernel, out_shape=(jax.ShapeDtypeStruct((tok, dim),...  14.7 us
    ppermute x6, waiting for transfers between devices, body(): perm = lambda v, p: lax.ppermute(v, 'ctx', p)  9.67 us
  transfers between devices with their start and end apart: 6, of which 4 were waited for; matrix products, arithmetic and copies ran while one was open for 1% of the time, Pallas kernels for 0%

profile of v2, /device:TPU:0, one launch (start us, length us, event | category | flops | bytes accessed | tf_op | source)
XLA Modules:
  0.0 318.7 jit_solution(2307741213974248433)
XLA Ops:
  0.7 0.7 reshape.262
  1.4 0.7 reshape.254
  2.1 0.7 reshape.255
  2.7 0.7 reshape.256
  3.4 0.7 reshape.257
  4.0 0.7 reshape.258
  4.7 0.7 reshape.259
  5.4 0.7 reshape.260
  6.0 0.7 reshape.261
  6.7 1.0 copy-done.2
  7.8 1.2 copy-done.5
  9.0 1.2 copy-done.6
  10.2 0.9 copy-done.8
  11.2 0.9 copy-done.9
  12.1 0.9 copy-done.10
  13.1 0.9 copy-done.11
  14.0 44.7 %gather_all.1 = (bf16[4,4,256,512]{3,2,1,0:T(8,128)(2,1)S(1)}, bf16[512,768]{1,0:T(8,128)(2,1)S(1)}, bf16[512,512]{1,0:T(8,128)(2,1)S(1)}, bf16[512,2048]{1,0:T(...) custom-call(bf16[2,256,512]{2,1,0:T(8,128)(2,1)S(1)} %copy-done.2, ...), custom_call_target="tpu_custom_call" | custom-call | tf_op jit(solution)/shard_map/gather_all/pallas_call | solution.py:433
  58.7 2.0 copy-done.1
  60.7 1.3 copy-done.3
  62.1 1.4 copy-done.4
  63.5 0.8 copy-done.7
  64.3 0.8 slice.119.wkv_ref
  65.1 0.7 slice.118.wq_ref
  66.2 1.2 gather_fusion
  67.4 0.6 constant_dynamic-slice_fusion.8
  68.0 36.0 %attn_fwd.1 = (f32[1024,256]{1,0:T(8,128)}, f32[8,1,512]{2,1,0:T(1,128)}, bf16[4096,256]{1,0:T(8,128)(2,1)}, bf16[4096,256]{1,0:T(8,128)(2,1)}, bf16[8,256,128]{2,1,0:T(8,128)(2,1)}, /*index=5*/bf16[1024,256]{1,0:T(8,128)(2,1)}) custom-call(s32[32]{0:T(128)} %gather_fusion, bf16[4096,512]{1,0:T(8,128)(2,1)} %bitcast.58, bf16[512,256]{1,0:T(8,128)(2,1)} %slice.118.wq_ref, ...), custom_call_target="tpu_custom_call" | custom-call | tf_op jit(solution)/shard_map/attn_fwd/pallas_call | solution.py:98
  104.0 1.3 convert_element_type.50
  105.4 0.6 collective-permute-start
  106.1 1.5 collective-permute-start.2
  107.6 0.6 slice.159
  108.2 0.6 reshape.274.bup_ref
  108.8 3.0 collective-permute-done
  111.8 1.7 collective-permute-done.2
  113.7 0.9 maximum_select_fusion.att_ref
  114.6 14.7 %dense.1 = (bf16[512,512]{1,0:T(8,128)(2,1)}, f32[512,512]{1,0:T(8,128)}, bf16[512,512]{1,0:T(8,128)(2,1)}, bf16[2,2304,512]{2,1,0:T(8,128)(2,1)}, f32[16,512]{1,0:T(8,128)}) custom-call(bf16[512,512]{1,0:T(8,128)(2,1)} %bitcast.60, bf16[512,512]{1,0:T(8,128)(2,1)} %bitcast.70, bf16[512,512]{1,0:T(8,128)(2,1)} %maximum_select_fusion.att_ref, ...), custom_call_target="tpu_custom_call" | custom-call | tf_op jit(solution)/shard_map/dense/pallas_call | solution.py:297
  129.3 1.4 dynamic-slice_bitcast_fusion.3
  130.7 0.6 collective-permute-start.3
  131.3 1.6 collective-permute-start.5
  132.9 0.8 scatter.4
  133.6 3.4 %collective-permute-done.3 = bf16[256,256]{1,0:T(8,128)(2,1)S(1)} collective-permute-done((bf16[256,256]{1,0:T(8,128)(2,1)S(1)}, bf16[256,256]{1,0:T(8,128)(2,1)S(1)}, u32[]{:S(2)}, u32[]{:S(2)}) %collective-permute-start.3) | collective-permute-done | bytes 131104 | tf_op jit(solution)/shard_map/ppermute | solution.py:639
  137.0 1.5 collective-permute-done.5
  138.6 0.8 pad_maximum_fusion.do_ref
  139.4 50.8 %attn_bwd.1 = (bf16[4096,512]{1,0:T(8,128)(2,1)}, bf16[2,768,256]{2,1,0:T(8,128)(2,1)}, f32[8,256]{1,0:T(8,128)}) custom-call(s32[32]{0:T(128)} %gather_fusion, bf16[4096,512]{1,0:T(8,128)(2,1)} %bitcast.59, bf16[4096,256]{1,0:T(8,128)(2,1)} %get-tuple-element.62.k_ref, bf16[4096,256]{1,0:T(8,128)(2,1)} %get-tuple-element.63.v_ref, ...), custom_call_target="tpu_custom_call" | custom-call | tf_op jit(solution)/shard_map/attn_bwd/pallas_call | solution.py:210
  190.3 0.8 fusion.7
  191.5 0.6 copy-done.15
  192.1 109.7 %reduce_all.1 = (bf16[2,256,512]{2,1,0:T(8,128)(2,1)}, bf16[3,768,512]{2,1,0:T(8,128)(2,1)}, bf16[1536,256]{1,0:T(8,128)(2,1)}, f32[24,512]{1,0:T(8,128)}) custom-call(bf16[4,1024,512]{2,1,0:T(8,128)(2,1)} %bitcast.62, bf16[2,2304,512]{2,1,0:T(8,128)(2,1)} %get-tuple-element.69.gw_ref, bf16[2,768,256]{2,1,0:T(8,128)(2,1)} %get-tuple-element.70.gq_ref, ...), custom_call_target="tpu_custom_call" | custom-call | tf_op jit(solution)/shard_map/reduce_all/pallas_call | solution.py:614
  301.8 3.2 %slice_convert_fusion = (f32[1024,512]{1,0:T(8,128)}, bf16[1024,512]{1,0:T(8,128)(2,1)S(1)}) fusion(bf16[2304,512]{1,0:T(8,128)(2,1)} %bitcast.63), kind=kLoop, calls=%fused_computation.2 | loop fusion | flops 524288 | bytes 5242880 | tf_op jit(solution)/shard_map/convert_element_type | solution.py:695
  305.0 1.8 slice_convert_fusion.1
  307.1 1.5 copy.44
  308.8 0.4 copy.40
  309.2 0.8 copy.45
  310.5 0.8 copy.46
  311.3 0.4 copy.42
  311.7 0.8 copy.47
  312.6 0.6 constant_dynamic-slice_fusion.7
  313.1 0.6 constant_dynamic-slice_fusion.6
  313.7 0.6 constant_dynamic-slice_fusion.5
  314.3 0.6 constant_dynamic-slice_fusion.4
  314.8 0.6 constant_dynamic-slice_fusion.3
  315.4 0.6 constant_dynamic-slice_fusion.2
  316.0 0.6 constant_dynamic-slice_fusion.1
  316.5 0.6 constant_dynamic-slice_fusion
  317.1 0.6 dynamic_slice.97
  317.7 1.0 add_convert_fusion
  (52 shorter events, 2.1 us)
Async XLA Ops:
  0.7 65.5 %copy-start = (s32[2,32]{1,0:T(2,128)S(1)}, s32[2,32]{1,0:T(2,128)}, u32[]{:S(2)}) copy-start(s32[2,32]{1,0:T(2,128)} %param.22) | copy-start | bytes 772
  6.7 1.0 copy-start.2
  7.8 1.2 copy-start.5
  9.0 1.2 copy-start.6
  10.2 0.9 copy-start.8
  11.2 0.9 copy-start.9
  12.1 0.9 copy-start.10
  13.1 0.9 copy-start.11
  14.0 51.9 %copy-start.17 = (s32[4]{0:T(128)S(1)}, s32[4]{0:T(128)}, u32[]{:S(2)}) copy-start(s32[4]{0:T(128)} %constant.196.clone) | copy-start | bytes 52
  58.7 2.0 copy-start.1
  60.7 1.3 copy-start.3
  62.1 1.4 copy-start.4
  63.5 0.8 copy-start.7
  105.4 6.4 %collective-permute-start = (bf16[256,256]{1,0:T(8,128)(2,1)S(1)}, bf16[256,256]{1,0:T(8,128)(2,1)S(1)}, u32[]{:S(2)}, u32[]{:S(2)}) collective-permute-start(bf16[256,256]{1,0:T(8,128)(2,1)S(1)} %get-tuple-element.91), channel_id=1, source_target_pairs={{0,4},{2,6},{4,0},{6,2},{8,12},{10,14},{12,8},{14,10},{16,20},{18,... | collective-permute-start | bytes 393224 | tf_op jit(solution)/shard_map/ppermute | solution.py:639
  105.9 5.9 %collective-permute-start.1 = (bf16[256,256]{1,0:T(8,128)(2,1)S(1)}, bf16[256,256]{1,0:T(8,128)(2,1)S(1)}, u32[]{:S(2)}, u32[]{:S(2)}) collective-permute-start(bf16[256,256]{1,0:T(8,128)(2,1)S(1)} %get-tuple-element.90), channel_id=1, source_target_pairs={{0,2},{2,0},{4,6},{6,4},{8,10},{10,8},{12,14},{14,12},{16,18},{18,... | collective-permute-start | bytes 393224 | tf_op jit(solution)/shard_map/ppermute | solution.py:639
  106.1 7.5 %collective-permute-start.2 = (bf16[256,256]{1,0:T(8,128)(2,1)S(1)}, bf16[256,256]{1,0:T(8,128)(2,1)S(1)}, u32[]{:S(2)}, u32[]{:S(2)}) collective-permute-start(bf16[256,256]{1,0:T(8,128)(2,1)S(1)} %get-tuple-element.89), channel_id=1, source_target_pairs={{0,6},{2,4},{4,2},{6,0},{8,14},{10,12},{12,10},{14,8},{16,22},{18,... | collective-permute-start | bytes 393224 | tf_op jit(solution)/shard_map/ppermute | solution.py:639
  130.7 6.4 %collective-permute-start.3 = (bf16[256,256]{1,0:T(8,128)(2,1)S(1)}, bf16[256,256]{1,0:T(8,128)(2,1)S(1)}, u32[]{:S(2)}, u32[]{:S(2)}) collective-permute-start(bf16[256,256]{1,0:T(8,128)(2,1)S(1)} %get-tuple-element.87), channel_id=1, source_target_pairs={{0,4},{2,6},{4,0},{6,2},{8,12},{10,14},{12,8},{14,10},{16,20},{18,... | collective-permute-start | bytes 393224 | tf_op jit(solution)/shard_map/ppermute | solution.py:639
  131.2 5.8 %collective-permute-start.4 = (bf16[256,256]{1,0:T(8,128)(2,1)S(1)}, bf16[256,256]{1,0:T(8,128)(2,1)S(1)}, u32[]{:S(2)}, u32[]{:S(2)}) collective-permute-start(bf16[256,256]{1,0:T(8,128)(2,1)S(1)} %get-tuple-element.86), channel_id=1, source_target_pairs={{0,2},{2,0},{4,6},{6,4},{8,10},{10,8},{12,14},{14,12},{16,18},{18,... | collective-permute-start | bytes 393224 | tf_op jit(solution)/shard_map/ppermute | solution.py:639
  131.3 7.3 %collective-permute-start.5 = (bf16[256,256]{1,0:T(8,128)(2,1)S(1)}, bf16[256,256]{1,0:T(8,128)(2,1)S(1)}, u32[]{:S(2)}, u32[]{:S(2)}) collective-permute-start(bf16[256,256]{1,0:T(8,128)(2,1)S(1)} %get-tuple-element.85), channel_id=1, source_target_pairs={{0,6},{2,4},{4,2},{6,0},{8,14},{10,12},{12,10},{14,8},{16,22},{18,... | collective-permute-start | bytes 393224 | tf_op jit(solution)/shard_map/ppermute | solution.py:639
  191.5 0.6 copy-start.15
  301.8 5.0 %copy-start.16 = (f32[24,512]{1,0:T(8,128)S(1)}, f32[24,512]{1,0:T(8,128)}, u32[]{:S(2)}) copy-start(f32[24,512]{1,0:T(8,128)} %get-tuple-element.75) | copy-start | bytes 147460
  307.1 1.5 copy-start.13
  310.0 2.5 copy-start.14
  310.4 7.2 %copy-start.12 = (f32[512,512]{1,0:T(8,128)S(1)}, f32[512,512]{1,0:T(8,128)}, u32[]{:S(2)}) copy-start(f32[512,512]{1,0:T(8,128)} %get-tuple-element.61) | copy-start | bytes 3145732

commit v3 on v2

--- a/solution.py
+++ b/solution.py
@@ -11,222 +11,335 @@
 norm_eps = 1e-05
 
 BLOCK = 128
+HEADS_HERE = 4
 LOG2E = 1.4426950408889634
+FAR = -1e30
 bf16, f32 = jnp.bfloat16, jnp.float32
 NT = (((1,), (1,)), ((), ()))
 TN = (((0,), (0,)), ((), ()))
 
+
 def dot(a, b, dims=(((1,), (0,)), ((), ()))):
     return lax.dot_general(a, b, dims, preferred_element_type=f32)
 
-def fwd_kernel(nb, blk_ref, x_ref, wq_ref, wkv_ref, bq_ref, bkv_ref,
-               o_ref, lse_ref, k_ref, v_ref, qt_ref, q_ref, vt_s, qs_s, acc_s, m_s, l_s, d_s):
-    qs_s[...] = jnp.zeros_like(qs_s)
-    d_s[...] = lax.broadcasted_iota(jnp.int32, d_s.shape, 0) - (lax.broadcasted_iota(jnp.int32, d_s.shape, 1) & 127)
-    def proj(p, _):
-        x = x_ref[pl.ds(pl.multiple_of(p * 256, 256), 256), :]
+
+def turned(v):
+    return v.astype(f32).T.astype(bf16)
+
+
+def head_slices():
+    return [(slice(64 * h, 64 * h + 64), slice(128 * h, 128 * h + 128)) for h in range(HEADS_HERE)]
+
+
+class Pairs:
+    def __init__(self, nb, first):
+        self.nb, self.first = nb, first
+
+    def first_lo(self, n):
+        return self.first(n) < self.nb // 2
+
+    def lo(self, n):
+        b = self.first(n)
+        return jnp.where(b < self.nb // 2, b, self.nb - 1 - b)
+
+    def ordered(self, n, v):
+        a, b = v[:BLOCK], v[BLOCK:]
+        first = self.first_lo(n)
+        return jnp.where(first, a, b), jnp.where(first, b, a)
+
+
+def project_chunk(pairs, r, x_ref, wkv_ref, wkvt_ref, bkv_ref, bkvt_ref, K, V, KT, VT):
+    def piece(p, _):
+        x = jnp.concatenate(pairs.ordered(r * 4 + p, x_ref[r, p]), axis=0)
         kv = dot(x, wkv_ref[...])
-        k = kv[:, :256].astype(bf16)
-        v = (kv[:, 256:] + bkv_ref[...]).astype(bf16)
+        k, v = kv[:, :256].astype(bf16), (kv[:, 256:] + bkv_ref[...]).astype(bf16)
+        kvt = dot(wkvt_ref[...], x, NT)
+        kt, vt = kvt[:256].astype(bf16), (kvt[256:] + bkvt_ref[...]).astype(bf16)
+        at = pl.ds(pl.multiple_of(p * BLOCK, BLOCK), BLOCK)
         for u in range(2):
-            r = pl.ds(pl.multiple_of(blk_ref[2 * p + u] * BLOCK, BLOCK), BLOCK)
-            k_ref[r, :] = k[u * BLOCK:(u + 1) * BLOCK]
-            vb = v[u * BLOCK:(u + 1) * BLOCK]
-            v_ref[r, :] = vb
-            vt_s[:, r] = vb.astype(f32).T.astype(bf16)
+            rows = slice(u * BLOCK, (u + 1) * BLOCK)
+            K[r, u, at, :] = k[rows]
+            V[r, u, at, :] = v[rows]
+            KT[r, u, :, at] = kt[:, rows]
+            VT[r, u, :, at] = vt[:, rows]
         return 0
-    lax.fori_loop(0, nb // 2, proj, 0)
-    def projq(p, _):
-        x = x_ref[pl.ds(pl.multiple_of(p * 256, 256), 256), :]
+    lax.fori_loop(0, 4, piece, 0)
+
+
+def project_queries(pairs, x_ref, wq_ref, bq_ref, qn, qt, qs):
+    qs[...] = jnp.zeros_like(qs)
+
+    def piece(p, _):
+        x = jnp.concatenate(pairs.ordered(p, x_ref[0, p]), axis=0)
         q = (dot(x, wq_ref[...]) + bq_ref[...]) * (LOG2E / 8.0)
-        q_ref[pl.ds(pl.multiple_of(p * 256, 256), 256), :] = q.astype(bf16)
         for u in range(2):
-            qt = q[u * BLOCK:(u + 1) * BLOCK].T.astype(bf16)
-            qt_ref[2 * p + u] = qt
-            for h in range(4):
-                qs_s[2 * p + u, 64 * h:64 * h + 64, 128 * h:128 * h + 128] = qt[64 * h:64 * h + 64]
+            mine = q[u * BLOCK:(u + 1) * BLOCK]
+            qn[p, u] = mine.astype(bf16)
+            t = mine.T.astype(bf16)
+            qt[p, u] = t
+            for hs, cs in head_slices():
+                qs[p, u, hs, cs] = t[hs]
         return 0
-    lax.fori_loop(0, 4, projq, 0)
-
-    def pair(p, _):
-        b0 = blk_ref[2 * p]
-        first_lo = b0 < nb // 2
-        lo = jnp.where(first_lo, b0, nb - 1 - b0)
-        hi = nb - 1 - lo
-        u_lo = 2 * p + jnp.where(first_lo, 0, 1)
-        u_hi = 2 * p + jnp.where(first_lo, 1, 0)
-        n_lo = lax.div(lo, 2)
-        n_hi = lax.div(hi, 2)
-        def scores(kt, u):
-            return dot(k_ref[pl.ds(pl.multiple_of(kt * 256, 256), 256), :], qs_s[u])
-        def pv(kt, p16):
-            c = pl.ds(pl.multiple_of(kt * 256, 256), 256)
-            return jnp.concatenate([dot(vt_s[0:128, c], p16[:, 0:256]), dot(vt_s[128:256, c], p16[:, 256:512])], axis=1)
-        for (s, kt, u, qp) in ((0, n_lo, u_lo, lo), (1, n_hi, u_hi, hi)):
-            st = scores(kt, u)
-            st = jnp.where(d_s[...] <= qp * 128 - kt * 256, st, -1e30)
-            m = jnp.max(st, axis=0, keepdims=True)
-            pr = jnp.exp2(st - m)
-            m_s[s] = m
-            l_s[s] = jnp.sum(pr, axis=0, keepdims=True)
-            acc_s[s] = pv(kt, pr.astype(bf16))
-        for t in range(nb // 2 - 1):
-            is_lo = t < n_lo
-            s = jnp.where(is_lo, 0, 1)
-            kt = jnp.where(is_lo, t, t - n_lo)
-            u = jnp.where(is_lo, u_lo, u_hi)
-            st = scores(kt, u)
-            m_old = m_s[s]
-            m = jnp.maximum(m_old, jnp.max(st, axis=0, keepdims=True))
-            pr = jnp.exp2(st - m)
-            al = jnp.exp2(m_old - m)
-            m_s[s] = m
-            l_s[s] = l_s[s] * al + jnp.sum(pr, axis=0, keepdims=True)
-            acc_s[s] = acc_s[s] * al + pv(kt, pr.astype(bf16))
-        for (s, u) in ((0, u_lo), (1, u_hi)):
-            l = l_s[s]
-            lse_ref[u] = m_s[s] + jnp.log2(l)
-            a = acc_s[s] * (1.0 / l)
-            ot = jnp.concatenate([a[64 * (h % 2):64 * (h % 2) + 64, 128 * h:128 * h + 128] for h in range(4)], axis=0)
-            o_ref[pl.ds(pl.multiple_of(u * 128, 128), 128), :] = ot.T
+    lax.fori_loop(0, 4, piece, 0)
+
+
+def by_pair(vt, p16):
+    return jnp.concatenate([dot(vt[0:128], p16[:, 0:256]), dot(vt[128:256], p16[:, 256:512])], axis=1)
+
+
+def unpair(a):
+    return jnp.concatenate([a[64 * (h % 2):64 * (h % 2) + 64, 128 * h:128 * h + 128] for h in range(HEADS_HERE)], axis=0)
+
+
+def fwd_step(pairs, r, i, own, K, VT, qs, m_s, l_s, acc, d_s, sb, pb):
+    col = lambda v: jnp.max(v, axis=0, keepdims=True)
+    tot = lambda v: jnp.sum(v, axis=0, keepdims=True)
+    lo_i = pairs.lo(i)
+    pick = [lo_i > pairs.lo(r * 4 + j) for j in range(4)]
+    sa = dot(K[r, 0], qs[i, 1])
+    for j in range(4):
+        u = jnp.where(pick[j], 0, 1)
+        s = dot(K[r, u, j * BLOCK:(j + 1) * BLOCK, :], qs[i, u])
+        if own:
+            s = jnp.where(d_s[...] <= jnp.where(i == j, 0, 2 * BLOCK), s, FAR)
+        sb[j] = s
+    tops = [col(sb[j]) for j in range(4)]
+    m_hi, m_lo = col(sa), None
+    for j in range(4):
+        m_hi = jnp.maximum(m_hi, jnp.where(pick[j], FAR, tops[j]))
+        t = jnp.where(pick[j], tops[j], FAR)
+        m_lo = t if m_lo is None else jnp.maximum(m_lo, t)
+    if own:
+        rows = pl.ds(pl.multiple_of(i * BLOCK, BLOCK), BLOCK)
+        sd = jnp.where(d_s[...] <= 0, dot(K[r, 0, rows, :], qs[i, 0]), FAR)
+        m_lo = jnp.maximum(m_lo, col(sd))
+    else:
+        old_hi, old_lo = m_s[i, 1], m_s[i, 0]
+        m_hi, m_lo = jnp.maximum(m_hi, old_hi), jnp.maximum(m_lo, old_lo)
+    pa = jnp.exp2(sa - m_hi)
+    l_hi, l_lo = tot(pa), jnp.zeros((1, 512), f32)
+    for j in range(4):
+        p = jnp.exp2(sb[j] - jnp.where(pick[j], m_lo, m_hi))
+        t = tot(p)
+        l_hi = l_hi + jnp.where(pick[j], 0.0, t)
+        l_lo = l_lo + jnp.where(pick[j], t, 0.0)
+        low = p.astype(bf16)
+        rows = slice(j * BLOCK, (j + 1) * BLOCK)
+        zero = jnp.zeros_like(low)
+        pb[0, rows, :] = jnp.where(pick[j], low, zero)
+        pb[1, rows, :] = jnp.where(pick[j], zero, low)
+    o_hi = by_pair(VT[r, 0], pa.astype(bf16)) + by_pair(VT[r, 1], pb[1])
+    o_lo = by_pair(VT[r, 0], pb[0])
+    if own:
+        p = jnp.exp2(sd - m_lo)
+        l_lo = l_lo + tot(p)
+        at = pl.ds(pl.multiple_of(i * BLOCK, BLOCK), BLOCK)
+        o_lo = o_lo + by_pair(VT[r, 0, :, at], p.astype(bf16))
+        l_s[i, 1], l_s[i, 0] = l_hi, l_lo
+        acc[i, 1], acc[i, 0] = o_hi, o_lo
+    else:
+        f_hi, f_lo = jnp.exp2(old_hi - m_hi), jnp.exp2(old_lo - m_lo)
+        l_s[i, 1] = l_s[i, 1] * f_hi + l_hi
+        l_s[i, 0] = l_s[i, 0] * f_lo + l_lo
+        acc[i, 1] = acc[i, 1] * f_hi + o_hi
+        acc[i, 0] = acc[i, 0] * f_lo + o_lo
+    m_s[i, 1], m_s[i, 0] = m_hi, m_lo
+
+
+def fwd_finish(pairs, m_s, l_s, acc, lse, ot, o_ref):
+    def pair(i, _):
+        first = pairs.first_lo(i)
+        out = []
+        for u in range(2):
+            l = l_s[i, u]
+            lse[i, u] = m_s[i, u] + jnp.log2(l)
+            t = unpair(acc[i, u] * (1.0 / l))
+            ot[i, u] = t
+            out.append(t.T.astype(bf16))
+        o_ref[i, 0:BLOCK, :] = jnp.where(first, out[0], out[1])
+        o_ref[i, BLOCK:2 * BLOCK, :] = jnp.where(first, out[1], out[0])
         return 0
     lax.fori_loop(0, 4, pair, 0)
 
-def attn_fwd(blk, x, wq, wkv, bq, bkv):
-    nb = blk.shape[0]
+
+def diagonal(d_s):
+    d_s[...] = lax.broadcasted_iota(jnp.int32, d_s.shape, 0) - (lax.broadcasted_iota(jnp.int32, d_s.shape, 1) & (BLOCK - 1))
+
+
+def fwd_local(nz, blk_ref, x_ref, wqkv_ref, bq_ref, bkv_ref, bkvt_ref, o_ref, ot, lse, K, V, KT, qn, qt, VT, qs, m_s, l_s, acc, d_s, sb, pb, wkvt):
+    pairs = Pairs(nz * 8, lambda n: blk_ref[2 * n])
+    diagonal(d_s)
+    wkvt[...] = turned(wqkv_ref[:, 256:])
+    project_queries(pairs, x_ref, wqkv_ref.at[:, 0:256], bq_ref, qn, qt, qs)
+    for r in range(nz):
+        project_chunk(pairs, r, x_ref, wqkv_ref.at[:, 256:768], wkvt, bkv_ref, bkvt_ref, K, V, KT, VT)
+        def step(i, _):
+            fwd_step(pairs, r, i, r == 0, K, VT, qs, m_s, l_s, acc, d_s, sb, pb)
+            return 0
+        lax.fori_loop(0, 4, step, 0)
+    fwd_finish(pairs, m_s, l_s, acc, lse, ot, o_ref)
+
+
+def fwd_outs(nz):
+    sds = jax.ShapeDtypeStruct
+    kv = sds((nz, 2, 512, 256), bf16)
+    return (sds((4, 256, 256), bf16), sds((4, 2, 256, 128), f32), sds((4, 2, 1, 512), f32), kv, kv, sds((nz, 2, 256, 512), bf16),
+            sds((4, 2, 128, 256), bf16), sds((4, 2, 256, 128), bf16))
+
+
+def fwd_scratch(nz):
+    M = pltpu.VMEM
+    return [M((nz, 2, 256, 512), bf16), M((4, 2, 256, 512), bf16), M((4, 2, 1, 512), f32), M((4, 2, 1, 512), f32), M((4, 2, 128, 512), f32),
+            M((128, 512), jnp.int32), M((4, 128, 512), f32), M((2, 512, 512), bf16), M((512, 512), bf16)]
+
+
+def attn_fwd(nz, blk, x, wqkv, bq, bkv):
     V = pl.BlockSpec(memory_space=pltpu.VMEM)
     return pl.pallas_call(
-        functools.partial(fwd_kernel, nb),
-        out_shape=(jax.ShapeDtypeStruct((1024, 256), f32), jax.ShapeDtypeStruct((8, 1, 512), f32),
-                   jax.ShapeDtypeStruct((nb * 128, 256), bf16), jax.ShapeDtypeStruct((nb * 128, 256), bf16),
-                   jax.ShapeDtypeStruct((8, 256, 128), bf16), jax.ShapeDtypeStruct((1024, 256), bf16)),
-        in_specs=[pl.BlockSpec(memory_space=pltpu.SMEM)] + [V] * 5, out_specs=(V,) * 6,
-        scratch_shapes=[pltpu.VMEM((256, nb * 128), bf16), pltpu.VMEM((8, 256, 512), bf16), pltpu.VMEM((2, 128, 512), f32),
-                        pltpu.VMEM((2, 1, 512), f32), pltpu.VMEM((2, 1, 512), f32), pltpu.VMEM((256, 512), jnp.int32)],
-        compiler_params=pltpu.CompilerParams(vmem_limit_bytes=56 << 20),
-        name="attn_fwd")(blk, x, wq, wkv, bq, bkv)
-
-def bwd_kernel(nb, blk_ref, x_ref, k_ref, v_ref, qt_ref, q_ref, lse_ref, do_ref, of_ref, wq_ref, wkv_ref,
-               dx_ref, gq_ref, db_ref, dw_ref, dxq_s, dqa_s, kt_s, qs_s, qn_s, dot_s, don_s, dl_s, dk_s, dv_s, dq_s, d_s):
-    qs_s[...] = jnp.zeros_like(qs_s)
-    qn_s[...] = jnp.zeros_like(qn_s)
-    dot_s[...] = jnp.zeros_like(dot_s)
-    don_s[...] = jnp.zeros_like(don_s)
-    dk_s[...] = jnp.zeros_like(dk_s)
-    dv_s[...] = jnp.zeros_like(dv_s)
-    d_s[...] = lax.broadcasted_iota(jnp.int32, d_s.shape, 0) - (lax.broadcasted_iota(jnp.int32, d_s.shape, 1) & 127)
-    def prep_k(j, _):
-        r = pl.ds(pl.multiple_of(j * 256, 256), 256)
-        kt_s[:, r] = k_ref[r, :].astype(f32).T.astype(bf16)
+        functools.partial(fwd_local, nz), out_shape=fwd_outs(nz),
+        in_specs=[pl.BlockSpec(memory_space=pltpu.SMEM)] + [V] * 5, out_specs=(V,) * 8, scratch_shapes=fwd_scratch(nz),
+        compiler_params=pltpu.CompilerParams(vmem_limit_bytes=58 << 20), name="attn_fwd")(blk, x, wqkv, bq, bkv, bkv.reshape(256, 1))
+
+
+def bwd_queries(pairs, do_ref, ot, qn, qt, qs, dos, qns, dons, dl):
+    for s in (qs, dos, qns, dons):
+        s[...] = jnp.zeros_like(s)
+
+    def piece(i, _):
+        for u, do in enumerate(pairs.ordered(i, do_ref[i])):
+            dot_t = do.astype(f32).T
+            prod = dot_t * ot[i, u]
+            low = dot_t.astype(bf16)
+            q, t = qn[i, u], qt[i, u]
+            for hs, cs in head_slices():
+                qs[i, u, hs, cs] = t[hs]
+                dos[i, u, hs, cs] = low[hs]
+                qns[i, u, cs, hs] = q[:, hs]
+                dons[i, u, cs, hs] = do[:, hs]
+                dl[i, u, :, cs] = jnp.sum(prod[hs], axis=0, keepdims=True)
         return 0
-    lax.fori_loop(0, nb // 2, prep_k, 0)
-    def prep_q(u, s):
-        r = pl.ds(pl.multiple_of(u * 128, 128), 128)
-        do = do_ref[r, :]
-        doT = do.astype(f32).T
-        dlT = doT * of_ref[r, :].T
-        q = q_ref[r, :]
-        qt = qt_ref[u]
-        for h in range(4):
-            hs = slice(64 * h, 64 * h + 64)
-            cs = slice(128 * h, 128 * h + 128)
-            qs_s[s, hs, cs] = qt[hs]
-            dot_s[s, hs, cs] = doT[hs].astype(bf16)
-            dl_s[s, :, cs] = jnp.sum(dlT[hs], axis=0, keepdims=True)
-            qn_s[s, cs, hs] = q[:, hs]
-            don_s[s, cs, hs] = do[:, hs]
-    def pair(p, _):
-        b0 = blk_ref[2 * p]
-        first_lo = b0 < nb // 2
-        lo = jnp.where(first_lo, b0, nb - 1 - b0)
-        hi = nb - 1 - lo
-        u_lo = 2 * p + jnp.where(first_lo, 0, 1)
-        u_hi = 2 * p + jnp.where(first_lo, 1, 0)
-        n_lo = lax.div(lo, 2)
-        n_hi = lax.div(hi, 2)
-        prep_q(u_lo, 0)
-        prep_q(u_hi, 1)
-        def step(s, kt, u, qp, masked):
-            r = pl.ds(pl.multiple_of(kt * 256, 256), 256)
-            st = dot(k_ref[r, :], qs_s[s]) - lse_ref[u]
-            if masked:
-                st = jnp.where(d_s[...] <= qp * 128 - kt * 256, st, -1e30)
-            pr = jnp.exp2(st)
-            dp = dot(v_ref[r, :], dot_s[s]) - dl_s[s]
-            ds = (pr * dp).astype(bf16)
-            dv_s[r, :] += dot(pr.astype(bf16), don_s[s])
-            dk_s[r, :] += dot(ds, qn_s[s])
-            dq = jnp.concatenate([dot(kt_s[0:128, r], ds[:, 0:256]), dot(kt_s[128:256, r], ds[:, 256:512])], axis=1)
-            if masked:
-                dq_s[s] = dq
-            else:
-                dq_s[s] += dq
-        step(0, n_lo, u_lo, lo, True)
-        step(1, n_hi, u_hi, hi, True)
-        for t in range(nb // 2 - 1):
-            is_lo = t < n_lo
-            step(jnp.where(is_lo, 0, 1), jnp.where(is_lo, t, t - n_lo), jnp.where(is_lo, u_lo, u_hi), 0, False)
-        for (s, u) in ((0, u_lo), (1, u_hi)):
-            a = dq_s[s] * 0.125
-            dqT = jnp.concatenate([a[64 * (h % 2):64 * (h % 2) + 64, 128 * h:128 * h + 128] for h in range(4)], axis=0)
-            dqa_s[pl.ds(pl.multiple_of(u * 128, 128), 128), :] = dqT.T.astype(bf16)
+    lax.fori_loop(0, 4, piece, 0)
+
+
+def bwd_step(pairs, r, i, own, first, K, V, KT, qs, dos, qns, dons, lse, dl, dk, dv, dq, d_s, gb):
+    lo_i = pairs.lo(i)
+    pick = [lo_i > pairs.lo(r * 4 + j) for j in range(4)]
+
+    def pieces(k, v, u, mask):
+        s = dot(k, qs[i, u]) - lse[i, u]
+        if mask is not None:
+            s = jnp.where(d_s[...] <= mask, s, FAR)
+        p = jnp.exp2(s)
+        g = p * (dot(v, dos[i, u]) - dl[i, u])
+        return p.astype(bf16), g.astype(bf16)
+
+    p, g = pieces(K[r, 0], V[r, 0], 1, None)
+    dv[0] += dot(p, dons[i, 1])
+    dk[0] += dot(g, qns[i, 1])
+    q_hi = by_pair(KT[r, 0], g)
+    for j in range(4):
+        u = jnp.where(pick[j], 0, 1)
+        rows = slice(j * BLOCK, (j + 1) * BLOCK)
+        p, g = pieces(K[r, u, rows, :], V[r, u, rows, :], u, jnp.where(i == j, 0, 2 * BLOCK) if own else None)
+        gv, gk = dot(p, dons[i, u]), dot(g, qns[i, u])
+        dv[0, rows, :] += jnp.where(pick[j], gv, 0.0)
+        dv[1, rows, :] += jnp.where(pick[j], 0.0, gv)
+        dk[0, rows, :] += jnp.where(pick[j], gk, 0.0)
+        dk[1, rows, :] += jnp.where(pick[j], 0.0, gk)
+        zero = jnp.zeros_like(g)
+        gb[0, rows, :] = jnp.where(pick[j], g, zero)
+        gb[1, rows, :] = jnp.where(pick[j], zero, g)
+    q_hi = q_hi + by_pair(KT[r, 1], gb[1])
+    q_lo = by_pair(KT[r, 0], gb[0])
+    if own:
+        rows = pl.ds(pl.multiple_of(i * BLOCK, BLOCK), BLOCK)
+        p, g = pieces(K[r, 0, rows, :], V[r, 0, rows, :], 0, 0)
+        dv[0, rows, :] += dot(p, dons[i, 0])
+        dk[0, rows, :] += dot(g, qns[i, 0])
+        q_lo = q_lo + by_pair(KT[r, 0, :, rows], g)
+    if first:
+        dq[i, 1], dq[i, 0] = q_hi, q_lo
+    else:
+        dq[i, 1] += q_hi
+        dq[i, 0] += q_lo
+
+
+def bwd_chunk_out(pairs, r, last, x_ref, wqkv_ref, dk, dv, dxq, dx, dw, db):
+    def piece(p, _):
+        at = pl.ds(pl.multiple_of(p * BLOCK, BLOCK), BLOCK)
+        g = [jnp.concatenate([(dk[u, at, :] * (1.0 / LOG2E)).astype(bf16), dv[u, at, :].astype(bf16)], axis=1) for u in range(2)]
+        first = pairs.first_lo(r * 4 + p)
+        g = jnp.concatenate([jnp.where(first, g[0], g[1]), jnp.where(first, g[1], g[0])], axis=0)
+        d = dot(g, wqkv_ref[:, 256:768], NT)
+        if last:
+            d = d + dxq[p]
+        dx[r, pl.ds(pl.multiple_of(p * 256, 256), 256), :] = d.astype(bf16)
+        dw[:, 256:768] += dot(x_ref[r, p], g, TN)
+        db[1:2, :] += jnp.sum(g[:, 256:].astype(f32), axis=0, keepdims=True)
         return 0
-    lax.fori_loop(0, 4, pair, 0)
-    dw_ref[...] = jnp.zeros_like(dw_ref)
-    db_ref[...] = jnp.zeros_like(db_ref)
-    def fin_q(u, _):
-        r = pl.ds(pl.multiple_of(u * 128, 128), 128)
-        dq = dqa_s[r, :]
-        dxq_s[r, :] = dot(dq, wq_ref[...], NT)
-        dw_ref[:, 0:256] += dot(x_ref[r, :], dq, TN)
-        db_ref[0:1, :] += jnp.sum(dq.astype(f32), axis=0, keepdims=True)
+    lax.fori_loop(0, 4, piece, 0)
+
+
+def bwd_query_out(pairs, x_ref, wqkv_ref, dq, dxq, dw, db):
+    def piece(i, _):
+        t = [(unpair(dq[i, u]) * 0.125).T.astype(bf16) for u in range(2)]
+        first = pairs.first_lo(i)
+        g = jnp.concatenate([jnp.where(first, t[0], t[1]), jnp.where(first, t[1], t[0])], axis=0)
+        dxq[i] = dot(g, wqkv_ref[:, 0:256], NT)
+        dw[:, 0:256] += dot(x_ref[0, i], g, TN)
+        db[0:1, :] += jnp.sum(g.astype(f32), axis=0, keepdims=True)
         return 0
-    lax.fori_loop(0, 8, fin_q, 0)
-    def fin_k(b, with_q):
-        r = pl.ds(pl.multiple_of(b * 128, 128), 128)
-        g = pl.ds(pl.multiple_of(blk_ref[b] * 128, 128), 128)
-        dkv = jnp.concatenate([(dk_s[g, :] * (1.0 / LOG2E)).astype(bf16), dv_s[g, :].astype(bf16)], axis=1)
-        d = dot(dkv, wkv_ref[...], NT)
-        if with_q:
-            d = d + dxq_s[r, :]
-        dx_ref[r, :] = d.astype(bf16)
-        dw_ref[:, 256:768] += dot(x_ref[r, :], dkv, TN)
-        db_ref[1:2, :] += jnp.sum(dkv[:, 256:].astype(f32), axis=0, keepdims=True)
-    def fin_a(b, _):
-        fin_k(b, True)
-        return 0
-    def fin_b(b, _):
-        fin_k(b, False)
-        return 0
-    lax.fori_loop(0, 8, fin_a, 0)
-    lax.fori_loop(8, nb, fin_b, 0)
+    lax.fori_loop(0, 4, piece, 0)
+
+
+def weight_rows(dw, gq):
     for k in range(2):
         for m in range(3):
-            gq_ref[k, m * 256:m * 256 + 256, :] = dw_ref[k * 256:k * 256 + 256, m * 256:m * 256 + 256].astype(bf16)
-
-def attn_bwd(blk, x, k, v, qt, q, lse, do, of, wq, wkv):
-    nb = blk.shape[0]
-    V = pl.BlockSpec(memory_space=pltpu.VMEM)
+            gq[k, m * 256:m * 256 + 256, :] = dw[k * 256:k * 256 + 256, m * 256:m * 256 + 256].astype(bf16)
+
+
+def bwd_local(nz, blk_ref, x_ref, wqkv_ref, K, V, KT, qn, qt, ot, lse, do_ref, dx, gq, db, qs, dos, qns, dons, dl, dk, dv, dq, d_s, gb, dxq, dw):
+    pairs = Pairs(nz * 8, lambda n: blk_ref[2 * n])
+    diagonal(d_s)
+    dw[...] = jnp.zeros_like(dw)
+    db[...] = jnp.zeros_like(db)
+    bwd_queries(pairs, do_ref, ot, qn, qt, qs, dos, qns, dons, dl)
+    for r in list(range(1, nz)) + [0]:
+        dk[...] = jnp.zeros_like(dk)
+        dv[...] = jnp.zeros_like(dv)
+        def step(i, _):
+            bwd_step(pairs, r, i, r == 0, r == 1, K, V, KT, qs, dos, qns, dons, lse, dl, dk, dv, dq, d_s, gb)
+            return 0
+        lax.fori_loop(0, 4, step, 0)
+        if r == 0:
+            bwd_query_out(pairs, x_ref, wqkv_ref, dq, dxq, dw, db)
+        bwd_chunk_out(pairs, r, r == 0, x_ref, wqkv_ref, dk, dv, dxq, dx, dw, db)
+    weight_rows(dw, gq)
+
+
+def bwd_scratch():
+    M = pltpu.VMEM
+    return [M((4, 2, 256, 512), bf16), M((4, 2, 256, 512), bf16), M((4, 2, 512, 256), bf16), M((4, 2, 512, 256), bf16), M((4, 2, 1, 512), f32),
+            M((2, 512, 256), f32), M((2, 512, 256), f32), M((4, 2, 128, 512), f32), M((128, 512), jnp.int32), M((2, 512, 512), bf16),
+            M((4, 256, 512), f32), M((512, 768), f32)]
+
+
+def attn_bwd(nz, blk, x, wqkv, K, V, KT, qn, qt, ot, lse, do):
+    S = pl.BlockSpec(memory_space=pltpu.VMEM)
+    sds = jax.ShapeDtypeStruct
     return pl.pallas_call(
-        functools.partial(bwd_kernel, nb),
-        out_shape=(jax.ShapeDtypeStruct((nb * 128, 512), bf16), jax.ShapeDtypeStruct((2, 768, 256), bf16),
-                   jax.ShapeDtypeStruct((8, 256), f32)),
-        in_specs=[pl.BlockSpec(memory_space=pltpu.SMEM)] + [V] * 10, out_specs=(V,) * 3,
-        scratch_shapes=[pltpu.VMEM((512, 768), f32), pltpu.VMEM((1024, 512), f32), pltpu.VMEM((1024, 256), bf16), pltpu.VMEM((256, nb * 128), bf16), pltpu.VMEM((2, 256, 512), bf16), pltpu.VMEM((2, 512, 256), bf16),
-                        pltpu.VMEM((2, 256, 512), bf16), pltpu.VMEM((2, 512, 256), bf16), pltpu.VMEM((2, 1, 512), f32),
-                        pltpu.VMEM((nb * 128, 256), f32), pltpu.VMEM((nb * 128, 256), f32), pltpu.VMEM((2, 128, 512), f32),
-                        pltpu.VMEM((256, 512), jnp.int32)],
-        compiler_params=pltpu.CompilerParams(vmem_limit_bytes=60 << 20),
-        name="attn_bwd")(blk, x, k, v, qt, q, lse, do, of, wq, wkv)
-
-
-def dense_kernel(x_ref, cot_ref, att_ref, wo_ref, wu_ref, wd_ref, vec_ref, bup_ref,
+        functools.partial(bwd_local, nz), out_shape=(sds((nz, 1024, 512), bf16), sds((2, 768, 256), bf16), sds((8, 256), f32)),
+        in_specs=[pl.BlockSpec(memory_space=pltpu.SMEM)] + [S] * 10, out_specs=(S,) * 3, scratch_shapes=bwd_scratch(),
+        compiler_params=pltpu.CompilerParams(vmem_limit_bytes=58 << 20), name="attn_bwd")(blk, x, wqkv, K, V, KT, qn, qt, ot, lse, do)
+
+
+def dense_kernel(x_ref, cot_ref, att_ref, wo_ref, wu_ref, wd_ref, sm_ref,
                  out_ref, dsm_ref, do_ref, gw_ref, gv_ref, act_s, gp_s, norm_s, dpre_s):
     ff = wu_ref.shape[1]
     chunk = 512
     x = x_ref[...].astype(f32)
-    vec = lambda i: vec_ref[i:i + 1, :]
-    b_out, g1, s1, b_down, g2, s2 = (vec(i) for i in range(6))
+    vec = lambda i: jnp.concatenate([sm_ref[0, i:i + 1, :], sm_ref[1, i:i + 1, :]], axis=1)
+    b_out, g1, s1, b_down, g2, s2 = (vec(i) for i in range(2, 8))
     mean = lambda v: jnp.mean(v, axis=-1, keepdims=True)
     col = lambda v: jnp.sum(v, axis=0, keepdims=True)
     mix = x + dot(att_ref[...], wo_ref[...]) + b_out
@@ -239,7 +352,9 @@
     ffn = None
     for f in range(0, ff, chunk):
         fs = slice(f, f + chunk)
-        pre = dot(nlow, wu_ref[:, fs]) + bup_ref[:, fs]
+        at = 8 + f % (ff // 2) // 256
+        b_up = jnp.concatenate([sm_ref[2 * f // ff, at + k:at + k + 1, :] for k in range(chunk // 256)], axis=1)
+        pre = dot(nlow, wu_ref[:, fs]) + b_up
         c0 = math.sqrt(2.0 / math.pi)
         sq = pre * pre
         th = jnp.tanh(c0 * pre * (1.0 + 0.044715 * sq))
@@ -289,7 +404,7 @@
     put(dot(att_ref[...], dbr, TN), 0, half_rows)
 
 
-def dense(x, cot, att, wo, wu, wd, vecs, bup):
+def dense(x, cot, att, wo, wu, wd, sm):
     V = pl.BlockSpec(memory_space=pltpu.VMEM)
     tok, dim = x.shape
     ff = wu.shape[1]
@@ -299,11 +414,11 @@
         out_shape=(jax.ShapeDtypeStruct((tok, dim), bf16), jax.ShapeDtypeStruct((tok, dim), f32),
                    jax.ShapeDtypeStruct((tok, dim), bf16), jax.ShapeDtypeStruct((2, rows, dim), bf16),
                    jax.ShapeDtypeStruct((16, dim), f32)),
-        in_specs=[V] * 8, out_specs=(V,) * 5,
+        in_specs=[V] * 7, out_specs=(V,) * 5,
         scratch_shapes=[pltpu.VMEM((tok, ff), bf16), pltpu.VMEM((tok, ff), f32), pltpu.VMEM((tok, dim), bf16),
                         pltpu.VMEM((8, 128), f32)],
         compiler_params=pltpu.CompilerParams(vmem_limit_bytes=56 << 20),
-        name="dense")(x, cot, att, wo, wu, wd, vecs, bup)
+        name="dense")(x, cot, att, wo, wu, wd, sm)
 
 
 MESH = pl.DeviceIdType.MESH
@@ -624,6 +739,153 @@
         name="reduce_all")(dx, gw, gq, gv)
 
 
+def chip_pairs(nz, order_ref):
+    me = lax.axis_index("ctx")
+    z, y, c = me // 4, lax.rem(me // 2, 2), lax.rem(me, 2)
+
+    def first(n):
+        r, p = n // 4, n % 4
+        a, b = p % 2, p // 2
+        yy, cc = y + a - 2 * y * a, c + b - 2 * c * b
+        return order_ref[y, 2 * (lax.rem(z - r + nz, nz) * 4 + yy * 2 + cc)]
+    return Pairs(nz * 8, first)
+
+
+def front_kernel(nz, order_ref, bqr, bvr, bor, g1r, s1r, bdr, g2r, s2r, bur, x_ref, wq_ref, wk_ref, wv_ref, wo_ref, wu_ref, wd_ref,
+                 att, wo, wu, wd, sm, xall, wqkv, ot_o, lse_o, K_o, V_o, KT_o, qn_o, qt_o,
+                 xs, ws, sms, K, V, KT, VT, qn, qt, qs, m_s, l_s, acc, d_s, sb, pb, wkvt, bkvt, ot, lse, o_s, send, recv, lsem):
+    me, wi, z, y, c, low, to = places(nz)
+    to["yc"] = (z * 4 + 3 - low, wi)
+    half, R = 256, wq_ref.shape[0]
+    local = []
+
+    def copy(src, dst):
+        cp = pltpu.make_async_copy(src, dst, lsem.at[len(local)])
+        cp.start()
+        local.append(cp)
+        return cp
+
+    own_x = copy(x_ref.at[y], xs.at[0, 0])
+    own_w = [copy(w.at[:, rows_of(c * half, half, 128)], ws.at[rows_of(wi * R, R), pl.ds(i * half, half)]) for i, w in enumerate((wq_ref, wk_ref, wv_ref))]
+    for i, v in enumerate((bqr, bvr, bor, g1r, s1r, bdr, g2r, s2r)):
+        sms[wi, i:i + 1, :] = v[...].astype(f32).reshape(1, half)
+    up_b = bur[...].astype(f32).reshape(1, 1024)
+    for i in range(4):
+        sms[wi, 8 + i:9 + i, :] = up_b[:, i * half:(i + 1) * half]
+    sms[wi, 12:16, :] = jnp.zeros((4, half), f32)
+    meet([to[k] for k in ("up", "down", "core", "y", "yc", "x")])
+    w = Wires(send, recv)
+    yx = w.go(x_ref.at[1 - y], xs.at[0, 1], to["y"])
+    ring, core = {}, {}
+    ring[1, 0] = w.go(x_ref.at[y], xs.at[1, 0], to["up"])
+    core[0, 0] = w.go(x_ref.at[y], xs.at[0, 2], to["core"])
+    wx = []
+    for i, m in enumerate((wq_ref, wk_ref, wv_ref)):
+        wx.append(w.go(m.at[:, rows_of(c * half, half, 128)], ws.at[rows_of(wi * R, R), pl.ds(i * half, half)], to["x"]))
+    wx.append(w.go(sms.at[wi], sms.at[wi], to["x"]))
+    big = []
+    for m, full in ((wo_ref, wo), (wu_ref, wu), (wd_ref, wd)):
+        n = m.shape[0]
+        h = n // 2
+        copy(m, full.at[rows_of(wi * n, n)])
+        big.append((w.go(m.at[rows_of(c * h, h)], full.at[rows_of(wi * n + c * h, h)], to["x"]), full, rows_of((1 - wi) * n + c * h, h)))
+
+    pairs = chip_pairs(nz, order_ref)
+    diagonal(d_s)
+    yx.wait_recv()
+    ring[1, 1] = w.go(xs.at[0, 1], xs.at[1, 1], to["up"])
+    core[0, 1] = w.go(xs.at[0, 1], xs.at[0, 3], to["core"])
+
+    def pump(r, s):
+        ring[r, s].wait_recv()
+        if r < nz - 1:
+            ring[r + 1, s] = w.go(xs.at[r, s], xs.at[r + 1, s], to["up"])
+        core[r, s] = w.go(xs.at[r, s], xs.at[r, 2 + s], to["core"])
+
+    shared = []
+
+    def share(k):
+        cp, full, where = big[k]
+        cp.wait_recv()
+        shared.append(w.go(full.at[where], full.at[where], to["core"]))
+
+    pump(1, 0)
+    for cp in own_w:
+        cp.wait()
+    for cp in wx:
+        cp.wait_recv()
+    copy(sms, sm)
+    copy(ws, wqkv)
+    wkvt[...] = turned(ws[:, 256:])
+    bv = sms[c, 1:2, :]
+    bkvt[...] = jnp.broadcast_to(bv, (8, half)).T[:, 0:1]
+    own_x.wait()
+    for s in range(2):
+        core[0, s].wait_recv()
+    project_queries(pairs, xs, ws.at[:, 0:256], sms.at[c, 0:1], qn, qt, qs)
+    copy(qn, qn_o)
+    copy(qt, qt_o)
+
+    def chunk(r):
+        project_chunk(pairs, r, xs, ws.at[:, 256:768], wkvt, sms.at[c, 1:2], bkvt, K, V, KT, VT)
+        for a, b in ((xs, xall), (K, K_o), (V, V_o), (KT, KT_o)):
+            copy(a.at[r], b.at[r])
+
+    def attend(r, start, stop):
+        def step(i, _):
+            fwd_step(pairs, r, i, r == 0, K, VT, qs, m_s, l_s, acc, d_s, sb, pb)
+            return 0
+        lax.fori_loop(start, stop, step, 0)
+
+    chunk(0)
+    pump(1, 1)
+    attend(0, 0, 2)
+    attend(0, 2, 4)
+    for r in range(1, nz):
+        if r + 1 < nz:
+            pump(r + 1, 0)
+        for s in range(2):
+            core[r, s].wait_recv()
+        chunk(r)
+        attend(r, 0, 2)
+        if r + 1 < nz:
+            pump(r + 1, 1)
+            share(r - 1)
+        attend(r, 2, 4)
+    fwd_finish(pairs, m_s, l_s, acc, lse, ot, o_s)
+    cols = pl.ds(pl.multiple_of(c * half, half), half)
+    outs = [w.go(o_s.at[p], att.at[y, :, cols], to[k]) for p, k in ((1, "y"), (2, "core"), (3, "yc"))]
+    copy(o_s.at[0], att.at[y, :, cols])
+    copy(ot, ot_o)
+    copy(lse, lse_o)
+    share(2)
+    for cp in outs + shared:
+        cp.wait_recv()
+    w.drain()
+    for cp in local[4:]:
+        cp.wait()
+
+
+def front(nz, order, vectors, x, weights):
+    A = pl.BlockSpec(memory_space=pltpu.HBM)
+    V = pl.BlockSpec(memory_space=pltpu.VMEM)
+    sds = jax.ShapeDtypeStruct
+    M = pltpu.VMEM
+    rows, dim = x.shape[1:]
+    wq, wk, wv, wo, wu, wd = weights
+    outs = [sds((2, rows, dim), bf16)] + [sds((2 * w.shape[0], w.shape[1]), bf16) for w in (wo, wu, wd)]
+    outs += [sds((2, 16, 256), f32), sds((nz, 4, rows, dim), bf16), sds((dim, 768), bf16)] + list(fwd_outs(nz)[1:])
+    scratch = [M((nz, 4, rows, dim), bf16), M((dim, 768), bf16), M((2, 16, 256), f32)]
+    scratch += [M((nz, 2, 512, 256), bf16)] * 2 + [M((nz, 2, 256, 512), bf16)] * 2 + [M((4, 2, 128, 256), bf16), M((4, 2, 256, 128), bf16)]
+    scratch += fwd_scratch(nz)[1:] + [M((256, 1), f32), M((4, 2, 256, 128), f32), M((4, 2, 1, 512), f32), M((4, 256, 256), bf16)]
+    scratch += [pltpu.SemaphoreType.DMA((40,)), pltpu.SemaphoreType.DMA((40,)), pltpu.SemaphoreType.DMA((40,))]
+    return pl.pallas_call(
+        functools.partial(front_kernel, nz), out_shape=tuple(outs),
+        in_specs=[pl.BlockSpec(memory_space=pltpu.SMEM)] + [V] * 9 + [A] * 7, out_specs=(A,) * len(outs), scratch_shapes=scratch,
+        compiler_params=pltpu.CompilerParams(collective_id=1, has_side_effects=True, vmem_limit_bytes=58 << 20), name="front")(
+            order, *vectors, x, *weights)
+
+
 def body(block_in, block_order, w_query, b_query, w_key, w_value, b_value, w_out, b_out, gain_one, shift_one,
          w_up, b_up, w_down, b_down, gain_two, shift_two, cotangent, *, nc, nw):
     seqs, rows, dim = block_in.shape
@@ -641,46 +903,38 @@
     pick = lambda v, i: lax.dynamic_index_in_dim(v, i, 0, keepdims=False)
 
     ours = nw == 2 and nz == 4
-    small = jnp.concatenate([v.reshape(-1, dim // nw) for v in (b_query, b_value, b_out, gain_one, shift_one, b_down, gain_two, shift_two, b_up)], axis=0)
-    if ours:
-        small = jnp.pad(small, ((0, -small.shape[0] % 16), (0, 0)))
-        x_all, wqkv, wo, wu, wd, small = gather_all(nz, block_in, (w_query, w_key, w_value, w_out, w_up, w_down), small)
-    else:
-        cols = lambda w: lax.dynamic_slice_in_dim(w, cc * half, half, 1)
-        wqkv = gather(jnp.concatenate([cols(w_query), cols(w_key), cols(w_value)], axis=1))
-        small = lax.all_gather(small, "wt", axis=0)
-        wo, wu, wd = gather(w_out), gather(w_up), gather(w_down)
-        x_all = gather_all(nz, block_in)[0]
-    x_all = x_all.reshape(-1, dim)
-    wq, wkv = wqkv[:, :half], wqkv[:, half:]
-    vecs = jnp.transpose(small[:, :8], (1, 0, 2)).reshape(8, dim).astype(f32)
-    bup = small[:, 8:8 + b_up.shape[0] // (dim // nw)].reshape(1, -1).astype(f32)
-    bq = lax.dynamic_slice_in_dim(vecs[0:1], cc * half, half, 1)
-    bkv = lax.dynamic_slice_in_dim(vecs[1:2], cc * half, half, 1)
-    dvec = vecs[2:8]
+    small = (b_query, b_value, b_out, gain_one, shift_one, b_down, gain_two, shift_two, b_up)
+    by_seq = lambda a, b: jnp.where(yy == 0, jnp.concatenate([a, b], 0), jnp.concatenate([b, a], 0))
     r_ids = (zz - jnp.arange(nz, dtype=jnp.int32)) % nz
     quad = (me % 4) ^ jnp.array([0, 2, 1, 3], jnp.int32)
     order_row = pick(block_order, yy)
     slots = (r_ids[:, None, None] * 4 + quad[None, :, None]) * hb + jnp.arange(hb, dtype=jnp.int32)
     blk = order_row[slots.reshape(-1)]
 
-    o, lse, k, v, qt, q = attn_fwd(blk, x_all, wq, wkv, bq, bkv)
-    o16 = o.astype(bf16)
-    o_self = o16[:rows]
-    o_y = perm(o16[rows:2 * rows], xor(2))
-    o_c = perm(o16[2 * rows:3 * rows], xor(1))
-    o_yc = perm(o16[3 * rows:], xor(3))
-    by_seq = lambda a, b: jnp.where(yy == 0, jnp.concatenate([a, b], 0), jnp.concatenate([b, a], 0))
-    mine, other = by_seq(o_self, o_y), by_seq(o_c, o_yc)
-    att = jnp.where(cc == 0, jnp.concatenate([mine, other], 1), jnp.concatenate([other, mine], 1))
-
-    out, dsm, d_o, gw, gv = dense(block_in.reshape(-1, dim), cotangent.reshape(-1, dim), att, wo, wu, wd, dvec, bup)
+    if ours:
+        att, wo, wu, wd, sm, x_all, wqkv, ot, lse, k, v, kt, qn, qt = front(nz, block_order, small, block_in, (w_query, w_key, w_value, w_out, w_up, w_down))
+        att = att.reshape(-1, dim)
+    else:
+        cols = lambda w: lax.dynamic_slice_in_dim(w, cc * half, half, 1)
+        wqkv = gather(jnp.concatenate([cols(w_query), cols(w_key), cols(w_value)], axis=1))
+        small = lax.all_gather(jnp.concatenate(small), "wt", axis=0)
+        vec8 = jnp.transpose(small[:, :8 * dim // nw].reshape(nw, 8, dim // nw), (1, 0, 2)).reshape(8, 2, half)
+        upb = small[:, 8 * dim // nw:].reshape(2, 4, half)
+        sm = jnp.pad(jnp.concatenate([jnp.transpose(vec8, (1, 0, 2)), upb], axis=1).astype(f32), ((0, 0), (0, 4), (0, 0)))
+        wo, wu, wd = gather(w_out), gather(w_up), gather(w_down)
+        x_all = gather_all(nz, block_in)[0]
+        o, ot, lse, k, v, kt, qn, qt = attn_fwd(nz, blk, x_all, wqkv, pick(sm, cc)[0:1], pick(sm, cc)[1:2])
+        o_self, o_y, o_c, o_yc = o[0], perm(o[1], xor(2)), perm(o[2], xor(1)), perm(o[3], xor(3))
+        mine, other = by_seq(o_self, o_y), by_seq(o_c, o_yc)
+        att = jnp.where(cc == 0, jnp.concatenate([mine, other], 1), jnp.concatenate([other, mine], 1))
+
+    out, dsm, d_o, gw, gv = dense(block_in.reshape(-1, dim), cotangent.reshape(-1, dim), att, wo, wu, wd, sm)
 
     d_o = d_o.reshape(seqs, rows, dim)
     d_own, d_oth = pick(d_o, yy), pick(d_o, 1 - yy)
     fh = lambda v, c: lax.dynamic_slice_in_dim(v, c * half, half, 1)
     do_all = jnp.concatenate([fh(d_own, cc), perm(fh(d_oth, cc), xor(2)), perm(fh(d_own, 1 - cc), xor(1)), perm(fh(d_oth, 1 - cc), xor(3))], axis=0)
-    dx, gq, gb = attn_bwd(blk, x_all, k, v, qt, q, lse, do_all, o, wq, wkv)
+    dx, gq, gb = attn_bwd(nz, blk, x_all, wqkv, k, v, kt, qn, qt, ot, lse, do_all.reshape(4, rows, half))
     gvec = jnp.zeros((24, dim), f32).at[:16].set(gv)
     gvec = lax.dynamic_update_slice(gvec, gb[0:1], (16, cc * half))
     gvec = lax.dynamic_update_slice(gvec, gb[1:2], (17, cc * half))

time: 319 us -> 282 us (0.88)
  local copies, waits for them, and re-layouts: 37.9 us -> 15.7 us
  waiting for transfers between devices: 9.67 us -> 4.17 us
  Pallas kernels: 256 us -> 252 us
    unnamed x41 -> x19, local copies, waits for them, and re-layouts: 16 us -> 3.13 us
    reshape x9 -> x0, local copies, waits for them, and re-layouts: 5.96 us -> none  [body(): v.reshape(-1, dim // nw)]
    ppermute x6 -> x3, waiting for transfers between devices: 9.67 us -> 4.17 us  [body(): perm = lambda v, p: lax.ppermute(v, 'ctx', p)]
    pallas_call x3 -> x2, Pallas kernels: 132 us -> 128 us  [the longest x1 79.7 us: front(): pl.pallas_call(functools.partial(front_kernel, nz), out_shape=tuple(outs)...]
  transfers between devices with their start and end apart: 6 -> 3, of which waited for: 4 -> 2; matrix products, arithmetic and copies ran while one was open for 1% -> 1% of each run, Pallas kernels for 0% -> 0%
where the time goes in v3:
time: 282 us
  Pallas kernels  252 us (89%)
  local copies, waits for them, and re-layouts  15.7 us (6%)
  other arithmetic  7.56 us (3%)
  waiting for transfers between devices  4.17 us (1%)
    pallas_call x1, Pallas kernels, reduce_all(): pl.pallas_call(functools.partial(reduce_kernel, nz), out_shape=(sds((2, 2...  109 us
    pallas_call x1, Pallas kernels, front(): pl.pallas_call(functools.partial(front_kernel, nz), out_shape=tuple(outs)...  79.7 us
    pallas_call x1, Pallas kernels, attn_bwd(): pl.pallas_call(functools.partial(bwd_local, nz), out_shape=(sds((nz, 1024...  48.6 us
    pallas_call x1, Pallas kernels, dense(): pl.pallas_call(dense_kernel, out_shape=(jax.ShapeDtypeStruct((tok, dim),...  14.7 us
  transfers between devices with their start and end apart: 3, of which 2 were waited for; matrix products, arithmetic and copies ran while one was open for 1% of the time, Pallas kernels for 0%

profile of v3, /device:TPU:0, one launch (start us, length us, event | category | flops | bytes accessed | tf_op | source)
XLA Modules:
  0.0 282.2 jit_solution(16419262289776086273)
XLA Ops:
  0.7 79.7 %front.1 = (bf16[2,256,512]{2,1,0:T(8,128)(2,1)}, bf16[512,512]{1,0:T(8,128)(2,1)}, bf16[512,2048]{1,0:T(8,128)(2,1)}, bf16[2048,512]{1,0:T(8,128)(2,1)}, f32[2,...) custom-call(s32[2,32]{1,0:T(2,128)} %order_ref.1, ...), custom_call_target="tpu_custom_call" | custom-call | tf_op jit(solution)/shard_map/front/pallas_call | solution.py:882
  80.5 0.0 copy-start.6
  80.5 0.0 copy-start.5
  80.5 14.7 %dense.1 = (bf16[512,512]{1,0:T(8,128)(2,1)}, f32[512,512]{1,0:T(8,128)}, bf16[512,512]{1,0:T(8,128)(2,1)}, bf16[2,2304,512]{2,1,0:T(8,128)(2,1)}, f32[16,512]{1,0:T(8,128)}) custom-call(bf16[512,512]{1,0:T(8,128)(2,1)} %bitcast.58, bf16[512,512]{1,0:T(8,128)(2,1)} %bitcast.63, bf16[512,512]{1,0:T(8,128)(2,1)} %bitcast.65, ...), custom_call_target="tpu_custom_call" | custom-call | tf_op jit(solution)/shard_map/dense/pallas_call | solution.py:412
  95.2 1.4 dynamic-slice_bitcast_fusion.3
  96.5 0.8 collective-permute-start.2
  97.3 0.9 collective-permute-start.1
  98.2 0.5 collective-permute-start
  98.7 0.0 copy-done.6
  98.8 0.1 add_multiply_fusion
  98.8 0.1 iota_add_fusion
  98.9 0.1 add.139
  99.0 0.0 copy-done.5
  99.1 1.2 gather_fusion
  100.3 0.8 scatter.4
  101.0 1.3 collective-permute-done.2
  102.3 0.0 collective-permute-done.1
  102.3 2.9 %collective-permute-done = bf16[256,256]{1,0:T(8,128)(2,1)S(1)} collective-permute-done((bf16[256,256]{1,0:T(8,128)(2,1)S(1)}, bf16[256,256]{1,0:T(8,128)(2,1)S(1)}, u32[]{:S(2)}, u32[]{:S(2)}) %collective-permute-start) | collective-permute-done | bytes 131104 | tf_op jit(solution)/shard_map/ppermute | solution.py:901
  105.2 0.8 pad_maximum_fusion
  106.0 48.6 %attn_bwd.1 = (bf16[4,1024,512]{2,1,0:T(8,128)(2,1)}, bf16[2,768,256]{2,1,0:T(8,128)(2,1)}, f32[8,256]{1,0:T(8,128)}) custom-call(s32[32]{0:T(128)} %gather_fusion, bf16[4,4,256,512]{3,2,1,0:T(8,128)(2,1)} %get-tuple-element.62.x_ref, bf16[512,768]{1,0:T(8,128)(2,1)} %get-tuple-element.63.wqkv_ref, bf16[4,2,512,256]{3,2,1,0:T(8,128)(2,1)} %get-tuple-element.64.K, ...), custom_call_target="tpu_custom_call" | custom-call | tf_op jit(solution)/shard_map/attn_bwd/pallas_call | solution.py:330
  154.7 0.8 fusion.5
  155.5 0.2 dynamic_update_slice.6
  155.6 0.3 dynamic_update_slice.7.gv_ref
  155.9 0.0 copy-start.3
  155.9 0.6 copy-done.3
  156.5 108.6 %reduce_all.1 = (bf16[2,256,512]{2,1,0:T(8,128)(2,1)}, bf16[3,768,512]{2,1,0:T(8,128)(2,1)}, bf16[1536,256]{1,0:T(8,128)(2,1)}, f32[24,512]{1,0:T(8,128)}) custom-call(bf16[4,1024,512]{2,1,0:T(8,128)(2,1)} %get-tuple-element.72.dx_ref, bf16[2,2304,512]{2,1,0:T(8,128)(2,1)} %get-tuple-element.73.gw_ref, bf16[2,768,256]{2,1,0:T(8,128)(2,1)} %get-tuple-element.74.gq_ref, ...), custom_call_target="tpu_custom_call" | custom-call | tf_op jit(solution)/shard_map/reduce_all/pallas_call | solution.py:729
  265.1 1.8 slice_convert_fusion.1
  266.9 0.0 copy-start.4
  266.9 0.0 copy-start.2
  266.9 0.0 copy-start.1
  266.9 3.3 %slice_convert_fusion = (f32[1024,512]{1,0:T(8,128)}, bf16[1024,512]{1,0:T(8,128)(2,1)S(1)}) fusion(bf16[2304,512]{1,0:T(8,128)(2,1)} %bitcast.55), kind=kLoop, calls=%fused_computation.2 | loop fusion | flops 524288 | bytes 5242880 | tf_op jit(solution)/shard_map/convert_element_type | solution.py:949
  270.2 0.0 copy-done.4
  270.3 0.0 copy-done.2
  270.3 0.0 copy-done.1
  270.3 0.1 slice_convert_fusion.2
  270.5 0.4 copy.40
  270.9 0.8 copy.45
  271.7 0.4 copy.41
  272.1 0.8 copy.46
  273.0 0.4 copy.42
  273.4 0.8 copy.47
  274.2 0.6 constant_dynamic-slice_fusion.7
  274.8 0.6 constant_dynamic-slice_fusion.6
  275.3 0.6 constant_dynamic-slice_fusion.5
  275.9 0.6 constant_dynamic-slice_fusion.4
  276.4 0.6 constant_dynamic-slice_fusion.3
  277.0 0.3 convert_bitcast_fusion
  277.3 0.0 copy-start
  277.3 1.5 copy.44
  278.8 0.6 constant_dynamic-slice_fusion.2
  279.4 0.6 constant_dynamic-slice_fusion.1
  280.0 0.6 constant_dynamic-slice_fusion
  280.5 0.6 dynamic_slice.89
  281.1 0.0 copy-done
  281.1 1.0 add_convert_fusion
  (8 shorter events, 0.1 us)
Async XLA Ops:
  80.5 18.3 %copy-start.6 = (s32[4]{0:T(128)S(1)}, s32[4]{0:T(128)}, u32[]{:S(2)}) copy-start(s32[4]{0:T(128)} %constant.194.clone) | copy-start | bytes 52
  80.5 18.5 %copy-start.5 = (s32[2,32]{1,0:T(2,128)S(1)}, s32[2,32]{1,0:T(2,128)}, u32[]{:S(2)}) copy-start(s32[2,32]{1,0:T(2,128)} %order_ref.1) | copy-start | bytes 772
  96.5 5.8 %collective-permute-start.2 = (bf16[256,256]{1,0:T(8,128)(2,1)S(1)}, bf16[256,256]{1,0:T(8,128)(2,1)S(1)}, u32[]{:S(2)}, u32[]{:S(2)}) collective-permute-start(bf16[256,256]{1,0:T(8,128)(2,1)S(1)} %get-tuple-element.89), channel_id=1, source_target_pairs={{0,6},{2,4},{4,2},{6,0},{8,14},{10,12},{12,10},{14,8},{16,22},{18,... | collective-permute-start | bytes 393224 | tf_op jit(solution)/shard_map/ppermute | solution.py:901
  97.3 5.0 %collective-permute-start.1 = (bf16[256,256]{1,0:T(8,128)(2,1)S(1)}, bf16[256,256]{1,0:T(8,128)(2,1)S(1)}, u32[]{:S(2)}, u32[]{:S(2)}) collective-permute-start(bf16[256,256]{1,0:T(8,128)(2,1)S(1)} %get-tuple-element.90), channel_id=1, source_target_pairs={{0,2},{2,0},{4,6},{6,4},{8,10},{10,8},{12,14},{14,12},{16,18},{18,... | collective-permute-start | bytes 393224 | tf_op jit(solution)/shard_map/ppermute | solution.py:901
  98.2 7.0 %collective-permute-start = (bf16[256,256]{1,0:T(8,128)(2,1)S(1)}, bf16[256,256]{1,0:T(8,128)(2,1)S(1)}, u32[]{:S(2)}, u32[]{:S(2)}) collective-permute-start(bf16[256,256]{1,0:T(8,128)(2,1)S(1)} %get-tuple-element.91), channel_id=1, source_target_pairs={{0,4},{2,6},{4,0},{6,2},{8,12},{10,14},{12,8},{14,10},{16,20},{18,... | collective-permute-start | bytes 393224 | tf_op jit(solution)/shard_map/ppermute | solution.py:901
  155.9 0.6 copy-start.3
  266.9 3.3 %copy-start.4 = (f32[24,512]{1,0:T(8,128)S(1)}, f32[24,512]{1,0:T(8,128)}, u32[]{:S(2)}) copy-start(f32[24,512]{1,0:T(8,128)} %get-tuple-element.79) | copy-start | bytes 147460
  266.9 3.4 %copy-start.2 = (bf16[2,256,512]{2,1,0:T(8,128)(2,1)S(1)}, bf16[2,256,512]{2,1,0:T(8,128)(2,1)}, u32[]{:S(2)}) copy-start(bf16[2,256,512]{2,1,0:T(8,128)(2,1)} %get-tuple-element.77) | copy-start | bytes 1572868
  266.9 3.4 %copy-start.1 = (bf16[1536,256]{1,0:T(8,128)(2,1)S(1)}, bf16[1536,256]{1,0:T(8,128)(2,1)}, u32[]{:S(2)}) copy-start(bf16[1536,256]{1,0:T(8,128)(2,1)} %get-tuple-element.78) | copy-start | bytes 2359300
  277.3 3.8 %copy-start = (f32[512,512]{1,0:T(8,128)S(1)}, f32[512,512]{1,0:T(8,128)}, u32[]{:S(2)}) copy-start(f32[512,512]{1,0:T(8,128)} %get-tuple-element.61) | copy-start | bytes 3145732
